TPU v7x, 32 devices: a whole 2x2x4 slice. The times are simulated.
32 devices in a mesh: mode: 8 (over z, x), row: 4 (over y, core).
Axes of the slice: x: 2, y: 2, z: 4, core: 2. Of those that a mesh axis runs over, the one named last changes fastest.
Arguments:
- forward: bfloat16 [64, 8, 2, 512], P('mode', 'row'), may hold values from -6 to 6
- backward: bfloat16 [64, 8, 2, 512], P('mode', 'row'), may hold values from -6 to 6
- propagator: bfloat16 [2, 512, 512], replicated, may hold values from -0.1875 to 0.1875
- row_taps: float32 [2, 3], replicated, may hold values from -3 to 3
- phase_masks: float32 [7, 8, 512], P(None, 'row'), may hold values from -3.140625 to 3.140625
- plane_index: int32 [4], replicated, may hold values from 0 to 6
- wave_ratio: float32 [4], replicated, may hold values from 0.7 to 1.4
- pair_list: int32 [80, 2], replicated, may hold values from 0 to 15, as said below
Outputs:
- coupling: float32 [2, 64, 64], P(None, 'mode')
- mask_grad: float32 [4, 8, 512], P(None, 'row')
Inputs may be any that keep to these rules, and one draw needn't show every extreme that they name: `pair_list`: each row names a target group and a forward group; no pair appears twice and every group is paired with itself; 80 pairs in all.
All inputs are finite; a program needn't handle non-finite values.
Results may differ from a plain program's by a relative error of at most 0.0078.
Values may be sent and summed in bfloat16 or wider, within the bound.
No kernel may reach another device: no remote copies, remote signals or barrier semaphores. Data moves between devices by JAX's collectives and lax.ppermute only.
A program may use at most 64 MiB of HBM per device.

v0:
```python
import math

import jax
import jax.numpy as jnp
from jax import lax
from jax.sharding import PartitionSpec as P

NG = 16


def padded_2(array, sides, width):
    for axis, dim in sides:
        peers, length = (lax.axis_size(axis), array.shape[dim])
        up = [(i, (i + 1) % peers) for i in range(peers - 1)]
        down = [(j, i) for i, j in up]
        last = lax.slice_in_dim(array, length - width, length, axis=dim)
        leading = lax.slice_in_dim(array, 0, width, axis=dim)
        before = lax.ppermute(last, axis, up)
        after = lax.ppermute(leading, axis, down)
        array = jnp.concatenate([before, array, after], axis=dim)
    return array


def chosen_phases(phase_masks, plane_index, wave_ratio):
    planes = jnp.arange(phase_masks.shape[0], dtype=jnp.int32)
    selector = (plane_index[:, None] == planes[None, :]).astype(jnp.float32)
    picked = jnp.einsum("wp,prc->wrc", selector, phase_masks, precision=lax.Precision.HIGHEST)
    return picked * wave_ratio[:, None, None]


def apply_mask(forward, phases):
    mode_total, row_total, _, width = forward.shape
    wave_total = phases.shape[0]
    shaped = forward.astype(jnp.float32).reshape(
        mode_total // wave_total, wave_total, row_total, 2, width
    )
    cosine = jnp.cos(phases)[None]
    sine = jnp.sin(phases)[None]
    real_part = shaped[:, :, :, 0] * cosine - shaped[:, :, :, 1] * sine
    imag_part = shaped[:, :, :, 0] * sine + shaped[:, :, :, 1] * cosine
    return jnp.stack([real_part, imag_part], axis=3).reshape(forward.shape).astype(jnp.bfloat16)


def forward_matrix(propagator):
    top_half = jnp.concatenate([propagator[0], propagator[1]], axis=1)
    low_half = jnp.concatenate([-propagator[1], propagator[0]], axis=1)
    return jnp.concatenate([top_half, low_half], axis=0)


def backward_matrix(propagator):
    top_half = jnp.concatenate([propagator[0].T, -propagator[1].T], axis=1)
    low_half = jnp.concatenate([propagator[1].T, propagator[0].T], axis=1)
    return jnp.concatenate([top_half, low_half], axis=0)


def propagate(fields, matrix):
    width = fields.shape[-1]
    result = jnp.dot(fields.reshape(-1, 2 * width), matrix, preferred_element_type=jnp.float32)
    return result.reshape(fields.shape)


def row_stencil(padded, row_taps, adjoint):
    values = padded.astype(jnp.float32)
    below_rows = values[:, :-2]
    center = values[:, 1:-1]
    above_rows = values[:, 2:]
    tap_real = row_taps[0]
    tap_imag = row_taps[1]
    if adjoint:
        sources = (above_rows, center, below_rows)
        tap_imag = -tap_imag
    else:
        sources = (below_rows, center, above_rows)
    real_sum = jnp.zeros(center[:, :, 0].shape, jnp.float32)
    imag_sum = jnp.zeros(center[:, :, 0].shape, jnp.float32)
    for position in range(3):
        source = sources[position]
        real_sum = (
            real_sum + tap_real[position] * source[:, :, 0] - tap_imag[position] * source[:, :, 1]
        )
        imag_sum = (
            imag_sum + tap_real[position] * source[:, :, 1] + tap_imag[position] * source[:, :, 0]
        )
    return jnp.stack([real_sum, imag_sum], axis=2)


def times_i(fields):
    return jnp.stack([-fields[:, :, 1], fields[:, :, 0]], axis=2)


def times_minus_i(fields):
    return jnp.stack([fields[:, :, 1], -fields[:, :, 0]], axis=2)


def body(forward, backward, propagator, row_taps, phase_masks, plane_index, wave_ratio, pair_list):
    local_modes, local_rows, _, width = forward.shape
    wave_total = wave_ratio.shape[0]
    mode_total = local_modes * lax.axis_size("mode")
    row_total = local_rows * lax.axis_size("row")
    group_size = mode_total // NG
    phases = chosen_phases(phase_masks, plane_index, wave_ratio)
    masked = apply_mask(forward, phases)
    spread = propagate(masked, forward_matrix(propagator)).astype(jnp.bfloat16)
    padded = padded_2(spread, (("row", 1),), 1)
    field = row_stencil(padded, row_taps, False).astype(jnp.bfloat16)
    field_flat = field.reshape(local_modes, -1)
    field_turned = times_minus_i(field).reshape(local_modes, -1)
    group_ids = jnp.arange(NG, dtype=jnp.int32)
    hits = (pair_list[:, 0][:, None, None] == group_ids[None, :, None]) & (
        pair_list[:, 1][:, None, None] == group_ids[None, None, :]
    )
    pair_matrix = jnp.sum(hits.astype(jnp.float32), axis=0)
    own_modes = lax.axis_index("mode") * local_modes + jnp.arange(local_modes, dtype=jnp.int32)
    own_onehot = ((own_modes // group_size)[:, None] == group_ids[None, :]).astype(jnp.float32)
    target_groups = jnp.arange(mode_total, dtype=jnp.int32) // group_size
    target_onehot = (target_groups[:, None] == group_ids[None, :]).astype(jnp.float32)
    own_pairs = jnp.dot(own_onehot, pair_matrix.T, precision=lax.Precision.HIGHEST)
    column_mask = jnp.dot(own_pairs, target_onehot.T, precision=lax.Precision.HIGHEST)
    shard_rows = lax.all_gather(backward, "mode", axis=0, tiled=True)
    rows_flat = shard_rows.reshape(shard_rows.shape[0], -1)
    real_part = jnp.einsum("nd,kd->nk", field_flat, rows_flat, preferred_element_type=jnp.float32)
    imag_part = jnp.einsum("nd,kd->nk", field_turned, rows_flat, preferred_element_type=jnp.float32)
    block = jnp.stack([real_part, imag_part])
    match_sum = lax.psum(block, "row")
    coupling = match_sum * (1.0 / math.sqrt(row_total * width)) * column_mask[None, :, :]
    weights = coupling.astype(jnp.bfloat16)
    shard_rows = lax.all_gather(backward, "mode", axis=0, tiled=True)
    row_count = shard_rows.shape[0]
    rows_flat = shard_rows.reshape(row_count, -1)
    rows_turned = times_i(shard_rows).reshape(row_count, -1)
    weight_real = weights[0]
    weight_imag = weights[1]
    running = jnp.dot(weight_real, rows_flat, preferred_element_type=jnp.float32)
    gathered = running + jnp.dot(weight_imag, rows_turned, preferred_element_type=jnp.float32)
    gathered = (
        (gathered * (1.0 / math.sqrt(mode_total))).astype(jnp.bfloat16).reshape(forward.shape)
    )
    padded_back = padded_2(gathered, (("row", 1),), 1)
    pulled = row_stencil(padded_back, row_taps, True).astype(jnp.bfloat16)
    adjoint = propagate(pulled, backward_matrix(propagator))
    masked_float = masked.astype(jnp.float32)
    term = masked_float[:, :, 1] * adjoint[:, :, 0] - masked_float[:, :, 0] * adjoint[:, :, 1]
    partial_grad = jnp.sum(
        term.reshape(local_modes // wave_total, wave_total, local_rows, width), axis=0
    )
    summed = lax.psum(partial_grad, "mode")
    mask_grad = summed * (-2.0 / math.sqrt(mode_total))
    return (coupling, mask_grad)


def solution(mesh):
    in_specs = (
        P("mode", "row", None, None),
        P("mode", "row", None, None),
        P(),
        P(),
        P(None, "row", None),
        P(),
        P(),
        P(),
    )
    out_specs = (P(None, "mode", None), P(None, "row", None))
    return jax.shard_map(body, mesh=mesh, in_specs=in_specs, out_specs=out_specs, check_vma=False)
```

profile of v0, /device:TPU:0, one launch (start us, length us, event | category | flops | bytes accessed | tf_op | source)
XLA Modules:
  0.0 117.6 jit_solution(7645582533571077190)
XLA Ops:
  0.7 2.7 %slice_bitcast_fusion = (bf16[512,512]{0,1:T(8,128)(2,1)}, bf16[512,512]{0,1:T(8,128)(2,1)}, bf16[512,512]{1,0:T(8,128)(2,1)}, bf16[512,512]{1,0:T(8,128)(2,1)}) fusion(bf16[2,512,512]{2,1,0:T(8,128)(2,1)} %param.10), kind=kLoop, calls=%fused_computation.10 | loop fusion | bytes 3145728 | tf_op jit(solution)/shard_map/transpose | solution.py:51
  3.4 0.9 fusion.19
  4.4 0.3 fusion.26
  4.8 1.8 %maximum_bitcast_fusion = bf16[1024,1024]{0,1:T(8,128)(2,1)S(1)} fusion(bf16[512,512]{1,0:T(8,128)(2,1)} %get-tuple-element.13, bf16[512,512]{1,0:T(8,128)(2,1)} %fusion.19, bf16[512,512]{1,0:T(8,128)(2,1)} %get-tuple-element.12), kind=kLoop, calls=%fused_computation.3 | loop fusion | flops 8388608 | bytes 3670016 | tf_op jit(solution)/shard_map/dot_general | solution.py:58
  6.6 2.6 %copy.33 = bf16[1024,1024]{1,0:T(8,128)(2,1)} copy(bf16[1024,1024]{0,1:T(8,128)(2,1)S(1)} %maximum_bitcast_fusion) | data formatting | bytes 4194304 | tf_op jit(solution)/shard_map/dot_general | solution.py:58
  9.2 2.3 %convolution_convert_fusion = bf16[8,2,2,512]{3,0,2,1:T(8,128)(2,1)S(1)} fusion(bf16[8,2,1024,1]{2,0,3,1:T(8,128)(2,1)S(1)} %bitcast.95, bf16[2,512,1024,1]{2,1,0,3:T(8,128)(2,1)} %bitcast.92), kind=kOutput, calls=%fused_computation.5 | convolution fusion | flops 33570816 | bytes 2162688 | tf_op jit(solution)/shard_map/dot_general | solution.py:58
  11.5 2.4 %collective-permute-start = (bf16[8,1,2,512]{3,0,2,1:T(8,128)(2,1)S(1)}, bf16[8,1,2,512]{3,0,2,1:T(8,128)(2,1)S(1)}, u32[]{:S(2)}, u32[]{:S(2)}) collective-permute-start(bf16[8,1,2,512]{3,0,2,1:T(8,128)(2,1)S(1)} %get-tuple-element.22), channel_id=1, source_target_pairs={{0,1},{1,2},{2,3},{4,5},{5,6},{6,7},{8,9},{9,10},{10,11},{12,13},{... | collective-permute-start | bytes 49160 | tf_op jit(solution)/shard_map/ppermute | solution.py:18
  13.9 1.3 %collective-permute-start.1 = (bf16[8,1,2,512]{3,0,2,1:T(8,128)(2,1)S(1)}, bf16[8,1,2,512]{3,0,2,1:T(8,128)(2,1)S(1)}, u32[]{:S(2)}, u32[]{:S(2)}) collective-permute-start(bf16[8,1,2,512]{3,0,2,1:T(8,128)(2,1)S(1)} %get-tuple-element.23), channel_id=1, source_target_pairs={{1,0},{2,1},{3,2},{5,4},{6,5},{7,6},{9,8},{10,9},{11,10},{13,12},{... | collective-permute-start | bytes 49160 | tf_op jit(solution)/shard_map/ppermute | solution.py:19
  15.2 0.8 fusion.20
  16.0 31.9 %all_gather.4 = bf16[64,2,2,512]{3,0,2,1:T(8,128)(2,1)S(1)} all-gather(bf16[8,2,2,512]{3,0,2,1:T(8,128)(2,1)S(1)} %copy.34), channel_id=1, replica_groups=mesh['mode'=8,'row'=4] {'mode'}, dimensions={0}, use_global_device_ids=true | all-gather | bytes 294912 | tf_op jit(solution)/shard_map/all_gather | solution.py:119
  48.6 1.8 %maximum_maximum_fusion = bf16[1024,1024]{0,1:T(8,128)(2,1)S(1)} fusion(bf16[512,512]{0,1:T(8,128)(2,1)} %get-tuple-element.11, bf16[512,512]{0,1:T(8,128)(2,1)} %get-tuple-element.10, bf16[512,512]{0,1:T(8,128)(2,1)} %fusion.20), kind=kLoop, calls=%fused_computation.4 | loop fusion | flops 8388608 | bytes 3670016 | tf_op jit(solution)/shard_map/concatenate | solution.py:53
  50.4 0.7 fusion.27
  52.0 3.7 %fusion.22 = (bf16[8,2,1,512]{3,0,2,1:T(8,128)(2,1)S(1)}, bf16[8,2,1,512]{3,0,2,1:T(8,128)(2,1)S(1)}) fusion(f32[8,4,2,512]{3,0,2,1:T(8,128)S(1)} %maximum_convert_fusion, f32[]{:T(128)} %bitcast.16, f32[]{:T(128)} %bitcast.15, f32[]{:T(128)} %bitcast.14, f32[]{:T(128)} %bitcast.13, f32[]{:T(128)} %bitcast.12, f32[]{:T(128)} %bitcast), kind=kLoop, calls=%fused_computation.70 | loop fusion | flops 106496 | bytes 229400 | tf_op jit(solution)/shard_map/neg | solution.py:92
  55.7 3.7 %add_convert_fusion.1 = bf16[8,2,1,512]{3,0,2,1:T(8,128)(2,1)S(1)} fusion(f32[8,4,2,512]{3,0,2,1:T(8,128)S(1)} %maximum_convert_fusion, f32[]{:T(128)} %bitcast.16, f32[]{:T(128)} %bitcast.15, f32[]{:T(128)} %bitcast.14, f32[]{:T(128)} %bitcast.13, f32[]{:T(128)} %bitcast.12, f32[]{:T(128)} %bitcast), kind=kLoop, calls=%fused_computation.33 | loop fusion | flops 98304 | bytes 213016 | tf_op jit(solution)/shard_map/slice | solution.py:92
  59.8 7.7 %psum.14 = f32[2,8,64]{2,1,0:T(8,128)S(1)} all-reduce(f32[2,8,64]{2,1,0:T(8,128)S(1)} %pad_maximum_fusion.2), channel_id=1, replica_groups=mesh['mode'=8,'row'=4] {'row'}, use_global_device_ids=true, to_apply=%region_0.0 | all-reduce | flops 1024 | bytes 8192 | tf_op jit(solution)/shard_map/psum | solution.py:124
  67.6 0.6 fusion.21
  68.5 2.3 %collective-permute-start.2 = (bf16[8,1,2,512]{3,0,2,1:T(8,128)(2,1)S(1)}, bf16[8,1,2,512]{3,0,2,1:T(8,128)(2,1)S(1)}, u32[]{:S(2)}, u32[]{:S(2)}) collective-permute-start(bf16[8,1,2,512]{3,0,2,1:T(8,128)(2,1)S(1)} %get-tuple-element.20), channel_id=1, source_target_pairs={{0,1},{1,2},{2,3},{4,5},{5,6},{6,7},{8,9},{9,10},{10,11},{12,13},{... | collective-permute-start | bytes 49160 | tf_op jit(solution)/shard_map/ppermute | solution.py:18
  70.8 1.3 %collective-permute-start.3 = (bf16[8,1,2,512]{3,0,2,1:T(8,128)(2,1)S(1)}, bf16[8,1,2,512]{3,0,2,1:T(8,128)(2,1)S(1)}, u32[]{:S(2)}, u32[]{:S(2)}) collective-permute-start(bf16[8,1,2,512]{3,0,2,1:T(8,128)(2,1)S(1)} %get-tuple-element.21), channel_id=1, source_target_pairs={{1,0},{2,1},{3,2},{5,4},{6,5},{7,6},{9,8},{10,9},{11,10},{13,12},{... | collective-permute-start | bytes 49160 | tf_op jit(solution)/shard_map/ppermute | solution.py:19
  72.1 0.7 fusion.28
  72.8 2.6 %collective-permute-done.3 = bf16[8,1,2,512]{3,0,2,1:T(8,128)(2,1)S(1)} collective-permute-done((bf16[8,1,2,512]{3,0,2,1:T(8,128)(2,1)S(1)}, bf16[8,1,2,512]{3,0,2,1:T(8,128)(2,1)S(1)}, u32[]{:S(2)}, u32[]{:S(2)}) %collective-permute-start.3) | collective-permute-done | bytes 16416 | tf_op jit(solution)/shard_map/ppermute | solution.py:19
  75.4 3.8 %subtract_convert_fusion = (bf16[8,2,1,512]{3,0,2,1:T(8,128)(2,1)S(1)}, bf16[8,2,1,512]{3,0,2,1:T(8,128)(2,1)S(1)}) fusion(f32[8,4,2,512]{3,0,2,1:T(8,128)S(1)} %maximum_convert_fusion.1, f32[]{:T(128)} %bitcast.30, f32[]{:T(128)} %bitcast.29, f32[]{:T(128)} %bitcast.28, f32[]{:T(128)} %bitcast.15, f32[]{:T(128)} %bitcast.13, f32[]{:T(128)} %bitcast), kind=kLoop, calls=%fused_computation.31 | loop fusion | flops 196608 | bytes 229400 | tf_op jit(solution)/shard_map/convert.1
  79.2 0.6 fusion.29
  79.9 37.1 %psum.15 = f32[4,2,512]{2,0,1:T(4,128)S(1)} all-reduce(f32[4,2,512]{2,0,1:T(4,128)S(1)} %reduce_sum.19), channel_id=1, replica_groups=mesh['mode'=8,'row'=4] {'mode'}, use_global_device_ids=true, to_apply=%region_3.4 | all-reduce | flops 4096 | bytes 32768 | tf_op jit(solution)/shard_map/psum | solution.py:146
  117.0 0.6 copy.37
  (55 shorter events, 2.4 us)
Async XLA Ops:
  0.6 3.7 %copy-start = (f32[7,2,512]{2,1,0:T(2,128)S(1)}, f32[7,2,512]{2,1,0:T(2,128)}, u32[]{:S(2)}) copy-start(f32[7,2,512]{2,1,0:T(2,128)} %param.12) | copy-start | bytes 86020
  0.6 2.8 %copy-start.1 = (bf16[2,512,512]{2,1,0:T(8,128)(2,1)S(1)}, bf16[2,512,512]{2,1,0:T(8,128)(2,1)}, u32[]{:S(2)}) copy-start(bf16[2,512,512]{2,1,0:T(8,128)(2,1)} %param.10) | copy-start | bytes 3145732
  0.7 3.6 %copy-start.2 = (bf16[8,2,2,512]{3,2,1,0:T(2,128)(2,1)S(1)}, bf16[8,2,2,512]{3,2,1,0:T(2,128)(2,1)}, u32[]{:S(2)}) copy-start(bf16[8,2,2,512]{3,2,1,0:T(2,128)(2,1)} %param.8) | copy-start | bytes 98308
  0.7 3.7 %copy-start.7 = (s32[4]{0:T(128)S(1)}, s32[4]{0:T(128)}, u32[]{:S(2)}) copy-start(s32[4]{0:T(128)} %param.13) | copy-start | bytes 52
  0.7 3.7 %copy-start.6 = (f32[4]{0:T(128)S(1)}, f32[4]{0:T(128)}, u32[]{:S(2)}) copy-start(f32[4]{0:T(128)} %param.14) | copy-start | bytes 52
  9.2 6.8 %copy-start.3 = (bf16[8,2,2,512]{3,2,1,0:T(2,128)(2,1)S(1)}, bf16[8,2,2,512]{3,2,1,0:T(2,128)(2,1)}, u32[]{:S(2)}) copy-start(bf16[8,2,2,512]{3,2,1,0:T(2,128)(2,1)} %param.9) | copy-start | bytes 98308
  9.2 38.7 %copy-start.5 = (s32[80,2]{0,1:T(2,128)S(1)}, s32[80,2]{0,1:T(2,128)}, u32[]{:S(2)}) copy-start(s32[80,2]{0,1:T(2,128)} %param.15) | copy-start | bytes 1924
  9.2 38.8 %copy-start.4 = (f32[2,3]{1,0:T(2,128)S(1)}, f32[2,3]{1,0:T(2,128)}, u32[]{:S(2)}) copy-start(f32[2,3]{1,0:T(2,128)} %param.11) | copy-start | bytes 76
  11.5 40.5 %collective-permute-start = (bf16[8,1,2,512]{3,0,2,1:T(8,128)(2,1)S(1)}, bf16[8,1,2,512]{3,0,2,1:T(8,128)(2,1)S(1)}, u32[]{:S(2)}, u32[]{:S(2)}) collective-permute-start(bf16[8,1,2,512]{3,0,2,1:T(8,128)(2,1)S(1)} %get-tuple-element.22), channel_id=1, source_target_pairs={{0,1},{1,2},{2,3},{4,5},{5,6},{6,7},{8,9},{9,10},{10,11},{12,13},{... | collective-permute-start | bytes 49160 | tf_op jit(solution)/shard_map/ppermute | solution.py:18
  13.9 38.1 %collective-permute-start.1 = (bf16[8,1,2,512]{3,0,2,1:T(8,128)(2,1)S(1)}, bf16[8,1,2,512]{3,0,2,1:T(8,128)(2,1)S(1)}, u32[]{:S(2)}, u32[]{:S(2)}) collective-permute-start(bf16[8,1,2,512]{3,0,2,1:T(8,128)(2,1)S(1)} %get-tuple-element.23), channel_id=1, source_target_pairs={{1,0},{2,1},{3,2},{5,4},{6,5},{7,6},{9,8},{10,9},{11,10},{13,12},{... | collective-permute-start | bytes 49160 | tf_op jit(solution)/shard_map/ppermute | solution.py:19
  68.5 4.2 %collective-permute-start.2 = (bf16[8,1,2,512]{3,0,2,1:T(8,128)(2,1)S(1)}, bf16[8,1,2,512]{3,0,2,1:T(8,128)(2,1)S(1)}, u32[]{:S(2)}, u32[]{:S(2)}) collective-permute-start(bf16[8,1,2,512]{3,0,2,1:T(8,128)(2,1)S(1)} %get-tuple-element.20), channel_id=1, source_target_pairs={{0,1},{1,2},{2,3},{4,5},{5,6},{6,7},{8,9},{9,10},{10,11},{12,13},{... | collective-permute-start | bytes 49160 | tf_op jit(solution)/shard_map/ppermute | solution.py:18
  70.8 4.6 %collective-permute-start.3 = (bf16[8,1,2,512]{3,0,2,1:T(8,128)(2,1)S(1)}, bf16[8,1,2,512]{3,0,2,1:T(8,128)(2,1)S(1)}, u32[]{:S(2)}, u32[]{:S(2)}) collective-permute-start(bf16[8,1,2,512]{3,0,2,1:T(8,128)(2,1)S(1)} %get-tuple-element.21), channel_id=1, source_target_pairs={{1,0},{2,1},{3,2},{5,4},{6,5},{7,6},{9,8},{10,9},{11,10},{13,12},{... | collective-permute-start | bytes 49160 | tf_op jit(solution)/shard_map/ppermute | solution.py:19
where the time goes:
time: 118 us
  blocking collectives  76.7 us (65%)
  other arithmetic  17.5 us (15%)
  local copies, waits for them, and re-layouts  8.32 us (7%)
  starting transfers between devices  7.2 us (6%)
  matrix products  4.26 us (4%)
  waiting for transfers between devices  2.63 us (2%)
    psum x1, blocking collectives, body(): summed = lax.psum(partial_grad, 'mode')  37.1 us
    all_gather x1, blocking collectives, body(): shard_rows = lax.all_gather(backward, 'mode', axis=0, tiled=True)  31.9 us
    psum x1, blocking collectives, body(): match_sum = lax.psum(block, 'row')  7.74 us
    ppermute x2, starting transfers between devices, padded_2(): before = lax.ppermute(last, axis, up)  4.61 us
    another operation x2, other arithmetic  3.81 us
    neg x1, other arithmetic, times_minus_i(): return jnp.stack([fields[:, :, 1], -fields[:, :, 0]], axis=2)  3.74 us
    slice x1, other arithmetic, times_minus_i(): return jnp.stack([fields[:, :, 1], -fields[:, :, 0]], axis=2)  3.74 us
    dot_general x2, matrix products, propagate(): jnp.dot(fields.reshape(-1, 2 * width), matrix, preferred_element_type=jnp...  2.92 us
  transfers between devices with their start and end apart: 4, of which 1 were waited for; matrix products, arithmetic and copies ran while one was open for 5% of the time, Pallas kernels for 0%

commit v1 on v0

v1 whole, which is shorter than its diff:
```python
import math

import jax
import jax.numpy as jnp
from jax import lax
from jax.experimental import pallas as pl
from jax.experimental.pallas import tpu as pltpu
from jax.sharding import PartitionSpec as P

NG = 16
VMEM_BYTES = 24 << 20
NT = (((1,), (1,)), ((), ()))
F32 = jnp.float32
BF16 = jnp.bfloat16


def size_of(item):
    return math.prod(item.shape) * jnp.dtype(item.dtype).itemsize


def local_call(fn, outs, arrays, scalars=(), flops=0):
    moved = sum(size_of(item) for item in (*arrays, *outs))
    if moved > VMEM_BYTES:
        return fn(*scalars, *arrays)
    first = len(scalars)
    count = first + len(arrays)

    def kernel(*refs):
        values = fn(*refs[:first], *[ref[...] for ref in refs[first:count]])
        for ref, value in zip(refs[count:], values):
            ref[...] = value

    return pl.pallas_call(
        kernel,
        out_shape=tuple(outs),
        in_specs=[pl.BlockSpec(memory_space=pltpu.SMEM)] * first
        + [pl.BlockSpec(memory_space=pltpu.VMEM)] * len(arrays),
        out_specs=tuple(pl.BlockSpec(memory_space=pltpu.VMEM) for _ in outs),
        cost_estimate=pl.CostEstimate(flops=flops, bytes_accessed=moved, transcendentals=0),
        compiler_params=pltpu.CompilerParams(vmem_limit_bytes=48 << 20),
    )(*scalars, *arrays)


def array(shape, dtype):
    return jax.ShapeDtypeStruct(shape, dtype)


def swapped(values, axis, distance):
    peers = lax.axis_size(axis)
    return lax.ppermute(values, axis, [(i, i ^ distance) for i in range(peers)])


def neighbour_rows(fields):
    peers = lax.axis_size("row")
    odd = lax.axis_index("row") % 2 == 1
    modes = fields.shape[0]
    first = fields[:, 0].reshape(modes, -1)
    last = fields[:, -1].reshape(modes, -1)
    even_pairs = [(i, i + 1) for i in range(0, peers - 1, 2)]
    odd_pairs = [(i, i + 1) for i in range(1, peers - 1, 2)]
    both_ways = lambda pairs: pairs + [(j, i) for i, j in pairs]
    over_odd = lax.ppermute(jnp.where(odd, last, first), "row", both_ways(odd_pairs))
    over_even = lax.ppermute(jnp.where(odd, first, last), "row", both_ways(even_pairs))
    return jnp.where(odd, over_even, over_odd), jnp.where(odd, over_odd, over_even)


def rounds_of(peers):
    bits = [1 << k for k in reversed(range(peers.bit_length() - 1))]
    head, tail = bits[:-2], bits[-2:]
    last = [tail[0], tail[1], tail[0] ^ tail[1]] if len(tail) == 2 else tail
    return head, last


def pulled_rows(rows, width):
    def fn(taps, own, before, after):
        half = rows * width
        real = [before[:, :width]] + [own[:, j * width : (j + 1) * width] for j in range(rows)]
        imag = [before[:, width:]] + [
            own[:, half + j * width : half + (j + 1) * width] for j in range(rows)
        ]
        real = [part.astype(F32) for part in real + [after[:, :width]]]
        imag = [part.astype(F32) for part in imag + [after[:, width:]]]
        out_real, out_imag = [], []
        for j in range(1, rows + 1):
            sources = (j + 1, j, j - 1)
            total_real = total_imag = 0.0
            for k in range(3):
                a, b = taps[0, k], taps[1, k]
                total_real = total_real + a * real[sources[k]] + b * imag[sources[k]]
                total_imag = total_imag + a * imag[sources[k]] - b * real[sources[k]]
            out_real.append(total_real)
            out_imag.append(total_imag)
        return (jnp.concatenate(out_real + out_imag, axis=1).astype(BF16),)

    return fn


def halves(pieces):
    whole = jnp.concatenate(pieces, axis=0) if len(pieces) > 1 else pieces[0]
    half = whole.shape[1] // 2
    return whole[:, :half], whole[:, half:]


def by_rows(values, width):
    return [values[:, at : at + width] for at in range(0, values.shape[1], width)]


def spread_all(width):
    def fn(cosine, sine, propagator, *pieces):
        real, imag = halves(pieces)
        total, half = real.shape
        shape = (total // cosine.shape[0], *cosine.shape)
        real = real.astype(F32).reshape(shape)
        imag = imag.astype(F32).reshape(shape)
        masked_real = (real * cosine - imag * sine).reshape(total, half).astype(BF16)
        masked_imag = (real * sine + imag * cosine).reshape(total, half).astype(BF16)
        masked = jnp.concatenate([masked_real, masked_imag], axis=0)
        stacked = jnp.concatenate(by_rows(masked, width), axis=0)
        over_real = jnp.dot(stacked, propagator[0], preferred_element_type=F32)
        over_imag = jnp.dot(stacked, propagator[1], preferred_element_type=F32)
        out_real, out_imag = [], []
        for at in range(0, stacked.shape[0], 2 * total):
            first, second = slice(at, at + total), slice(at + total, at + 2 * total)
            out_real.append(over_real[first] - over_imag[second])
            out_imag.append(over_imag[first] + over_real[second])
        spread = jnp.concatenate(
            [jnp.concatenate(out_real, axis=1), jnp.concatenate(out_imag, axis=1)], axis=0
        )
        return masked, spread.astype(BF16)

    return fn


def project(spread, *pieces):
    targets = jnp.concatenate(halves(pieces), axis=0)
    total = targets.shape[0] // 2
    product = lax.dot_general(spread, targets, NT, preferred_element_type=F32)
    real = product[:total, :total] + product[total:, total:]
    imag = product[total:, :total] - product[:total, total:]
    return (jnp.concatenate([real, imag], axis=1),)


def back_propagated(width):
    def fn(propagator, *pieces):
        targets = jnp.concatenate(halves(pieces), axis=0)
        total = targets.shape[0] // 2
        stacked = jnp.concatenate(by_rows(targets, width), axis=0)
        over_real = lax.dot_general(stacked, propagator[0], NT, preferred_element_type=F32)
        over_imag = lax.dot_general(stacked, propagator[1], NT, preferred_element_type=F32)
        out_real, out_imag = [], []
        for at in range(0, stacked.shape[0], 2 * total):
            first, second = slice(at, at + total), slice(at + total, at + 2 * total)
            out_real.append(over_real[first] + over_imag[second])
            out_imag.append(over_real[second] - over_imag[first])
        result = jnp.concatenate(
            [jnp.concatenate(out_real, axis=1), jnp.concatenate(out_imag, axis=1)], axis=0
        )
        return (result.astype(BF16),)

    return fn


def finish(local_modes, waves, rows, width, scale_pixels, scale_grad):
    def fn(mask, order, back, masked, *partials):
        total = mask.shape[0]
        summed = partials[0]
        for part in partials[1:]:
            summed = summed + part
        real = summed[:, :total] * scale_pixels * mask
        imag = summed[:, total:] * scale_pixels * mask
        own = jnp.concatenate([real[:local_modes], imag[:local_modes]], axis=0)
        own = jnp.dot(own, order, precision=lax.Precision.HIGHEST, preferred_element_type=F32)
        coupling = own.reshape(2, local_modes, total)
        weight_real, weight_imag = real.astype(BF16), imag.astype(BF16)
        weights = jnp.concatenate(
            [
                jnp.concatenate([weight_real, -weight_imag], axis=1),
                jnp.concatenate([weight_imag, weight_real], axis=1),
            ],
            axis=0,
        )
        adjoint = jnp.dot(weights, back, preferred_element_type=F32)
        fields = masked.astype(F32)
        term = fields[total:] * adjoint[:total] - fields[:total] * adjoint[total:]
        group = 2 * waves
        folded = jnp.sum(term.reshape(total // group, group, rows * width), axis=0)
        folded = (folded[:waves] + folded[waves:]) * scale_grad
        grad = jnp.stack(by_rows(folded, width), axis=1)
        return coupling, grad

    return fn


def body(forward, backward, propagator, row_taps, phase_masks, plane_index, wave_ratio, pair_list):
    local_modes, rows, _, width = forward.shape
    waves = wave_ratio.shape[0]
    mode_peers = lax.axis_size("mode")
    row_peers = lax.axis_size("row")
    total = local_modes * mode_peers
    row_total = rows * row_peers
    group_size = total // NG
    half = rows * width

    flat = lambda fields: fields.transpose(0, 2, 1, 3).reshape(local_modes, 2 * half)
    own_forward, own_backward = flat(forward), flat(backward)

    before, after = neighbour_rows(backward)
    (own_pulled,) = local_call(
        pulled_rows(rows, width),
        [array((local_modes, 2 * half), BF16)],
        [own_backward, before, after],
        [row_taps],
        flops=24 * local_modes * half,
    )

    head, last = rounds_of(mode_peers)
    keys = [0]
    fields, targets = own_forward, own_pulled
    for distance in head:
        fields = jnp.concatenate([fields, swapped(fields, "mode", distance)], axis=0)
        targets = jnp.concatenate([targets, swapped(targets, "mode", distance)], axis=0)
        keys = keys + [key ^ distance for key in keys]
    field_pieces = [fields] + [swapped(fields, "mode", distance) for distance in last]
    target_pieces = [targets] + [swapped(targets, "mode", distance) for distance in last]
    keys = keys + [key ^ distance for distance in last for key in keys]

    planes = jnp.arange(phase_masks.shape[0], dtype=jnp.int32)
    selector = (plane_index[:, None] == planes[None, :]).astype(F32)
    picked = jnp.einsum("wp,prc->wrc", selector, phase_masks, precision=lax.Precision.HIGHEST)
    phases = (picked * wave_ratio[:, None, None]).reshape(waves, half)
    cosine = jnp.tile(jnp.cos(phases), (2, 1))
    sine = jnp.tile(jnp.sin(phases), (2, 1))

    peers = jnp.asarray(keys, jnp.int32) ^ lax.axis_index("mode").astype(jnp.int32)
    lanes = jnp.arange(local_modes, dtype=jnp.int32)
    numbers = (peers[:, None] * local_modes + lanes[None, :]).reshape(total)
    groups = numbers // group_size
    to_target = (pair_list[:, 0][:, None] == groups[None, :]).astype(BF16)
    to_forward = (pair_list[:, 1][:, None] == groups[None, :]).astype(BF16)
    mask = lax.dot_general(
        to_forward, to_target, (((0,), (0,)), ((), ())), preferred_element_type=F32
    )
    order = (numbers[:, None] == jnp.arange(total, dtype=jnp.int32)[None, :]).astype(F32)

    masked, spread = local_call(
        spread_all(width),
        [array((2 * total, half), BF16)] * 2,
        [cosine, sine, propagator, *field_pieces],
        flops=8 * total * half * width,
    )
    (partial,) = local_call(
        project,
        [array((total, 2 * total), F32)],
        [spread, *target_pieces],
        flops=8 * total * total * half,
    )
    partials = [partial] + [swapped(partial, "row", d) for d in range(row_peers - 1, 0, -1)]
    (back,) = local_call(
        back_propagated(width),
        [array((2 * total, half), BF16)],
        [propagator, *target_pieces],
        flops=8 * total * half * width,
    )
    coupling, mask_grad = local_call(
        finish(
            local_modes,
            waves,
            rows,
            width,
            1.0 / math.sqrt(row_total * width),
            -2.0 / total,
        ),
        [array((2, local_modes, total), F32), array((waves, rows, width), F32)],
        [mask, order, back, masked, *partials],
        flops=8 * total * total * half,
    )
    return coupling, mask_grad


def solution(mesh):
    in_specs = (
        P("mode", "row", None, None),
        P("mode", "row", None, None),
        P(),
        P(),
        P(None, "row", None),
        P(),
        P(),
        P(),
    )
    out_specs = (P(None, "mode", None), P(None, "row", None))
    return jax.shard_map(body, mesh=mesh, in_specs=in_specs, out_specs=out_specs, check_vma=False)
```

time: 118 us -> 32.8 us (0.28)
  blocking collectives: 76.7 us -> 0 us
  other arithmetic: 17.5 us -> 1.69 us
  starting transfers between devices: 7.2 us -> 15.3 us
  local copies, waits for them, and re-layouts: 8.32 us -> 3.12 us
  waiting for transfers between devices: 2.63 us -> 7.2 us
  matrix products: 4.26 us -> 1.26 us
  Pallas kernels: 0 us -> 2.89 us
    psum x2 -> x0, blocking collectives: 44.8 us -> none  [the longest x1 37.1 us: body(): summed = lax.psum(partial_grad, 'mode')]
    all_gather x1 -> x0, blocking collectives: 31.9 us -> none  [body(): shard_rows = lax.all_gather(backward, 'mode', axis=0, tiled=True)]
    ppermute x4 -> x13, starting transfers between devices: 7.2 us -> 15.3 us  [the longest x11 14.1 us: swapped(): return lax.ppermute(values, axis, [(i, i ^ distance) for i in range(peers)])]
    neg x5 -> x0, other arithmetic: 5.46 us -> none  [the longest x1 3.74 us: times_minus_i(): return jnp.stack([fields[:, :, 1], -fields[:, :, 0]], axis=2)]
    ppermute x4 -> x13, waiting for transfers between devices: 2.63 us -> 7.2 us  [the longest x11 7.2 us: swapped(): return lax.ppermute(values, axis, [(i, i ^ distance) for i in range(peers)])]
    another operation x5 -> x0, other arithmetic: 3.89 us -> none
    slice x1 -> x0, other arithmetic: 3.74 us -> none  [times_minus_i(): return jnp.stack([fields[:, :, 1], -fields[:, :, 0]], axis=2)]
    dot_general x9 -> x2, matrix products: 4.26 us -> 1.26 us  [the longest x1 1 us: body(): jnp.einsum('wp,prc->wrc', selector, phase_masks, precision=lax.Precision....]
  transfers between devices with their start and end apart: 4 -> 13, of which waited for: 1 -> 5; matrix products, arithmetic and copies ran while one was open for 5% -> 14% of each run, Pallas kernels for 0% -> 5%
where the time goes in v1:
time: 32.8 us; the launch traced here: 32.2 us
  starting transfers between devices  15.3 us (47%)
  waiting for transfers between devices  7.2 us (22%)
  local copies, waits for them, and re-layouts  3.12 us (10%)
  Pallas kernels  2.89 us (9%)
  other arithmetic  1.69 us (5%)
  matrix products  1.26 us (4%)
  between operations  0.83 us (3%)
    ppermute x11, starting transfers between devices, swapped(): return lax.ppermute(values, axis, [(i, i ^ distance) for i in range(peers)])  14.1 us
    ppermute x11, waiting for transfers between devices, swapped(): return lax.ppermute(values, axis, [(i, i ^ distance) for i in range(peers)])  7.2 us
    pallas_call x5, Pallas kernels, local_call(): pl.pallas_call(kernel, out_shape=tuple(outs), in_specs=[pl.BlockSpec(memo...  2.89 us
    transpose x2, local copies, waits for them, and re-layouts, body(): fields.transpose(0, 2, 1, 3).reshape(local_modes, 2 * half)  1.54 us
    dot_general x1, matrix products, body(): jnp.einsum('wp,prc->wrc', selector, phase_masks, precision=lax.Precision....  1 us
    unnamed x1, other arithmetic  0.86 us
    eq x1, local copies, waits for them, and re-layouts, body(): to_forward = (pair_list[:, 1][:, None] == groups[None, :]).astype(BF16)  0.76 us
    unnamed x8, local copies, waits for them, and re-layouts  0.7 us
  transfers between devices with their start and end apart: 13, of which 5 were waited for; matrix products, arithmetic and copies ran while one was open for 14% of the time, Pallas kernels for 5%

profile of v1, /device:TPU:0, one launch (start us, length us, event | category | flops | bytes accessed | tf_op | source)
XLA Modules:
  0.0 32.2 jit_solution(16861813719222001716)
XLA Ops:
  0.7 0.9 %fusion.9 = (bf16[1,8,2,512]{3,2,1,0:T(2,128)(2,1)S(1)}, bf16[1,8,2,512]{3,2,1,0:T(2,128)(2,1)S(1)}) fusion(pred[]{:T(512)S(6)} %eq.69, bf16[8,2,2,512]{3,2,1,0:T(2,128)(2,1)} %param.10), kind=kLoop, calls=%fused_computation.15 | loop fusion | flops 16384 | bytes 65537
  1.5 0.5 %collective-permute-start = (bf16[8,1024]{1,0:T(8,128)(2,1)S(1)}, bf16[8,1024]{1,0:T(8,128)(2,1)S(1)}, u32[]{:S(2)}, u32[]{:S(2)}) collective-permute-start(bf16[8,1024]{1,0:T(8,128)(2,1)S(1)} %bitcast.30), channel_id=1, source_target_pairs={{0,1},{2,3},{1,0},{3,2},{4,5},{6,7},{5,4},{7,6},{8,9},{10,11},{9,8... | collective-permute-start | bytes 49160 | tf_op jit(solution)/shard_map/ppermute | solution.py:63
  2.1 0.7 %collective-permute-start.1 = (bf16[8,1024]{1,0:T(8,128)(2,1)S(1)}, bf16[8,1024]{1,0:T(8,128)(2,1)S(1)}, u32[]{:S(2)}, u32[]{:S(2)}) collective-permute-start(bf16[8,1024]{1,0:T(8,128)(2,1)S(1)} %bitcast.31), channel_id=1, source_target_pairs={{1,2},{2,1},{5,6},{6,5},{9,10},{10,9},{13,14},{14,13},{17,18},{18,... | collective-permute-start | bytes 49160 | tf_op jit(solution)/shard_map/ppermute | solution.py:62
  2.7 0.8 %copy.13 = bf16[8,2,2,512]{3,0,2,1:T(8,128)(2,1)S(1)} copy(bf16[8,2,2,512]{3,1,2,0:T(2,128)(2,1)} %bitcast.27) | data formatting | bytes 65536 | tf_op jit(solution)/shard_map/transpose | solution.py:204
  3.5 3.7 %collective-permute-start.6 = (bf16[8,2048]{1,0:T(8,128)(2,1)S(1)}, bf16[8,2048]{1,0:T(8,128)(2,1)S(1)}, u32[]{:S(2)}, u32[]{:S(2)}) collective-permute-start(bf16[8,2048]{1,0:T(8,128)(2,1)S(1)} %bitcast.25), channel_id=1, source_target_pairs={{0,16},{4,20},{8,24},{12,28},{16,0},{20,4},{24,8},{28,12},{1,17},{... | collective-permute-start | bytes 98312 | tf_op jit(solution)/shard_map/ppermute | solution.py:50
  7.2 0.7 %xor_multiply_fusion = s32[8]{0:T(128)S(1)} fusion(s32[8]{0:T(128)} %constant.40.clone, s32[]{:T(128)S(6)} %axis_index.23), kind=kLoop, calls=%fused_computation.27 | loop fusion | flops 16 | bytes 68 | tf_op jit(solution)/shard_map/mul | solution.py:236
  8.0 0.8 %slice_bitcast_fusion.1 = (s32[80]{0:T(128)S(1)}, s32[80]{0:T(128)S(1)}) fusion(s32[80,2]{0,1:T(2,128)} %param.16), kind=kLoop, calls=%fused_computation.28 | loop fusion | bytes 1280 | tf_op jit(solution)/shard_map/eq | solution.py:239
  8.7 1.0 %fusion.13 = (f32[4,2,512]{2,0,1:T(4,128)S(1)}, f32[4,2,512]{2,0,1:T(4,128)S(1)}) fusion(f32[4]{0:T(128)} %param.15, f32[7,2,512]{2,1,0:T(2,128)S(1)} %copy-done, s32[4]{0:T(128)} %param.14), kind=kOutput, calls=%fused_computation.29 | convolution fusion | flops 348188 | bytes 61472 | tf_op jit(solution)/shard_map/wp,prc->wrc/dot_general | solution.py:229
  9.8 0.8 %copy.11 = bf16[8,2,2,512]{3,0,2,1:T(8,128)(2,1)S(1)} copy(bf16[8,2,2,512]{3,1,2,0:T(2,128)(2,1)} %bitcast.24) | data formatting | bytes 65536 | tf_op jit(solution)/shard_map/transpose | solution.py:204
  10.6 0.7 %copy-done.2 = f32[2,3]{1,0:T(2,128)S(1)} copy-done((f32[2,3]{1,0:T(2,128)S(1)}, f32[2,3]{1,0:T(2,128)}, u32[]{:S(2)}) %copy-start.2) | copy-done | bytes 48
  11.2 0.6 %shard_map.104 = bf16[8,2048]{1,0:T(8,128)(2,1)S(1)} custom-call(f32[2,3]{1,0:T(2,128)S(1)} %copy-done.2, bf16[8,2048]{1,0:T(8,128)(2,1)S(1)} %bitcast.23, bf16[8,1024]{1,0:T(8,128)(2,1)S(1)} %get-tuple-element.7.refs_2_, bf16[8,1024]{1,0:T(8,128)(2,1)S(1)} %get-tuple-element.6.refs_3_), custom_call_target="tpu_custom_call" | custom-call | flops 196608 | bytes 98304 | tf_op jit(solution)/shard_map/pallas_call | solution.py:33
  11.9 2.0 %collective-permute-start.7 = (bf16[16,2048]{1,0:T(8,128)(2,1)S(1)}, bf16[16,2048]{1,0:T(8,128)(2,1)S(1)}, u32[]{:S(2)}, u32[]{:S(2)}) collective-permute-start(bf16[16,2048]{1,0:T(8,128)(2,1)S(1)} %pad_maximum_fusion.1.refs_3_), channel_id=1, source_target_pairs={{0,8},{4,12},{8,0},{12,4},{16,24},{20,28},{24,16},{28,20},{1,9},{5... | collective-permute-start | bytes 196616 | tf_op jit(solution)/shard_map/ppermute | solution.py:50
  13.9 1.5 %collective-permute-start.8 = (bf16[16,2048]{1,0:T(8,128)(2,1)S(1)}, bf16[16,2048]{1,0:T(8,128)(2,1)S(1)}, u32[]{:S(2)}, u32[]{:S(2)}) collective-permute-start(bf16[16,2048]{1,0:T(8,128)(2,1)S(1)} %pad_maximum_fusion.1.refs_3_), channel_id=1, source_target_pairs={{0,4},{4,0},{8,12},{12,8},{16,20},{20,16},{24,28},{28,24},{1,5},{5... | collective-permute-start | bytes 196616 | tf_op jit(solution)/shard_map/ppermute | solution.py:50
  15.5 1.2 %collective-permute-done.2 = bf16[8,2048]{1,0:T(8,128)(2,1)S(1)} collective-permute-done((bf16[8,2048]{1,0:T(8,128)(2,1)S(1)}, bf16[8,2048]{1,0:T(8,128)(2,1)S(1)}, u32[]{:S(2)}, u32[]{:S(2)}) %collective-permute-start.2) | collective-permute-done | bytes 32800 | tf_op jit(solution)/shard_map/ppermute | solution.py:50
  16.7 1.6 %collective-permute-start.3 = (bf16[16,2048]{1,0:T(8,128)(2,1)S(1)}, bf16[16,2048]{1,0:T(8,128)(2,1)S(1)}, u32[]{:S(2)}, u32[]{:S(2)}) collective-permute-start(bf16[16,2048]{1,0:T(8,128)(2,1)S(1)} %pad_maximum_fusion.refs_1_), channel_id=1, source_target_pairs={{0,8},{4,12},{8,0},{12,4},{16,24},{20,28},{24,16},{28,20},{1,9},{5... | collective-permute-start | bytes 196616 | tf_op jit(solution)/shard_map/ppermute | solution.py:50
  18.3 1.5 %collective-permute-start.4 = (bf16[16,2048]{1,0:T(8,128)(2,1)S(1)}, bf16[16,2048]{1,0:T(8,128)(2,1)S(1)}, u32[]{:S(2)}, u32[]{:S(2)}) collective-permute-start(bf16[16,2048]{1,0:T(8,128)(2,1)S(1)} %pad_maximum_fusion.refs_1_), channel_id=1, source_target_pairs={{0,4},{4,0},{8,12},{12,8},{16,20},{20,16},{24,28},{28,24},{1,5},{5... | collective-permute-start | bytes 196616 | tf_op jit(solution)/shard_map/ppermute | solution.py:50
  20.6 0.5 %shard_map.106 = (bf16[128,1024]{1,0:T(8,128)(2,1)S(1)}, bf16[128,1024]{1,0:T(8,128)(2,1)S(1)}) custom-call(f32[8,1024]{1,0:T(8,128)S(1)} %tile.9.refs_0_, f32[8,1024]{1,0:T(8,128)S(1)} %tile.21.refs_1_, bf16[2,512,512]{2,1,0:T(8,128)(2,1)S(1)} %copy-done.1, bf16[16,2048]{1,0:T(8,128)(2,1)S(1)} %pad_maximum_fusion.1.refs_3_, ...), custom_call_target="tpu_custom_call" | custom-call | flops 268435456 | bytes 1900544 | tf_op jit(solution)/shard_map/pallas_call | solution.py:33
  21.0 0.5 %collective-permute-done.3.refs_2_ = bf16[16,2048]{1,0:T(8,128)(2,1)S(1)} collective-permute-done((bf16[16,2048]{1,0:T(8,128)(2,1)S(1)}, bf16[16,2048]{1,0:T(8,128)(2,1)S(1)}, u32[]{:S(2)}, u32[]{:S(2)}) %collective-permute-start.3) | collective-permute-done | bytes 65568 | tf_op jit(solution)/shard_map/ppermute | solution.py:50
  21.5 1.5 %collective-permute-done.4.refs_3_ = bf16[16,2048]{1,0:T(8,128)(2,1)S(1)} collective-permute-done((bf16[16,2048]{1,0:T(8,128)(2,1)S(1)}, bf16[16,2048]{1,0:T(8,128)(2,1)S(1)}, u32[]{:S(2)}, u32[]{:S(2)}) %collective-permute-start.4) | collective-permute-done | bytes 65568 | tf_op jit(solution)/shard_map/ppermute | solution.py:50
  23.0 2.4 %collective-permute-done.5.refs_4_ = bf16[16,2048]{1,0:T(8,128)(2,1)S(1)} collective-permute-done((bf16[16,2048]{1,0:T(8,128)(2,1)S(1)}, bf16[16,2048]{1,0:T(8,128)(2,1)S(1)}, u32[]{:S(2)}, u32[]{:S(2)}) %collective-permute-start.5) | collective-permute-done | bytes 65568 | tf_op jit(solution)/shard_map/ppermute | solution.py:50
  25.9 3.2 %collective-permute-start.11 = (f32[64,128]{1,0:T(8,128)S(1)}, f32[64,128]{1,0:T(8,128)S(1)}, u32[]{:S(2)}, u32[]{:S(2)}) collective-permute-start(f32[64,128]{1,0:T(8,128)S(1)} %shard_map.107.refs_4_), channel_id=1, source_target_pairs={{0,2},{1,3},{2,0},{3,1},{4,6},{5,7},{6,4},{7,5},{8,10},{9,11},{10,... | collective-permute-start | bytes 98312 | tf_op jit(solution)/shard_map/ppermute | solution.py:50
  29.1 0.5 %shard_map.105.refs_2_ = bf16[128,1024]{1,0:T(8,128)(2,1)S(1)} custom-call(bf16[2,512,512]{2,1,0:T(8,128)(2,1)S(1)} %copy-done.1, bf16[16,2048]{1,0:T(8,128)(2,1)S(1)} %pad_maximum_fusion.refs_1_, bf16[16,2048]{1,0:T(8,128)(2,1)S(1)} %collective-permute-done.3.refs_2_, bf16[16,2048]{1,0:T(8,128)(2,1)S(1)} %collective-permute-done.4.refs_3_, ...), custom_call_target="tpu_custom_call" | custom-call | flops 268435456 | bytes 1572864 | tf_op jit(solution)/shard_map/pallas_call | solution.py:33
  29.6 1.6 %collective-permute-done.11.refs_6_ = f32[64,128]{1,0:T(8,128)S(1)} collective-permute-done((f32[64,128]{1,0:T(8,128)S(1)}, f32[64,128]{1,0:T(8,128)S(1)}, u32[]{:S(2)}, u32[]{:S(2)}) %collective-permute-start.11) | collective-permute-done | bytes 32800 | tf_op jit(solution)/shard_map/ppermute | solution.py:50
  31.2 1.0 %shard_map.108 = (f32[2,8,64]{2,1,0:T(8,128)}, f32[4,2,512]{2,1,0:T(2,128)}) custom-call(f32[64,64]{1,0:T(8,128)S(1)} %fusion.refs_0_, f32[64,64]{1,0:T(8,128)S(1)} %fusion.4.refs_1_, bf16[128,1024]{1,0:T(8,128)(2,1)S(1)} %shard_map.105.refs_2_, bf16[128,1024]{1,0:T(8,128)(2,1)S(1)} %get-tuple-element.4.refs_3_, f32[64,128]{1,0:T(8,128)S(1)} %shard_map.107.refs_4_, ...), custom_call_target="tpu_custom_call" | custom-call | flops 33554432 | bytes 708608 | tf_op jit(solution)/shard_map/pallas_call | solution.py:33
  (33 shorter events, 1.7 us)
Async XLA Ops:
  0.6 8.1 %copy-start = (f32[7,2,512]{2,1,0:T(2,128)S(1)}, f32[7,2,512]{2,1,0:T(2,128)}, u32[]{:S(2)}) copy-start(f32[7,2,512]{2,1,0:T(2,128)} %param.13) | copy-start | bytes 86020
  0.6 19.9 %copy-start.1 = (bf16[2,512,512]{2,1,0:T(8,128)(2,1)S(1)}, bf16[2,512,512]{2,1,0:T(8,128)(2,1)}, u32[]{:S(2)}) copy-start(bf16[2,512,512]{2,1,0:T(8,128)(2,1)} %refs_2_.1) | copy-start | bytes 3145732
  1.5 9.0 %collective-permute-start = (bf16[8,1024]{1,0:T(8,128)(2,1)S(1)}, bf16[8,1024]{1,0:T(8,128)(2,1)S(1)}, u32[]{:S(2)}, u32[]{:S(2)}) collective-permute-start(bf16[8,1024]{1,0:T(8,128)(2,1)S(1)} %bitcast.30), channel_id=1, source_target_pairs={{0,1},{2,3},{1,0},{3,2},{4,5},{6,7},{5,4},{7,6},{8,9},{10,11},{9,8... | collective-permute-start | bytes 49160 | tf_op jit(solution)/shard_map/ppermute | solution.py:63
  2.1 8.5 %collective-permute-start.1 = (bf16[8,1024]{1,0:T(8,128)(2,1)S(1)}, bf16[8,1024]{1,0:T(8,128)(2,1)S(1)}, u32[]{:S(2)}, u32[]{:S(2)}) collective-permute-start(bf16[8,1024]{1,0:T(8,128)(2,1)S(1)} %bitcast.31), channel_id=1, source_target_pairs={{1,2},{2,1},{5,6},{6,5},{9,10},{10,9},{13,14},{14,13},{17,18},{18,... | collective-permute-start | bytes 49160 | tf_op jit(solution)/shard_map/ppermute | solution.py:62
  3.5 8.4 %collective-permute-start.6 = (bf16[8,2048]{1,0:T(8,128)(2,1)S(1)}, bf16[8,2048]{1,0:T(8,128)(2,1)S(1)}, u32[]{:S(2)}, u32[]{:S(2)}) collective-permute-start(bf16[8,2048]{1,0:T(8,128)(2,1)S(1)} %bitcast.25), channel_id=1, source_target_pairs={{0,16},{4,20},{8,24},{12,28},{16,0},{20,4},{24,8},{28,12},{1,17},{... | collective-permute-start | bytes 98312 | tf_op jit(solution)/shard_map/ppermute | solution.py:50
  10.6 0.7 %copy-start.2 = (f32[2,3]{1,0:T(2,128)S(1)}, f32[2,3]{1,0:T(2,128)}, u32[]{:S(2)}) copy-start(f32[2,3]{1,0:T(2,128)} %refs_0_.2) | copy-start | bytes 76
  11.8 4.9 %collective-permute-start.2 = (bf16[8,2048]{1,0:T(8,128)(2,1)S(1)}, bf16[8,2048]{1,0:T(8,128)(2,1)S(1)}, u32[]{:S(2)}, u32[]{:S(2)}) collective-permute-start(bf16[8,2048]{1,0:T(8,128)(2,1)S(1)} %shard_map.104), channel_id=1, source_target_pairs={{0,16},{4,20},{8,24},{12,28},{16,0},{20,4},{24,8},{28,12},{1,17},{... | collective-permute-start | bytes 98312 | tf_op jit(solution)/shard_map/ppermute | solution.py:50
  11.9 7.9 %collective-permute-start.7 = (bf16[16,2048]{1,0:T(8,128)(2,1)S(1)}, bf16[16,2048]{1,0:T(8,128)(2,1)S(1)}, u32[]{:S(2)}, u32[]{:S(2)}) collective-permute-start(bf16[16,2048]{1,0:T(8,128)(2,1)S(1)} %pad_maximum_fusion.1.refs_3_), channel_id=1, source_target_pairs={{0,8},{4,12},{8,0},{12,4},{16,24},{20,28},{24,16},{28,20},{1,9},{5... | collective-permute-start | bytes 196616 | tf_op jit(solution)/shard_map/ppermute | solution.py:50
  13.9 6.7 %collective-permute-start.8 = (bf16[16,2048]{1,0:T(8,128)(2,1)S(1)}, bf16[16,2048]{1,0:T(8,128)(2,1)S(1)}, u32[]{:S(2)}, u32[]{:S(2)}) collective-permute-start(bf16[16,2048]{1,0:T(8,128)(2,1)S(1)} %pad_maximum_fusion.1.refs_3_), channel_id=1, source_target_pairs={{0,4},{4,0},{8,12},{12,8},{16,20},{20,16},{24,28},{28,24},{1,5},{5... | collective-permute-start | bytes 196616 | tf_op jit(solution)/shard_map/ppermute | solution.py:50
  15.4 5.2 %collective-permute-start.9 = (bf16[16,2048]{1,0:T(8,128)(2,1)S(1)}, bf16[16,2048]{1,0:T(8,128)(2,1)S(1)}, u32[]{:S(2)}, u32[]{:S(2)}) collective-permute-start(bf16[16,2048]{1,0:T(8,128)(2,1)S(1)} %pad_maximum_fusion.1.refs_3_), channel_id=1, source_target_pairs={{0,12},{4,8},{8,4},{12,0},{16,28},{20,24},{24,20},{28,16},{1,13},{... | collective-permute-start | bytes 196616 | tf_op jit(solution)/shard_map/ppermute | solution.py:50
  16.7 4.8 %collective-permute-start.3 = (bf16[16,2048]{1,0:T(8,128)(2,1)S(1)}, bf16[16,2048]{1,0:T(8,128)(2,1)S(1)}, u32[]{:S(2)}, u32[]{:S(2)}) collective-permute-start(bf16[16,2048]{1,0:T(8,128)(2,1)S(1)} %pad_maximum_fusion.refs_1_), channel_id=1, source_target_pairs={{0,8},{4,12},{8,0},{12,4},{16,24},{20,28},{24,16},{28,20},{1,9},{5... | collective-permute-start | bytes 196616 | tf_op jit(solution)/shard_map/ppermute | solution.py:50
  18.3 4.7 %collective-permute-start.4 = (bf16[16,2048]{1,0:T(8,128)(2,1)S(1)}, bf16[16,2048]{1,0:T(8,128)(2,1)S(1)}, u32[]{:S(2)}, u32[]{:S(2)}) collective-permute-start(bf16[16,2048]{1,0:T(8,128)(2,1)S(1)} %pad_maximum_fusion.refs_1_), channel_id=1, source_target_pairs={{0,4},{4,0},{8,12},{12,8},{16,20},{20,16},{24,28},{28,24},{1,5},{5... | collective-permute-start | bytes 196616 | tf_op jit(solution)/shard_map/ppermute | solution.py:50
  19.8 5.6 %collective-permute-start.5 = (bf16[16,2048]{1,0:T(8,128)(2,1)S(1)}, bf16[16,2048]{1,0:T(8,128)(2,1)S(1)}, u32[]{:S(2)}, u32[]{:S(2)}) collective-permute-start(bf16[16,2048]{1,0:T(8,128)(2,1)S(1)} %pad_maximum_fusion.refs_1_), channel_id=1, source_target_pairs={{0,12},{4,8},{8,4},{12,0},{16,28},{20,24},{24,20},{28,16},{1,13},{... | collective-permute-start | bytes 196616 | tf_op jit(solution)/shard_map/ppermute | solution.py:50
  25.8 3.8 %collective-permute-start.10 = (f32[64,128]{1,0:T(8,128)S(1)}, f32[64,128]{1,0:T(8,128)S(1)}, u32[]{:S(2)}, u32[]{:S(2)}) collective-permute-start(f32[64,128]{1,0:T(8,128)S(1)} %shard_map.107.refs_4_), channel_id=1, source_target_pairs={{0,3},{1,2},{2,1},{3,0},{4,7},{5,6},{6,5},{7,4},{8,11},{9,10},{10,... | collective-permute-start | bytes 98312 | tf_op jit(solution)/shard_map/ppermute | solution.py:50
  25.9 5.3 %collective-permute-start.11 = (f32[64,128]{1,0:T(8,128)S(1)}, f32[64,128]{1,0:T(8,128)S(1)}, u32[]{:S(2)}, u32[]{:S(2)}) collective-permute-start(f32[64,128]{1,0:T(8,128)S(1)} %shard_map.107.refs_4_), channel_id=1, source_target_pairs={{0,2},{1,3},{2,0},{3,1},{4,6},{5,7},{6,4},{7,5},{8,10},{9,11},{10,... | collective-permute-start | bytes 98312 | tf_op jit(solution)/shard_map/ppermute | solution.py:50
  29.0 2.2 %collective-permute-start.12 = (f32[64,128]{1,0:T(8,128)S(1)}, f32[64,128]{1,0:T(8,128)S(1)}, u32[]{:S(2)}, u32[]{:S(2)}) collective-permute-start(f32[64,128]{1,0:T(8,128)S(1)} %shard_map.107.refs_4_), channel_id=1, source_target_pairs={{0,1},{1,0},{2,3},{3,2},{4,5},{5,4},{6,7},{7,6},{8,9},{9,8},{10,11... | collective-permute-start | bytes 98312 | tf_op jit(solution)/shard_map/ppermute | solution.py:50

commit v2 on v1

--- a/solution.py
+++ b/solution.py
@@ -18,27 +18,25 @@
     return math.prod(item.shape) * jnp.dtype(item.dtype).itemsize
 
 
-def local_call(fn, outs, arrays, scalars=(), flops=0):
+def local_call(fn, outs, arrays, flops=0):
     moved = sum(size_of(item) for item in (*arrays, *outs))
     if moved > VMEM_BYTES:
-        return fn(*scalars, *arrays)
-    first = len(scalars)
-    count = first + len(arrays)
+        return fn(*arrays)
+    count = len(arrays)
 
     def kernel(*refs):
-        values = fn(*refs[:first], *[ref[...] for ref in refs[first:count]])
+        values = fn(*[ref[...] for ref in refs[:count]])
         for ref, value in zip(refs[count:], values):
             ref[...] = value
 
     return pl.pallas_call(
         kernel,
         out_shape=tuple(outs),
-        in_specs=[pl.BlockSpec(memory_space=pltpu.SMEM)] * first
-        + [pl.BlockSpec(memory_space=pltpu.VMEM)] * len(arrays),
+        in_specs=[pl.BlockSpec(memory_space=pltpu.VMEM)] * count,
         out_specs=tuple(pl.BlockSpec(memory_space=pltpu.VMEM) for _ in outs),
         cost_estimate=pl.CostEstimate(flops=flops, bytes_accessed=moved, transcendentals=0),
         compiler_params=pltpu.CompilerParams(vmem_limit_bytes=48 << 20),
-    )(*scalars, *arrays)
+    )(*arrays)
 
 
 def array(shape, dtype):
@@ -54,14 +52,14 @@
     peers = lax.axis_size("row")
     odd = lax.axis_index("row") % 2 == 1
     modes = fields.shape[0]
-    first = fields[:, 0].reshape(modes, -1)
-    last = fields[:, -1].reshape(modes, -1)
     even_pairs = [(i, i + 1) for i in range(0, peers - 1, 2)]
     odd_pairs = [(i, i + 1) for i in range(1, peers - 1, 2)]
     both_ways = lambda pairs: pairs + [(j, i) for i, j in pairs]
-    over_odd = lax.ppermute(jnp.where(odd, last, first), "row", both_ways(odd_pairs))
-    over_even = lax.ppermute(jnp.where(odd, first, last), "row", both_ways(even_pairs))
-    return jnp.where(odd, over_even, over_odd), jnp.where(odd, over_odd, over_even)
+    over_odd = lax.ppermute(fields, "row", both_ways(odd_pairs))
+    over_even = lax.ppermute(fields, "row", both_ways(even_pairs))
+    before = jnp.where(odd, over_even[:, -1], over_odd[:, -1])
+    after = jnp.where(odd, over_odd[:, 0], over_even[:, 0])
+    return before.reshape(modes, -1), after.reshape(modes, -1)
 
 
 def rounds_of(peers):
@@ -85,7 +83,7 @@
             sources = (j + 1, j, j - 1)
             total_real = total_imag = 0.0
             for k in range(3):
-                a, b = taps[0, k], taps[1, k]
+                a, b = taps[0:1, k : k + 1], taps[1:2, k : k + 1]
                 total_real = total_real + a * real[sources[k]] + b * imag[sources[k]]
                 total_imag = total_imag + a * imag[sources[k]] - b * real[sources[k]]
             out_real.append(total_real)
@@ -202,27 +200,31 @@
     half = rows * width
 
     flat = lambda fields: fields.transpose(0, 2, 1, 3).reshape(local_modes, 2 * half)
-    own_forward, own_backward = flat(forward), flat(backward)
-
+    own_backward = flat(backward)
     before, after = neighbour_rows(backward)
     (own_pulled,) = local_call(
         pulled_rows(rows, width),
         [array((local_modes, 2 * half), BF16)],
-        [own_backward, before, after],
-        [row_taps],
+        [jnp.pad(row_taps, ((0, 6), (0, 125))), own_backward, before, after],
         flops=24 * local_modes * half,
     )
 
     head, last = rounds_of(mode_peers)
-    keys = [0]
-    fields, targets = own_forward, own_pulled
+    distances = head + last[:2]
+    fields, targets = forward, own_pulled
     for distance in head:
-        fields = jnp.concatenate([fields, swapped(fields, "mode", distance)], axis=0)
+        received = swapped(fields, "mode", distance)
+        if fields.ndim > 2:
+            fields, received = flat(fields), flat(received)
+        fields = jnp.concatenate([fields, received], axis=0)
         targets = jnp.concatenate([targets, swapped(targets, "mode", distance)], axis=0)
-        keys = keys + [key ^ distance for key in keys]
+    if fields.ndim > 2:
+        fields = flat(fields)
+    targets, pair_list, plane_index, wave_ratio, phase_masks = lax.optimization_barrier(
+        (targets, pair_list, plane_index, wave_ratio, phase_masks)
+    )
     field_pieces = [fields] + [swapped(fields, "mode", distance) for distance in last]
     target_pieces = [targets] + [swapped(targets, "mode", distance) for distance in last]
-    keys = keys + [key ^ distance for distance in last for key in keys]
 
     planes = jnp.arange(phase_masks.shape[0], dtype=jnp.int32)
     selector = (plane_index[:, None] == planes[None, :]).astype(F32)
@@ -231,16 +233,18 @@
     cosine = jnp.tile(jnp.cos(phases), (2, 1))
     sine = jnp.tile(jnp.sin(phases), (2, 1))
 
-    peers = jnp.asarray(keys, jnp.int32) ^ lax.axis_index("mode").astype(jnp.int32)
-    lanes = jnp.arange(local_modes, dtype=jnp.int32)
-    numbers = (peers[:, None] * local_modes + lanes[None, :]).reshape(total)
+    places = jnp.arange(total, dtype=jnp.int32)
+    peers = lax.axis_index("mode").astype(jnp.int32)
+    for k, distance in enumerate(distances):
+        peers = peers ^ ((places // (local_modes << k)) % 2 * distance)
+    numbers = peers * local_modes + places % local_modes
     groups = numbers // group_size
     to_target = (pair_list[:, 0][:, None] == groups[None, :]).astype(BF16)
     to_forward = (pair_list[:, 1][:, None] == groups[None, :]).astype(BF16)
     mask = lax.dot_general(
         to_forward, to_target, (((0,), (0,)), ((), ())), preferred_element_type=F32
     )
-    order = (numbers[:, None] == jnp.arange(total, dtype=jnp.int32)[None, :]).astype(F32)
+    order = (numbers[:, None] == places[None, :]).astype(F32)
 
     masked, spread = local_call(
         spread_all(width),

time: 32.8 us -> 29.2 us (0.89)
  other arithmetic: 1.69 us -> 0.14 us
  local copies, waits for them, and re-layouts: 3.12 us -> 2.3 us
  waiting for transfers between devices: 7.2 us -> 6.51 us
  Pallas kernels: 2.89 us -> 2.44 us
    unnamed x1, other arithmetic: 0.86 us -> 0.04 us
    transpose x2 -> x3, local copies, waits for them, and re-layouts: 1.54 us -> 0.79 us  [body(): fields.transpose(0, 2, 1, 3).reshape(local_modes, 2 * half)]
    ppermute x11, waiting for transfers between devices: 7.2 us -> 6.5 us  [swapped(): return lax.ppermute(values, axis, [(i, i ^ distance) for i in range(peers)])]
    pad x0 -> x1, local copies, waits for them, and re-layouts: none -> 0.68 us  [body(): jnp.pad(row_taps, ((0, 6), (0, 125)))]
    unnamed x8, local copies, waits for them, and re-layouts: 0.7 us -> 0.03 us
    mul x1 -> x0, other arithmetic: 0.66 us -> none  [body(): numbers = (peers[:, None] * local_modes + lanes[None, :]).reshape(total)]
    pallas_call x5, Pallas kernels: 2.89 us -> 2.44 us  [local_call(): pl.pallas_call(kernel, out_shape=tuple(outs), in_specs=[pl.BlockSpec(memo...]
  transfers between devices with their start and end apart: 13 -> 13, of which waited for: 5 -> 5; matrix products, arithmetic and copies ran while one was open for 14% -> 13% of each run, Pallas kernels for 5% -> 4%
where the time goes in v2:
time: 29.2 us; the launch traced here: 28.8 us
  starting transfers between devices  15.3 us (52%)
  waiting for transfers between devices  6.51 us (22%)
  Pallas kernels  2.44 us (8%)
  local copies, waits for them, and re-layouts  2.3 us (8%)
  matrix products  1.26 us (4%)
  between operations  0.83 us (3%)
    ppermute x11, starting transfers between devices, swapped(): return lax.ppermute(values, axis, [(i, i ^ distance) for i in range(peers)])  14.2 us
    ppermute x11, waiting for transfers between devices, swapped(): return lax.ppermute(values, axis, [(i, i ^ distance) for i in range(peers)])  6.5 us
    pallas_call x5, Pallas kernels, local_call(): pl.pallas_call(kernel, out_shape=tuple(outs), in_specs=[pl.BlockSpec(memo...  2.44 us
    dot_general x1, matrix products, body(): jnp.einsum('wp,prc->wrc', selector, phase_masks, precision=lax.Precision....  1 us
    transpose x3, local copies, waits for them, and re-layouts, body(): fields.transpose(0, 2, 1, 3).reshape(local_modes, 2 * half)  0.79 us
    eq x1, local copies, waits for them, and re-layouts, body(): to_forward = (pair_list[:, 1][:, None] == groups[None, :]).astype(BF16)  0.76 us
    pad x1, local copies, waits for them, and re-layouts, body(): jnp.pad(row_taps, ((0, 6), (0, 125)))  0.68 us
    ppermute x1, starting transfers between devices, neighbour_rows(): over_odd = lax.ppermute(fields, 'row', both_ways(odd_pairs))  0.65 us
  transfers between devices with their start and end apart: 13, of which 5 were waited for; matrix products, arithmetic and copies ran while one was open for 13% of the time, Pallas kernels for 4%

profile of v2, /device:TPU:0, one launch (start us, length us, event | category | flops | bytes accessed | tf_op | source)
XLA Modules:
  0.0 28.8 jit_solution(3078838332101402178)
XLA Ops:
  0.7 0.5 %collective-permute-start = (bf16[8,2,2,512]{3,2,1,0:T(2,128)(2,1)}, bf16[8,2,2,512]{3,2,1,0:T(2,128)(2,1)S(1)}, u32[]{:S(2)}, u32[]{:S(2)}) collective-permute-start(bf16[8,2,2,512]{3,2,1,0:T(2,128)(2,1)} %param.9), channel_id=1, source_target_pairs={{0,1},{2,3},{1,0},{3,2},{4,5},{6,7},{5,4},{7,6},{8,9},{10,11},{9,8... | collective-permute-start | bytes 98312 | tf_op jit(solution)/shard_map/ppermute | solution.py:59
  1.2 0.7 %collective-permute-start.1 = (bf16[8,2,2,512]{3,2,1,0:T(2,128)(2,1)}, bf16[8,2,2,512]{3,2,1,0:T(2,128)(2,1)S(1)}, u32[]{:S(2)}, u32[]{:S(2)}) collective-permute-start(bf16[8,2,2,512]{3,2,1,0:T(2,128)(2,1)} %param.9), channel_id=1, source_target_pairs={{1,2},{2,1},{5,6},{6,5},{9,10},{10,9},{13,14},{14,13},{17,18},{18,... | collective-permute-start | bytes 98312 | tf_op jit(solution)/shard_map/ppermute | solution.py:58
  1.8 3.8 %collective-permute-start.6 = (bf16[8,2,2,512]{3,2,1,0:T(2,128)(2,1)}, bf16[8,2,2,512]{3,2,1,0:T(2,128)(2,1)S(1)}, u32[]{:S(2)}, u32[]{:S(2)}) collective-permute-start(bf16[8,2,2,512]{3,2,1,0:T(2,128)(2,1)} %param.8), channel_id=1, source_target_pairs={{0,16},{4,20},{8,24},{12,28},{16,0},{20,4},{24,8},{28,12},{1,17},{... | collective-permute-start | bytes 98312 | tf_op jit(solution)/shard_map/ppermute | solution.py:48
  5.8 0.8 %copy.12 = bf16[8,2,2,512]{3,0,2,1:T(8,128)(2,1)S(1)} copy(bf16[8,2,2,512]{3,1,2,0:T(2,128)(2,1)} %bitcast.31) | data formatting | bytes 65536 | tf_op jit(solution)/shard_map/transpose | solution.py:202
  6.5 0.7 %pad.4.refs_0_ = f32[8,128]{1,0:T(8,128)S(1)} pad(f32[2,3]{1,0:T(2,128)} %param.11, f32[]{:T(128)} %constant.108.clone.1), padding=0_6x0_125 | pad | bytes 4124 | tf_op jit(solution)/shard_map/jit(_pad)/pad | solution.py:208
  7.3 0.1 shard_map.95
  7.5 0.2 collective-permute-done.6
  7.8 2.0 %collective-permute-start.7 = (bf16[16,2048]{1,0:T(8,128)(2,1)S(1)}, bf16[16,2048]{1,0:T(8,128)(2,1)S(1)}, u32[]{:S(2)}, u32[]{:S(2)}) collective-permute-start(bf16[16,2048]{1,0:T(8,128)(2,1)S(1)} %pad_maximum_fusion.1.refs_3_), channel_id=1, source_target_pairs={{0,8},{4,12},{8,0},{12,4},{16,24},{20,28},{24,16},{28,20},{1,9},{5... | collective-permute-start | bytes 196616 | tf_op jit(solution)/shard_map/ppermute | solution.py:48
  9.8 1.5 %collective-permute-start.8 = (bf16[16,2048]{1,0:T(8,128)(2,1)S(1)}, bf16[16,2048]{1,0:T(8,128)(2,1)S(1)}, u32[]{:S(2)}, u32[]{:S(2)}) collective-permute-start(bf16[16,2048]{1,0:T(8,128)(2,1)S(1)} %pad_maximum_fusion.1.refs_3_), channel_id=1, source_target_pairs={{0,4},{4,0},{8,12},{12,8},{16,20},{20,16},{24,28},{28,24},{1,5},{5... | collective-permute-start | bytes 196616 | tf_op jit(solution)/shard_map/ppermute | solution.py:48
  11.3 1.1 %collective-permute-done.2 = bf16[8,2048]{1,0:T(8,128)(2,1)S(1)} collective-permute-done((bf16[8,2048]{1,0:T(8,128)(2,1)S(1)}, bf16[8,2048]{1,0:T(8,128)(2,1)S(1)}, u32[]{:S(2)}, u32[]{:S(2)}) %collective-permute-start.2) | collective-permute-done | bytes 32800 | tf_op jit(solution)/shard_map/ppermute | solution.py:48
  12.4 1.5 %collective-permute-start.3 = (bf16[16,2048]{1,0:T(8,128)(2,1)S(1)}, bf16[16,2048]{1,0:T(8,128)(2,1)S(1)}, u32[]{:S(2)}, u32[]{:S(2)}) collective-permute-start(bf16[16,2048]{1,0:T(8,128)(2,1)S(1)} %pad_maximum_fusion.refs_1_), channel_id=1, source_target_pairs={{0,8},{4,12},{8,0},{12,4},{16,24},{20,28},{24,16},{28,20},{1,9},{5... | collective-permute-start | bytes 196616 | tf_op jit(solution)/shard_map/ppermute | solution.py:48
  13.9 1.5 %collective-permute-start.4 = (bf16[16,2048]{1,0:T(8,128)(2,1)S(1)}, bf16[16,2048]{1,0:T(8,128)(2,1)S(1)}, u32[]{:S(2)}, u32[]{:S(2)}) collective-permute-start(bf16[16,2048]{1,0:T(8,128)(2,1)S(1)} %pad_maximum_fusion.refs_1_), channel_id=1, source_target_pairs={{0,4},{4,0},{8,12},{12,8},{16,20},{20,16},{24,28},{28,24},{1,5},{5... | collective-permute-start | bytes 196616 | tf_op jit(solution)/shard_map/ppermute | solution.py:48
  15.4 1.0 %fusion.24 = (f32[4,2,512]{2,0,1:T(4,128)S(1)}, f32[4,2,512]{2,0,1:T(4,128)S(1)}) fusion(f32[4]{0:T(128)} %param.14, f32[7,2,512]{2,1,0:T(2,128)S(1)} %copy-done, s32[4]{0:T(128)} %param.13), kind=kOutput, calls=%fused_computation.56 | convolution fusion | flops 348188 | bytes 61472 | tf_op jit(solution)/shard_map/wp,prc->wrc/dot_general | solution.py:231
  16.4 0.6 %collective-permute-start.5 = (bf16[16,2048]{1,0:T(8,128)(2,1)S(1)}, bf16[16,2048]{1,0:T(8,128)(2,1)S(1)}, u32[]{:S(2)}, u32[]{:S(2)}) collective-permute-start(bf16[16,2048]{1,0:T(8,128)(2,1)S(1)} %pad_maximum_fusion.refs_1_), channel_id=1, source_target_pairs={{0,12},{4,8},{8,4},{12,0},{16,28},{20,24},{24,20},{28,16},{1,13},{... | collective-permute-start | bytes 196616 | tf_op jit(solution)/shard_map/ppermute | solution.py:48
  17.0 0.8 %slice_bitcast_fusion.1 = (s32[80]{0:T(128)S(1)}, s32[80]{0:T(128)S(1)}) fusion(s32[80,2]{0,1:T(2,128)} %param.15), kind=kLoop, calls=%fused_computation.55 | loop fusion | bytes 1280 | tf_op jit(solution)/shard_map/eq | solution.py:243
  17.8 0.5 %shard_map.97 = (bf16[128,1024]{1,0:T(8,128)(2,1)S(1)}, bf16[128,1024]{1,0:T(8,128)(2,1)S(1)}) custom-call(f32[8,1024]{1,0:T(8,128)S(1)} %tile.9.refs_0_, f32[8,1024]{1,0:T(8,128)S(1)} %tile.21.refs_1_, bf16[2,512,512]{2,1,0:T(8,128)(2,1)S(1)} %copy-done.1, bf16[16,2048]{1,0:T(8,128)(2,1)S(1)} %pad_maximum_fusion.1.refs_3_, ...), custom_call_target="tpu_custom_call" | custom-call | flops 268435456 | bytes 1900544 | tf_op jit(solution)/shard_map/pallas_call | solution.py:32
  18.3 0.9 %collective-permute-done.4.refs_3_ = bf16[16,2048]{1,0:T(8,128)(2,1)S(1)} collective-permute-done((bf16[16,2048]{1,0:T(8,128)(2,1)S(1)}, bf16[16,2048]{1,0:T(8,128)(2,1)S(1)}, u32[]{:S(2)}, u32[]{:S(2)}) %collective-permute-start.4) | collective-permute-done | bytes 65568 | tf_op jit(solution)/shard_map/ppermute | solution.py:48
  19.3 2.9 %collective-permute-done.5.refs_4_ = bf16[16,2048]{1,0:T(8,128)(2,1)S(1)} collective-permute-done((bf16[16,2048]{1,0:T(8,128)(2,1)S(1)}, bf16[16,2048]{1,0:T(8,128)(2,1)S(1)}, u32[]{:S(2)}, u32[]{:S(2)}) %collective-permute-start.5) | collective-permute-done | bytes 65568 | tf_op jit(solution)/shard_map/ppermute | solution.py:48
  22.1 0.4 %shard_map.98.refs_4_ = f32[64,128]{1,0:T(8,128)S(1)} custom-call(bf16[128,1024]{1,0:T(8,128)(2,1)S(1)} %get-tuple-element.15.refs_0_, bf16[16,2048]{1,0:T(8,128)(2,1)S(1)} %pad_maximum_fusion.refs_1_, bf16[16,2048]{1,0:T(8,128)(2,1)S(1)} %collective-permute-done.3.refs_2_, bf16[16,2048]{1,0:T(8,128)(2,1)S(1)} %collective-permute-done.4.refs_3_, ...), custom_call_target="tpu_custom_call" | custom-call | flops 33554432 | bytes 557056 | tf_op jit(solution)/shard_map/pallas_call | solution.py:32
  22.6 3.1 %collective-permute-start.11 = (f32[64,128]{1,0:T(8,128)S(1)}, f32[64,128]{1,0:T(8,128)S(1)}, u32[]{:S(2)}, u32[]{:S(2)}) collective-permute-start(f32[64,128]{1,0:T(8,128)S(1)} %shard_map.98.refs_4_), channel_id=1, source_target_pairs={{0,2},{1,3},{2,0},{3,1},{4,6},{5,7},{6,4},{7,5},{8,10},{9,11},{10,... | collective-permute-start | bytes 98312 | tf_op jit(solution)/shard_map/ppermute | solution.py:48
  25.7 0.3 fusion.refs_0_
  25.9 0.5 %shard_map.96.refs_2_ = bf16[128,1024]{1,0:T(8,128)(2,1)S(1)} custom-call(bf16[2,512,512]{2,1,0:T(8,128)(2,1)S(1)} %copy-done.1, bf16[16,2048]{1,0:T(8,128)(2,1)S(1)} %pad_maximum_fusion.refs_1_, bf16[16,2048]{1,0:T(8,128)(2,1)S(1)} %collective-permute-done.3.refs_2_, bf16[16,2048]{1,0:T(8,128)(2,1)S(1)} %collective-permute-done.4.refs_3_, ...), custom_call_target="tpu_custom_call" | custom-call | flops 268435456 | bytes 1572864 | tf_op jit(solution)/shard_map/pallas_call | solution.py:32
  26.4 1.4 %collective-permute-done.11.refs_6_ = f32[64,128]{1,0:T(8,128)S(1)} collective-permute-done((f32[64,128]{1,0:T(8,128)S(1)}, f32[64,128]{1,0:T(8,128)S(1)}, u32[]{:S(2)}, u32[]{:S(2)}) %collective-permute-start.11) | collective-permute-done | bytes 32800 | tf_op jit(solution)/shard_map/ppermute | solution.py:48
  27.8 1.0 %shard_map.99 = (f32[2,8,64]{2,1,0:T(8,128)}, f32[4,2,512]{2,1,0:T(2,128)}) custom-call(f32[64,64]{1,0:T(8,128)S(1)} %fusion.refs_0_, f32[64,64]{1,0:T(8,128)S(1)} %fusion.4.refs_1_, bf16[128,1024]{1,0:T(8,128)(2,1)S(1)} %shard_map.96.refs_2_, bf16[128,1024]{1,0:T(8,128)(2,1)S(1)} %get-tuple-element.14.refs_3_, f32[64,128]{1,0:T(8,128)S(1)} %shard_map.98.refs_4_, ...), custom_call_target="tpu_custom_call" | custom-call | flops 33554432 | bytes 708608 | tf_op jit(solution)/shard_map/pallas_call | solution.py:32
  (31 shorter events, 0.6 us)
Async XLA Ops:
  0.6 14.8 %copy-start = (f32[7,2,512]{2,1,0:T(2,128)S(1)}, f32[7,2,512]{2,1,0:T(2,128)}, u32[]{:S(2)}) copy-start(f32[7,2,512]{2,1,0:T(2,128)} %param.12) | copy-start | bytes 86020
  0.6 5.1 %copy-start.2 = (bf16[8,2,2,512]{3,2,1,0:T(2,128)(2,1)S(1)}, bf16[8,2,2,512]{3,2,1,0:T(2,128)(2,1)}, u32[]{:S(2)}) copy-start(bf16[8,2,2,512]{3,2,1,0:T(2,128)(2,1)} %param.9) | copy-start | bytes 98308
  0.7 17.2 %copy-start.1 = (bf16[2,512,512]{2,1,0:T(8,128)(2,1)S(1)}, bf16[2,512,512]{2,1,0:T(8,128)(2,1)}, u32[]{:S(2)}) copy-start(bf16[2,512,512]{2,1,0:T(8,128)(2,1)} %refs_2_.1) | copy-start | bytes 3145732
  0.7 6.6 %collective-permute-start = (bf16[8,2,2,512]{3,2,1,0:T(2,128)(2,1)}, bf16[8,2,2,512]{3,2,1,0:T(2,128)(2,1)S(1)}, u32[]{:S(2)}, u32[]{:S(2)}) collective-permute-start(bf16[8,2,2,512]{3,2,1,0:T(2,128)(2,1)} %param.9), channel_id=1, source_target_pairs={{0,1},{2,3},{1,0},{3,2},{4,5},{6,7},{5,4},{7,6},{8,9},{10,11},{9,8... | collective-permute-start | bytes 98312 | tf_op jit(solution)/shard_map/ppermute | solution.py:59
  1.2 6.0 %collective-permute-start.1 = (bf16[8,2,2,512]{3,2,1,0:T(2,128)(2,1)}, bf16[8,2,2,512]{3,2,1,0:T(2,128)(2,1)S(1)}, u32[]{:S(2)}, u32[]{:S(2)}) collective-permute-start(bf16[8,2,2,512]{3,2,1,0:T(2,128)(2,1)} %param.9), channel_id=1, source_target_pairs={{1,2},{2,1},{5,6},{6,5},{9,10},{10,9},{13,14},{14,13},{17,18},{18,... | collective-permute-start | bytes 98312 | tf_op jit(solution)/shard_map/ppermute | solution.py:58
  1.8 5.9 %collective-permute-start.6 = (bf16[8,2,2,512]{3,2,1,0:T(2,128)(2,1)}, bf16[8,2,2,512]{3,2,1,0:T(2,128)(2,1)S(1)}, u32[]{:S(2)}, u32[]{:S(2)}) collective-permute-start(bf16[8,2,2,512]{3,2,1,0:T(2,128)(2,1)} %param.8), channel_id=1, source_target_pairs={{0,16},{4,20},{8,24},{12,28},{16,0},{20,4},{24,8},{28,12},{1,17},{... | collective-permute-start | bytes 98312 | tf_op jit(solution)/shard_map/ppermute | solution.py:48
  7.4 5.0 %collective-permute-start.2 = (bf16[8,2048]{1,0:T(8,128)(2,1)S(1)}, bf16[8,2048]{1,0:T(8,128)(2,1)S(1)}, u32[]{:S(2)}, u32[]{:S(2)}) collective-permute-start(bf16[8,2048]{1,0:T(8,128)(2,1)S(1)} %shard_map.95), channel_id=1, source_target_pairs={{0,16},{4,20},{8,24},{12,28},{16,0},{20,4},{24,8},{28,12},{1,17},{... | collective-permute-start | bytes 98312 | tf_op jit(solution)/shard_map/ppermute | solution.py:48
  7.8 8.6 %collective-permute-start.7 = (bf16[16,2048]{1,0:T(8,128)(2,1)S(1)}, bf16[16,2048]{1,0:T(8,128)(2,1)S(1)}, u32[]{:S(2)}, u32[]{:S(2)}) collective-permute-start(bf16[16,2048]{1,0:T(8,128)(2,1)S(1)} %pad_maximum_fusion.1.refs_3_), channel_id=1, source_target_pairs={{0,8},{4,12},{8,0},{12,4},{16,24},{20,28},{24,16},{28,20},{1,9},{5... | collective-permute-start | bytes 196616 | tf_op jit(solution)/shard_map/ppermute | solution.py:48
  9.8 8.1 %collective-permute-start.8 = (bf16[16,2048]{1,0:T(8,128)(2,1)S(1)}, bf16[16,2048]{1,0:T(8,128)(2,1)S(1)}, u32[]{:S(2)}, u32[]{:S(2)}) collective-permute-start(bf16[16,2048]{1,0:T(8,128)(2,1)S(1)} %pad_maximum_fusion.1.refs_3_), channel_id=1, source_target_pairs={{0,4},{4,0},{8,12},{12,8},{16,20},{20,16},{24,28},{28,24},{1,5},{5... | collective-permute-start | bytes 196616 | tf_op jit(solution)/shard_map/ppermute | solution.py:48
  11.2 6.6 %collective-permute-start.9 = (bf16[16,2048]{1,0:T(8,128)(2,1)S(1)}, bf16[16,2048]{1,0:T(8,128)(2,1)S(1)}, u32[]{:S(2)}, u32[]{:S(2)}) collective-permute-start(bf16[16,2048]{1,0:T(8,128)(2,1)S(1)} %pad_maximum_fusion.1.refs_3_), channel_id=1, source_target_pairs={{0,12},{4,8},{8,4},{12,0},{16,28},{20,24},{24,20},{28,16},{1,13},{... | collective-permute-start | bytes 196616 | tf_op jit(solution)/shard_map/ppermute | solution.py:48
  12.4 5.9 %collective-permute-start.3 = (bf16[16,2048]{1,0:T(8,128)(2,1)S(1)}, bf16[16,2048]{1,0:T(8,128)(2,1)S(1)}, u32[]{:S(2)}, u32[]{:S(2)}) collective-permute-start(bf16[16,2048]{1,0:T(8,128)(2,1)S(1)} %pad_maximum_fusion.refs_1_), channel_id=1, source_target_pairs={{0,8},{4,12},{8,0},{12,4},{16,24},{20,28},{24,16},{28,20},{1,9},{5... | collective-permute-start | bytes 196616 | tf_op jit(solution)/shard_map/ppermute | solution.py:48
  13.9 5.4 %collective-permute-start.4 = (bf16[16,2048]{1,0:T(8,128)(2,1)S(1)}, bf16[16,2048]{1,0:T(8,128)(2,1)S(1)}, u32[]{:S(2)}, u32[]{:S(2)}) collective-permute-start(bf16[16,2048]{1,0:T(8,128)(2,1)S(1)} %pad_maximum_fusion.refs_1_), channel_id=1, source_target_pairs={{0,4},{4,0},{8,12},{12,8},{16,20},{20,16},{24,28},{28,24},{1,5},{5... | collective-permute-start | bytes 196616 | tf_op jit(solution)/shard_map/ppermute | solution.py:48
  16.4 5.7 %collective-permute-start.5 = (bf16[16,2048]{1,0:T(8,128)(2,1)S(1)}, bf16[16,2048]{1,0:T(8,128)(2,1)S(1)}, u32[]{:S(2)}, u32[]{:S(2)}) collective-permute-start(bf16[16,2048]{1,0:T(8,128)(2,1)S(1)} %pad_maximum_fusion.refs_1_), channel_id=1, source_target_pairs={{0,12},{4,8},{8,4},{12,0},{16,28},{20,24},{24,20},{28,16},{1,13},{... | collective-permute-start | bytes 196616 | tf_op jit(solution)/shard_map/ppermute | solution.py:48
  22.5 3.9 %collective-permute-start.10 = (f32[64,128]{1,0:T(8,128)S(1)}, f32[64,128]{1,0:T(8,128)S(1)}, u32[]{:S(2)}, u32[]{:S(2)}) collective-permute-start(f32[64,128]{1,0:T(8,128)S(1)} %shard_map.98.refs_4_), channel_id=1, source_target_pairs={{0,3},{1,2},{2,1},{3,0},{4,7},{5,6},{6,5},{7,4},{8,11},{9,10},{10,... | collective-permute-start | bytes 98312 | tf_op jit(solution)/shard_map/ppermute | solution.py:48
  22.6 5.2 %collective-permute-start.11 = (f32[64,128]{1,0:T(8,128)S(1)}, f32[64,128]{1,0:T(8,128)S(1)}, u32[]{:S(2)}, u32[]{:S(2)}) collective-permute-start(f32[64,128]{1,0:T(8,128)S(1)} %shard_map.98.refs_4_), channel_id=1, source_target_pairs={{0,2},{1,3},{2,0},{3,1},{4,6},{5,7},{6,4},{7,5},{8,10},{9,11},{10,... | collective-permute-start | bytes 98312 | tf_op jit(solution)/shard_map/ppermute | solution.py:48
  25.6 2.2 %collective-permute-start.12 = (f32[64,128]{1,0:T(8,128)S(1)}, f32[64,128]{1,0:T(8,128)S(1)}, u32[]{:S(2)}, u32[]{:S(2)}) collective-permute-start(f32[64,128]{1,0:T(8,128)S(1)} %shard_map.98.refs_4_), channel_id=1, source_target_pairs={{0,1},{1,0},{2,3},{3,2},{4,5},{5,4},{6,7},{7,6},{8,9},{9,8},{10,11... | collective-permute-start | bytes 98312 | tf_op jit(solution)/shard_map/ppermute | solution.py:48

commit v3 on v2

--- a/solution.py
+++ b/solution.py
@@ -67,6 +67,11 @@
     head, tail = bits[:-2], bits[-2:]
     last = [tail[0], tail[1], tail[0] ^ tail[1]] if len(tail) == 2 else tail
     return head, last
+
+
+def gathered_last(values, last):
+    pieces = [swapped(values, "mode", distance) for distance in reversed(last)]
+    return [values] + pieces[::-1]
 
 
 def pulled_rows(rows, width):
@@ -211,20 +216,19 @@
 
     head, last = rounds_of(mode_peers)
     distances = head + last[:2]
-    fields, targets = forward, own_pulled
+    both = jnp.concatenate([flat(forward), own_pulled], axis=1)
+    fields = jnp.zeros((1, 1))
+    targets = both
     for distance in head:
-        received = swapped(fields, "mode", distance)
-        if fields.ndim > 2:
-            fields, received = flat(fields), flat(received)
-        fields = jnp.concatenate([fields, received], axis=0)
         targets = jnp.concatenate([targets, swapped(targets, "mode", distance)], axis=0)
     if fields.ndim > 2:
         fields = flat(fields)
     targets, pair_list, plane_index, wave_ratio, phase_masks = lax.optimization_barrier(
         (targets, pair_list, plane_index, wave_ratio, phase_masks)
     )
-    field_pieces = [fields] + [swapped(fields, "mode", distance) for distance in last]
-    target_pieces = [targets] + [swapped(targets, "mode", distance) for distance in last]
+    pieces = gathered_last(targets, last)
+    field_pieces = [p[:, : 2 * half] for p in pieces]
+    target_pieces = [p[:, 2 * half :] for p in pieces]
 
     planes = jnp.arange(phase_masks.shape[0], dtype=jnp.int32)
     selector = (plane_index[:, None] == planes[None, :]).astype(F32)

time: 29.2 us -> 27.3 us (0.935)
  starting transfers between devices: 15.3 us -> 11.2 us
  waiting for transfers between devices: 6.51 us -> 9.43 us
  matrix products: 1.26 us -> 0.59 us
    ppermute x11 -> x7, starting transfers between devices: 14.2 us -> 10 us  [swapped(): return lax.ppermute(values, axis, [(i, i ^ distance) for i in range(peers)])]
    ppermute x11 -> x7, waiting for transfers between devices: 6.5 us -> 9.42 us  [swapped(): return lax.ppermute(values, axis, [(i, i ^ distance) for i in range(peers)])]
    unnamed x8 -> x18, local copies, waits for them, and re-layouts: 0.03 us -> 2.09 us
    transpose x3 -> x2, local copies, waits for them, and re-layouts: 0.79 us -> 0.02 us  [body(): fields.transpose(0, 2, 1, 3).reshape(local_modes, 2 * half)]
    eq x1, local copies, waits for them, and re-layouts: 0.76 us -> 0.01 us  [body(): to_forward = (pair_list[:, 1][:, None] == groups[None, :]).astype(BF16)]
    pad x1, local copies, waits for them, and re-layouts: 0.68 us -> 0.01 us  [body(): jnp.pad(row_taps, ((0, 6), (0, 125)))]
    dot_general x1, matrix products: 1 us -> 0.33 us  [body(): jnp.einsum('wp,prc->wrc', selector, phase_masks, precision=lax.Precision....]
  transfers between devices with their start and end apart: 13 -> 9, of which waited for: 5 -> 4; matrix products, arithmetic and copies ran while one was open for 13% -> 3% of each run, Pallas kernels for 4% -> 2%
where the time goes in v3:
time: 27.3 us; the launch traced here: 26.9 us
  starting transfers between devices  11.2 us (41%)
  waiting for transfers between devices  9.43 us (35%)
  Pallas kernels  2.45 us (9%)
  local copies, waits for them, and re-layouts  2.2 us (8%)
  between operations  0.9 us (3%)
  matrix products  0.59 us (2%)
    ppermute x7, starting transfers between devices, swapped(): return lax.ppermute(values, axis, [(i, i ^ distance) for i in range(peers)])  10 us
    ppermute x7, waiting for transfers between devices, swapped(): return lax.ppermute(values, axis, [(i, i ^ distance) for i in range(peers)])  9.42 us
    pallas_call x5, Pallas kernels, local_call(): pl.pallas_call(kernel, out_shape=tuple(outs), in_specs=[pl.BlockSpec(memo...  2.45 us
    unnamed x18, local copies, waits for them, and re-layouts  2.09 us
    ppermute x1, starting transfers between devices, neighbour_rows(): over_odd = lax.ppermute(fields, 'row', both_ways(odd_pairs))  0.65 us
  transfers between devices with their start and end apart: 9, of which 4 were waited for; matrix products, arithmetic and copies ran while one was open for 3% of the time, Pallas kernels for 2%

profile of v3, /device:TPU:0, one launch (start us, length us, event | category | flops | bytes accessed | tf_op | source)
XLA Modules:
  0.0 26.9 jit_solution(15020170287261573937)
XLA Ops:
  0.7 0.5 %collective-permute-start = (bf16[8,2,2,512]{3,2,1,0:T(2,128)(2,1)}, bf16[8,2,2,512]{3,2,1,0:T(2,128)(2,1)S(1)}, u32[]{:S(2)}, u32[]{:S(2)}) collective-permute-start(bf16[8,2,2,512]{3,2,1,0:T(2,128)(2,1)} %param.9), channel_id=1, source_target_pairs={{0,1},{2,3},{1,0},{3,2},{4,5},{6,7},{5,4},{7,6},{8,9},{10,11},{9,8... | collective-permute-start | bytes 98312 | tf_op jit(solution)/shard_map/ppermute | solution.py:59
  1.2 0.7 %collective-permute-start.1 = (bf16[8,2,2,512]{3,2,1,0:T(2,128)(2,1)}, bf16[8,2,2,512]{3,2,1,0:T(2,128)(2,1)S(1)}, u32[]{:S(2)}, u32[]{:S(2)}) collective-permute-start(bf16[8,2,2,512]{3,2,1,0:T(2,128)(2,1)} %param.9), channel_id=1, source_target_pairs={{1,2},{2,1},{5,6},{6,5},{9,10},{10,9},{13,14},{14,13},{17,18},{18,... | collective-permute-start | bytes 98312 | tf_op jit(solution)/shard_map/ppermute | solution.py:58
  1.9 0.7 %copy-done.2 = bf16[8,2,2,512]{3,2,1,0:T(2,128)(2,1)S(1)} copy-done((bf16[8,2,2,512]{3,2,1,0:T(2,128)(2,1)S(1)}, bf16[8,2,2,512]{3,2,1,0:T(2,128)(2,1)}, u32[]{:S(2)}) %copy-start.2) | copy-done | bytes 32792
  2.7 0.7 %copy-done.5 = f32[2,3]{1,0:T(2,128)S(1)} copy-done((f32[2,3]{1,0:T(2,128)S(1)}, f32[2,3]{1,0:T(2,128)}, u32[]{:S(2)}) %copy-start.5) | copy-done | bytes 48
  3.4 0.1 shard_map.95
  3.6 3.7 %collective-permute-start.2 = (bf16[8,4096]{1,0:T(8,128)(2,1)S(1)}, bf16[8,4096]{1,0:T(8,128)(2,1)S(1)}, u32[]{:S(2)}, u32[]{:S(2)}) collective-permute-start(bf16[8,4096]{1,0:T(8,128)(2,1)S(1)} %pad_maximum_fusion.1), channel_id=1, source_target_pairs={{0,16},{4,20},{8,24},{12,28},{16,0},{20,4},{24,8},{28,12},{1,17},{... | collective-permute-start | bytes 196616 | tf_op jit(solution)/shard_map/ppermute | solution.py:48
  7.2 0.1 fusion.4.refs_1_
  7.3 2.2 %collective-permute-done.2 = bf16[8,4096]{1,0:T(8,128)(2,1)S(1)} collective-permute-done((bf16[8,4096]{1,0:T(8,128)(2,1)S(1)}, bf16[8,4096]{1,0:T(8,128)(2,1)S(1)}, u32[]{:S(2)}, u32[]{:S(2)}) %collective-permute-start.2) | collective-permute-done | bytes 65568 | tf_op jit(solution)/shard_map/ppermute | solution.py:48
  9.5 2.9 %collective-permute-start.5 = (bf16[16,4096]{1,0:T(8,128)(2,1)S(1)}, bf16[16,4096]{1,0:T(8,128)(2,1)S(1)}, u32[]{:S(2)}, u32[]{:S(2)}) collective-permute-start(bf16[16,4096]{1,0:T(8,128)(2,1)S(1)} %pad_maximum_fusion), channel_id=1, source_target_pairs={{0,12},{4,8},{8,4},{12,0},{16,28},{20,24},{24,20},{28,16},{1,13},{... | collective-permute-start | bytes 393224 | tf_op jit(solution)/shard_map/ppermute | solution.py:48
  12.4 0.5 %collective-permute-start.4 = (bf16[16,4096]{1,0:T(8,128)(2,1)S(1)}, bf16[16,4096]{1,0:T(8,128)(2,1)S(1)}, u32[]{:S(2)}, u32[]{:S(2)}) collective-permute-start(bf16[16,4096]{1,0:T(8,128)(2,1)S(1)} %pad_maximum_fusion), channel_id=1, source_target_pairs={{0,4},{4,0},{8,12},{12,8},{16,20},{20,16},{24,28},{28,24},{1,5},{5... | collective-permute-start | bytes 393224 | tf_op jit(solution)/shard_map/ppermute | solution.py:48
  12.9 0.1 collective-permute-start.3
  13.1 0.3 %fusion.28 = (f32[4,2,512]{2,0,1:T(4,128)S(1)}, f32[4,2,512]{2,0,1:T(4,128)S(1)}) fusion(f32[4]{0:T(128)S(1)} %copy-done.6, f32[7,2,512]{2,1,0:T(2,128)S(1)} %copy-done, s32[4]{0:T(128)S(1)} %copy-done.7), kind=kOutput, calls=%fused_computation.60 | convolution fusion | flops 348188 | bytes 61472 | tf_op jit(solution)/shard_map/wp,prc->wrc/dot_general | solution.py:235
  13.5 0.6 %copy-done.4 = s32[80,2]{0,1:T(2,128)S(1)} copy-done((s32[80,2]{0,1:T(2,128)S(1)}, s32[80,2]{0,1:T(2,128)}, u32[]{:S(2)}) %copy-start.4) | copy-done | bytes 664
  14.2 1.3 %collective-permute-done.5 = bf16[16,4096]{1,0:T(8,128)(2,1)S(1)} collective-permute-done((bf16[16,4096]{1,0:T(8,128)(2,1)S(1)}, bf16[16,4096]{1,0:T(8,128)(2,1)S(1)}, u32[]{:S(2)}, u32[]{:S(2)}) %collective-permute-start.5) | collective-permute-done | bytes 131104 | tf_op jit(solution)/shard_map/ppermute | solution.py:48
  15.4 4.6 %collective-permute-done.4 = bf16[16,4096]{1,0:T(8,128)(2,1)S(1)} collective-permute-done((bf16[16,4096]{1,0:T(8,128)(2,1)S(1)}, bf16[16,4096]{1,0:T(8,128)(2,1)S(1)}, u32[]{:S(2)}, u32[]{:S(2)}) %collective-permute-start.4) | collective-permute-done | bytes 131104 | tf_op jit(solution)/shard_map/ppermute | solution.py:48
  20.1 0.5 %shard_map.97 = (bf16[128,1024]{1,0:T(8,128)(2,1)S(1)}, bf16[128,1024]{1,0:T(8,128)(2,1)S(1)}) custom-call(f32[8,1024]{1,0:T(8,128)S(1)} %tile.9.refs_0_, f32[8,1024]{1,0:T(8,128)S(1)} %tile.21.refs_1_, bf16[2,512,512]{2,1,0:T(8,128)(2,1)S(1)} %copy-done.1, bf16[16,2048]{1,0:T(8,128)(2,1)S(1)} %get-tuple-element.22.refs_3_, ...), custom_call_target="tpu_custom_call" | custom-call | flops 268435456 | bytes 1900544 | tf_op jit(solution)/shard_map/pallas_call | solution.py:32
  20.6 0.3 %shard_map.98.refs_4_ = f32[64,128]{1,0:T(8,128)S(1)} custom-call(bf16[128,1024]{1,0:T(8,128)(2,1)S(1)} %get-tuple-element.15.refs_0_, bf16[16,2048]{1,0:T(8,128)(2,1)S(1)} %get-tuple-element.23.refs_1_, bf16[16,2048]{1,0:T(8,128)(2,1)S(1)} %get-tuple-element.21.refs_2_, bf16[16,2048]{1,0:T(8,128)(2,1)S(1)} %get-tuple-element.19.refs_3_, ...), custom_call_target="tpu_custom_call" | custom-call | flops 33554432 | bytes 557056 | tf_op jit(solution)/shard_map/pallas_call | solution.py:32
  20.9 0.1 collective-permute-start.6
  21.0 2.7 %collective-permute-start.7 = (f32[64,128]{1,0:T(8,128)S(1)}, f32[64,128]{1,0:T(8,128)S(1)}, u32[]{:S(2)}, u32[]{:S(2)}) collective-permute-start(f32[64,128]{1,0:T(8,128)S(1)} %shard_map.98.refs_4_), channel_id=1, source_target_pairs={{0,2},{1,3},{2,0},{3,1},{4,6},{5,7},{6,4},{7,5},{8,10},{9,11},{10,... | collective-permute-start | bytes 98312 | tf_op jit(solution)/shard_map/ppermute | solution.py:48
  23.7 0.0 collective-permute-start.8
  23.7 0.3 fusion.refs_0_
  24.0 0.5 %shard_map.96.refs_2_ = bf16[128,1024]{1,0:T(8,128)(2,1)S(1)} custom-call(bf16[2,512,512]{2,1,0:T(8,128)(2,1)S(1)} %copy-done.1, bf16[16,2048]{1,0:T(8,128)(2,1)S(1)} %get-tuple-element.23.refs_1_, bf16[16,2048]{1,0:T(8,128)(2,1)S(1)} %get-tuple-element.21.refs_2_, bf16[16,2048]{1,0:T(8,128)(2,1)S(1)} %get-tuple-element.19.refs_3_, ...), custom_call_target="tpu_custom_call" | custom-call | flops 268435456 | bytes 1572864 | tf_op jit(solution)/shard_map/pallas_call | solution.py:32
  24.5 1.4 %collective-permute-done.7.refs_6_ = f32[64,128]{1,0:T(8,128)S(1)} collective-permute-done((f32[64,128]{1,0:T(8,128)S(1)}, f32[64,128]{1,0:T(8,128)S(1)}, u32[]{:S(2)}, u32[]{:S(2)}) %collective-permute-start.7) | collective-permute-done | bytes 32800 | tf_op jit(solution)/shard_map/ppermute | solution.py:48
  25.8 1.0 %shard_map.99 = (f32[2,8,64]{2,1,0:T(8,128)}, f32[4,2,512]{2,1,0:T(2,128)}) custom-call(f32[64,64]{1,0:T(8,128)S(1)} %fusion.refs_0_, f32[64,64]{1,0:T(8,128)S(1)} %fusion.4.refs_1_, bf16[128,1024]{1,0:T(8,128)(2,1)S(1)} %shard_map.96.refs_2_, bf16[128,1024]{1,0:T(8,128)(2,1)S(1)} %get-tuple-element.14.refs_3_, f32[64,128]{1,0:T(8,128)S(1)} %shard_map.98.refs_4_, ...), custom_call_target="tpu_custom_call" | custom-call | flops 33554432 | bytes 708608 | tf_op jit(solution)/shard_map/pallas_call | solution.py:32
  (36 shorter events, 0.2 us)
Async XLA Ops:
  0.6 12.4 %copy-start = (f32[7,2,512]{2,1,0:T(2,128)S(1)}, f32[7,2,512]{2,1,0:T(2,128)}, u32[]{:S(2)}) copy-start(f32[7,2,512]{2,1,0:T(2,128)} %param.12) | copy-start | bytes 86020
  0.6 1.2 %copy-start.3 = (bf16[8,2,2,512]{3,2,1,0:T(2,128)(2,1)S(1)}, bf16[8,2,2,512]{3,2,1,0:T(2,128)(2,1)}, u32[]{:S(2)}) copy-start(bf16[8,2,2,512]{3,2,1,0:T(2,128)(2,1)} %param.9) | copy-start | bytes 98308
  0.7 2.7 %collective-permute-start = (bf16[8,2,2,512]{3,2,1,0:T(2,128)(2,1)}, bf16[8,2,2,512]{3,2,1,0:T(2,128)(2,1)S(1)}, u32[]{:S(2)}, u32[]{:S(2)}) collective-permute-start(bf16[8,2,2,512]{3,2,1,0:T(2,128)(2,1)} %param.9), channel_id=1, source_target_pairs={{0,1},{2,3},{1,0},{3,2},{4,5},{6,7},{5,4},{7,6},{8,9},{10,11},{9,8... | collective-permute-start | bytes 98312 | tf_op jit(solution)/shard_map/ppermute | solution.py:59
  1.2 2.2 %collective-permute-start.1 = (bf16[8,2,2,512]{3,2,1,0:T(2,128)(2,1)}, bf16[8,2,2,512]{3,2,1,0:T(2,128)(2,1)S(1)}, u32[]{:S(2)}, u32[]{:S(2)}) collective-permute-start(bf16[8,2,2,512]{3,2,1,0:T(2,128)(2,1)} %param.9), channel_id=1, source_target_pairs={{1,2},{2,1},{5,6},{6,5},{9,10},{10,9},{13,14},{14,13},{17,18},{18,... | collective-permute-start | bytes 98312 | tf_op jit(solution)/shard_map/ppermute | solution.py:58
  1.9 0.8 %copy-start.2 = (bf16[8,2,2,512]{3,2,1,0:T(2,128)(2,1)S(1)}, bf16[8,2,2,512]{3,2,1,0:T(2,128)(2,1)}, u32[]{:S(2)}) copy-start(bf16[8,2,2,512]{3,2,1,0:T(2,128)(2,1)} %param.8) | copy-start | bytes 98308
  2.6 0.7 %copy-start.5 = (f32[2,3]{1,0:T(2,128)S(1)}, f32[2,3]{1,0:T(2,128)}, u32[]{:S(2)}) copy-start(f32[2,3]{1,0:T(2,128)} %param.11) | copy-start | bytes 76
  2.6 10.4 %copy-start.6 = (f32[4]{0:T(128)S(1)}, f32[4]{0:T(128)}, u32[]{:S(2)}) copy-start(f32[4]{0:T(128)} %param.14) | copy-start | bytes 52
  2.6 10.4 %copy-start.7 = (s32[4]{0:T(128)S(1)}, s32[4]{0:T(128)}, u32[]{:S(2)}) copy-start(s32[4]{0:T(128)} %param.13) | copy-start | bytes 52
  3.3 16.8 %copy-start.1 = (bf16[2,512,512]{2,1,0:T(8,128)(2,1)S(1)}, bf16[2,512,512]{2,1,0:T(8,128)(2,1)}, u32[]{:S(2)}) copy-start(bf16[2,512,512]{2,1,0:T(8,128)(2,1)} %refs_2_.1) | copy-start | bytes 3145732
  3.6 5.9 %collective-permute-start.2 = (bf16[8,4096]{1,0:T(8,128)(2,1)S(1)}, bf16[8,4096]{1,0:T(8,128)(2,1)S(1)}, u32[]{:S(2)}, u32[]{:S(2)}) collective-permute-start(bf16[8,4096]{1,0:T(8,128)(2,1)S(1)} %pad_maximum_fusion.1), channel_id=1, source_target_pairs={{0,16},{4,20},{8,24},{12,28},{16,0},{20,4},{24,8},{28,12},{1,17},{... | collective-permute-start | bytes 196616 | tf_op jit(solution)/shard_map/ppermute | solution.py:48
  9.5 5.9 %collective-permute-start.5 = (bf16[16,4096]{1,0:T(8,128)(2,1)S(1)}, bf16[16,4096]{1,0:T(8,128)(2,1)S(1)}, u32[]{:S(2)}, u32[]{:S(2)}) collective-permute-start(bf16[16,4096]{1,0:T(8,128)(2,1)S(1)} %pad_maximum_fusion), channel_id=1, source_target_pairs={{0,12},{4,8},{8,4},{12,0},{16,28},{20,24},{24,20},{28,16},{1,13},{... | collective-permute-start | bytes 393224 | tf_op jit(solution)/shard_map/ppermute | solution.py:48
  12.4 7.7 %collective-permute-start.4 = (bf16[16,4096]{1,0:T(8,128)(2,1)S(1)}, bf16[16,4096]{1,0:T(8,128)(2,1)S(1)}, u32[]{:S(2)}, u32[]{:S(2)}) collective-permute-start(bf16[16,4096]{1,0:T(8,128)(2,1)S(1)} %pad_maximum_fusion), channel_id=1, source_target_pairs={{0,4},{4,0},{8,12},{12,8},{16,20},{20,16},{24,28},{28,24},{1,5},{5... | collective-permute-start | bytes 393224 | tf_op jit(solution)/shard_map/ppermute | solution.py:48
  12.9 7.1 %collective-permute-start.3 = (bf16[16,4096]{1,0:T(8,128)(2,1)S(1)}, bf16[16,4096]{1,0:T(8,128)(2,1)S(1)}, u32[]{:S(2)}, u32[]{:S(2)}) collective-permute-start(bf16[16,4096]{1,0:T(8,128)(2,1)S(1)} %pad_maximum_fusion), channel_id=1, source_target_pairs={{0,8},{4,12},{8,0},{12,4},{16,24},{20,28},{24,16},{28,20},{1,9},{5... | collective-permute-start | bytes 393224 | tf_op jit(solution)/shard_map/ppermute | solution.py:48
  13.5 0.7 %copy-start.4 = (s32[80,2]{0,1:T(2,128)S(1)}, s32[80,2]{0,1:T(2,128)}, u32[]{:S(2)}) copy-start(s32[80,2]{0,1:T(2,128)} %param.15) | copy-start | bytes 1924
  20.9 3.5 %collective-permute-start.6 = (f32[64,128]{1,0:T(8,128)S(1)}, f32[64,128]{1,0:T(8,128)S(1)}, u32[]{:S(2)}, u32[]{:S(2)}) collective-permute-start(f32[64,128]{1,0:T(8,128)S(1)} %shard_map.98.refs_4_), channel_id=1, source_target_pairs={{0,3},{1,2},{2,1},{3,0},{4,7},{5,6},{6,5},{7,4},{8,11},{9,10},{10,... | collective-permute-start | bytes 98312 | tf_op jit(solution)/shard_map/ppermute | solution.py:48
  21.0 4.8 %collective-permute-start.7 = (f32[64,128]{1,0:T(8,128)S(1)}, f32[64,128]{1,0:T(8,128)S(1)}, u32[]{:S(2)}, u32[]{:S(2)}) collective-permute-start(f32[64,128]{1,0:T(8,128)S(1)} %shard_map.98.refs_4_), channel_id=1, source_target_pairs={{0,2},{1,3},{2,0},{3,1},{4,6},{5,7},{6,4},{7,5},{8,10},{9,11},{10,... | collective-permute-start | bytes 98312 | tf_op jit(solution)/shard_map/ppermute | solution.py:48
  23.7 2.2 %collective-permute-start.8 = (f32[64,128]{1,0:T(8,128)S(1)}, f32[64,128]{1,0:T(8,128)S(1)}, u32[]{:S(2)}, u32[]{:S(2)}) collective-permute-start(f32[64,128]{1,0:T(8,128)S(1)} %shard_map.98.refs_4_), channel_id=1, source_target_pairs={{0,1},{1,0},{2,3},{3,2},{4,5},{5,4},{6,7},{7,6},{8,9},{9,8},{10,11... | collective-permute-start | bytes 98312 | tf_op jit(solution)/shard_map/ppermute | solution.py:48

commit v4 on v3

--- a/solution.py
+++ b/solution.py
@@ -48,30 +48,33 @@
     return lax.ppermute(values, axis, [(i, i ^ distance) for i in range(peers)])
 
 
-def neighbour_rows(fields):
+def pairs_of(peers, first):
+    pairs = [(i, i + 1) for i in range(first, peers - 1, 2)]
+    return pairs + [(j, i) for i, j in pairs]
+
+
+def neighbour_rows(fields, width):
     peers = lax.axis_size("row")
     odd = lax.axis_index("row") % 2 == 1
-    modes = fields.shape[0]
-    even_pairs = [(i, i + 1) for i in range(0, peers - 1, 2)]
-    odd_pairs = [(i, i + 1) for i in range(1, peers - 1, 2)]
-    both_ways = lambda pairs: pairs + [(j, i) for i, j in pairs]
-    over_odd = lax.ppermute(fields, "row", both_ways(odd_pairs))
-    over_even = lax.ppermute(fields, "row", both_ways(even_pairs))
-    before = jnp.where(odd, over_even[:, -1], over_odd[:, -1])
-    after = jnp.where(odd, over_odd[:, 0], over_even[:, 0])
-    return before.reshape(modes, -1), after.reshape(modes, -1)
+    half = fields.shape[1] // 2
+    row_at = lambda at: jnp.concatenate(
+        [fields[:, at : at + width], fields[:, half + at : half + at + width]], axis=1
+    )
+    first, last = row_at(0), row_at(half - width)
+    over_odd = lax.ppermute(jnp.where(odd, last, first), "row", pairs_of(peers, 1))
+    over_even = lax.ppermute(jnp.where(odd, first, last), "row", pairs_of(peers, 0))
+    return jnp.where(odd, over_even, over_odd), jnp.where(odd, over_odd, over_even)
 
 
 def rounds_of(peers):
     bits = [1 << k for k in reversed(range(peers.bit_length() - 1))]
     head, tail = bits[:-2], bits[-2:]
-    last = [tail[0], tail[1], tail[0] ^ tail[1]] if len(tail) == 2 else tail
+    last = [tail[0] ^ tail[1], tail[0], tail[1]] if len(tail) == 2 else tail
     return head, last
 
 
 def gathered_last(values, last):
-    pieces = [swapped(values, "mode", distance) for distance in reversed(last)]
-    return [values] + pieces[::-1]
+    return [values] + [swapped(values, "mode", distance) for distance in last]
 
 
 def pulled_rows(rows, width):
@@ -98,19 +101,19 @@
     return fn
 
 
-def halves(pieces):
-    whole = jnp.concatenate(pieces, axis=0) if len(pieces) > 1 else pieces[0]
-    half = whole.shape[1] // 2
-    return whole[:, :half], whole[:, half:]
+def parts_of(pieces, first):
+    quarter = pieces[0].shape[1] // 4
+    cut = lambda at: [piece[:, at * quarter : (at + 1) * quarter] for piece in pieces]
+    return jnp.concatenate(cut(first), axis=0), jnp.concatenate(cut(first + 1), axis=0)
 
 
 def by_rows(values, width):
     return [values[:, at : at + width] for at in range(0, values.shape[1], width)]
 
 
-def spread_all(width):
+def masked_and_spread(width):
     def fn(cosine, sine, propagator, *pieces):
-        real, imag = halves(pieces)
+        real, imag = parts_of(pieces, 0)
         total, half = real.shape
         shape = (total // cosine.shape[0], *cosine.shape)
         real = real.astype(F32).reshape(shape)
@@ -134,18 +137,28 @@
     return fn
 
 
-def project(spread, *pieces):
-    targets = jnp.concatenate(halves(pieces), axis=0)
-    total = targets.shape[0] // 2
-    product = lax.dot_general(spread, targets, NT, preferred_element_type=F32)
-    real = product[:total, :total] + product[total:, total:]
-    imag = product[total:, :total] - product[:total, total:]
-    return (jnp.concatenate([real, imag], axis=1),)
+def both_parts(stacks):
+    cut = lambda stack, part: stack[part * (stack.shape[0] // 2) :][: stack.shape[0] // 2]
+    return jnp.concatenate([cut(stack, part) for part in (0, 1) for stack in stacks], axis=0)
+
+
+def project(width, late):
+    def fn(cosine, sine, propagator, early_spread, *pieces):
+        masked, spread = masked_and_spread(width)(cosine, sine, propagator, *pieces[-late:])
+        spread = both_parts([early_spread, spread])
+        targets = jnp.concatenate(parts_of(pieces, 2), axis=0)
+        total = targets.shape[0] // 2
+        product = lax.dot_general(spread, targets, NT, preferred_element_type=F32)
+        real = product[:total, :total] + product[total:, total:]
+        imag = product[total:, :total] - product[:total, total:]
+        return masked, jnp.concatenate([real, imag], axis=1)
+
+    return fn
 
 
 def back_propagated(width):
     def fn(propagator, *pieces):
-        targets = jnp.concatenate(halves(pieces), axis=0)
+        targets = jnp.concatenate(parts_of(pieces, 2), axis=0)
         total = targets.shape[0] // 2
         stacked = jnp.concatenate(by_rows(targets, width), axis=0)
         over_real = lax.dot_general(stacked, propagator[0], NT, preferred_element_type=F32)
@@ -164,7 +177,7 @@
 
 
 def finish(local_modes, waves, rows, width, scale_pixels, scale_grad):
-    def fn(mask, order, back, masked, *partials):
+    def fn(mask, order, back, early, late, *partials):
         total = mask.shape[0]
         summed = partials[0]
         for part in partials[1:]:
@@ -183,7 +196,7 @@
             axis=0,
         )
         adjoint = jnp.dot(weights, back, preferred_element_type=F32)
-        fields = masked.astype(F32)
+        fields = both_parts([early, late]).astype(F32)
         term = fields[total:] * adjoint[:total] - fields[:total] * adjoint[total:]
         group = 2 * waves
         folded = jnp.sum(term.reshape(total // group, group, rows * width), axis=0)
@@ -204,31 +217,31 @@
     group_size = total // NG
     half = rows * width
 
-    flat = lambda fields: fields.transpose(0, 2, 1, 3).reshape(local_modes, 2 * half)
-    own_backward = flat(backward)
-    before, after = neighbour_rows(backward)
-    (own_pulled,) = local_call(
-        pulled_rows(rows, width),
-        [array((local_modes, 2 * half), BF16)],
-        [jnp.pad(row_taps, ((0, 6), (0, 125))), own_backward, before, after],
-        flops=24 * local_modes * half,
-    )
-
+    flat = lambda fields: fields.transpose(0, 2, 1, 3).reshape(fields.shape[0], 2 * half)
     head, last = rounds_of(mode_peers)
     distances = head + last[:2]
-    both = jnp.concatenate([flat(forward), own_pulled], axis=1)
-    fields = jnp.zeros((1, 1))
-    targets = both
+    targets, fields = backward, forward
     for distance in head:
-        targets = jnp.concatenate([targets, swapped(targets, "mode", distance)], axis=0)
-    if fields.ndim > 2:
-        fields = flat(fields)
-    targets, pair_list, plane_index, wave_ratio, phase_masks = lax.optimization_barrier(
-        (targets, pair_list, plane_index, wave_ratio, phase_masks)
-    )
-    pieces = gathered_last(targets, last)
-    field_pieces = [p[:, : 2 * half] for p in pieces]
-    target_pieces = [p[:, 2 * half :] for p in pieces]
+        near, far = (targets, fields), [
+            swapped(values, "mode", distance) for values in (targets, fields)
+        ]
+        if targets.ndim > 2:
+            near, far = [flat(values) for values in near], [flat(values) for values in far]
+        targets, fields = [jnp.concatenate(both, axis=0) for both in zip(near, far)]
+    if targets.ndim > 2:
+        targets, fields = flat(targets), flat(fields)
+    before, after = neighbour_rows(targets, width)
+    (pulled,) = local_call(
+        pulled_rows(rows, width),
+        [array(targets.shape, BF16)],
+        [jnp.pad(row_taps, ((0, 6), (0, 125))), targets, before, after],
+        flops=24 * targets.shape[0] * half,
+    )
+    both = jnp.concatenate([fields, pulled], axis=1)
+    both, pair_list, plane_index, wave_ratio, phase_masks = lax.optimization_barrier(
+        (both, pair_list, plane_index, wave_ratio, phase_masks)
+    )
+    pieces = gathered_last(both, last)
 
     planes = jnp.arange(phase_masks.shape[0], dtype=jnp.int32)
     selector = (plane_index[:, None] == planes[None, :]).astype(F32)
@@ -250,23 +263,26 @@
     )
     order = (numbers[:, None] == places[None, :]).astype(F32)
 
-    masked, spread = local_call(
-        spread_all(width),
-        [array((2 * total, half), BF16)] * 2,
-        [cosine, sine, propagator, *field_pieces],
-        flops=8 * total * half * width,
-    )
-    (partial,) = local_call(
-        project,
-        [array((total, 2 * total), F32)],
-        [spread, *target_pieces],
-        flops=8 * total * total * half,
+    early = (len(pieces) + 1) // 2
+    late = len(pieces) - early
+    early_total, late_total = early * both.shape[0], late * both.shape[0]
+    early_masked, early_spread = local_call(
+        masked_and_spread(width),
+        [array((2 * early_total, half), BF16)] * 2,
+        [cosine, sine, propagator, *pieces[:early]],
+        flops=8 * early_total * half * width,
+    )
+    late_masked, partial = local_call(
+        project(width, late),
+        [array((2 * late_total, half), BF16), array((total, 2 * total), F32)],
+        [cosine, sine, propagator, early_spread, *pieces],
+        flops=8 * late_total * half * width + 8 * total * total * half,
     )
     partials = [partial] + [swapped(partial, "row", d) for d in range(row_peers - 1, 0, -1)]
     (back,) = local_call(
         back_propagated(width),
         [array((2 * total, half), BF16)],
-        [propagator, *target_pieces],
+        [propagator, *pieces],
         flops=8 * total * half * width,
     )
     coupling, mask_grad = local_call(
@@ -279,7 +295,7 @@
             -2.0 / total,
         ),
         [array((2, local_modes, total), F32), array((waves, rows, width), F32)],
-        [mask, order, back, masked, *partials],
+        [mask, order, back, early_masked, late_masked, *partials],
         flops=8 * total * total * half,
     )
     return coupling, mask_grad

time: 27.3 us -> 27 us (0.989)
  waiting for transfers between devices: 9.43 us -> 8.77 us
    unnamed x18 -> x12, local copies, waits for them, and re-layouts: 2.09 us -> 0.68 us
    transpose x2 -> x4, local copies, waits for them, and re-layouts: 0.02 us -> 0.8 us  [body(): fields.transpose(0, 2, 1, 3).reshape(fields.shape[0], 2 * half)]
    pad x1, local copies, waits for them, and re-layouts: 0.01 us -> 0.68 us  [body(): jnp.pad(row_taps, ((0, 6), (0, 125)))]
    ppermute x7 -> x8, waiting for transfers between devices: 9.42 us -> 8.77 us  [swapped(): return lax.ppermute(values, axis, [(i, i ^ distance) for i in range(peers)])]
    ppermute x7 -> x8, starting transfers between devices: 10 us -> 10.6 us  [swapped(): return lax.ppermute(values, axis, [(i, i ^ distance) for i in range(peers)])]
    ppermute x2, starting transfers between devices: 1.17 us -> 0.73 us  [the longest x1 0.66 us: neighbour_rows(): lax.ppermute(jnp.where(odd, last, first), 'row', pairs_of(peers, 1))]
  transfers between devices with their start and end apart: 9 -> 10, of which waited for: 4 -> 6; matrix products, arithmetic and copies ran while one was open for 3% -> 8% of each run, Pallas kernels for 2% -> 3%
where the time goes in v4:
time: 27 us; the launch traced here: 26.6 us
  starting transfers between devices  11.3 us (42%)
  waiting for transfers between devices  8.77 us (32%)
  Pallas kernels  2.65 us (10%)
  local copies, waits for them, and re-layouts  2.22 us (8%)
  between operations  0.86 us (3%)
  matrix products  0.59 us (2%)
    ppermute x8, starting transfers between devices, swapped(): return lax.ppermute(values, axis, [(i, i ^ distance) for i in range(peers)])  10.6 us
    ppermute x8, waiting for transfers between devices, swapped(): return lax.ppermute(values, axis, [(i, i ^ distance) for i in range(peers)])  8.77 us
    pallas_call x5, Pallas kernels, local_call(): pl.pallas_call(kernel, out_shape=tuple(outs), in_specs=[pl.BlockSpec(memo...  2.65 us
    transpose x4, local copies, waits for them, and re-layouts, body(): fields.transpose(0, 2, 1, 3).reshape(fields.shape[0], 2 * half)  0.8 us
    unnamed x12, local copies, waits for them, and re-layouts  0.68 us
    pad x1, local copies, waits for them, and re-layouts, body(): jnp.pad(row_taps, ((0, 6), (0, 125)))  0.68 us
    ppermute x1, starting transfers between devices, neighbour_rows(): lax.ppermute(jnp.where(odd, last, first), 'row', pairs_of(peers, 1))  0.66 us
  transfers between devices with their start and end apart: 10, of which 6 were waited for; matrix products, arithmetic and copies ran while one was open for 8% of the time, Pallas kernels for 3%

profile of v4, /device:TPU:0, one launch (start us, length us, event | category | flops | bytes accessed | tf_op | source)
XLA Modules:
  0.0 26.6 jit_solution(10899301041874925285)
XLA Ops:
  0.7 4.1 %collective-permute-start.1 = (bf16[8,2,2,512]{3,2,1,0:T(2,128)(2,1)}, bf16[8,2,2,512]{3,2,1,0:T(2,128)(2,1)S(1)}, u32[]{:S(2)}, u32[]{:S(2)}) collective-permute-start(bf16[8,2,2,512]{3,2,1,0:T(2,128)(2,1)} %param.9), channel_id=1, source_target_pairs={{0,16},{4,20},{8,24},{12,28},{16,0},{20,4},{24,8},{28,12},{1,17},{... | collective-permute-start | bytes 98312 | tf_op jit(solution)/shard_map/ppermute | solution.py:48
  4.8 0.1 collective-permute-start
  4.9 0.1 fusion.4.refs_1_
  5.0 0.8 %copy.10 = bf16[8,2,2,512]{3,0,2,1:T(8,128)(2,1)S(1)} copy(bf16[8,2,2,512]{3,1,2,0:T(2,128)(2,1)} %bitcast.26) | data formatting | bytes 65536 | tf_op jit(solution)/shard_map/transpose | solution.py:220
  5.7 0.7 %pad.4.refs_0_ = f32[8,128]{1,0:T(8,128)S(1)} pad(f32[2,3]{1,0:T(2,128)} %param.11, f32[]{:T(128)} %constant.109.clone.1), padding=0_6x0_125 | pad | bytes 4124 | tf_op jit(solution)/shard_map/jit(_pad)/pad | solution.py:237
  6.4 0.8 %collective-permute-done.1 = bf16[8,2,2,512]{3,2,1,0:T(2,128)(2,1)S(1)} collective-permute-done((bf16[8,2,2,512]{3,2,1,0:T(2,128)(2,1)}, bf16[8,2,2,512]{3,2,1,0:T(2,128)(2,1)S(1)}, u32[]{:S(2)}, u32[]{:S(2)}) %collective-permute-start.1) | collective-permute-done | bytes 32800 | tf_op jit(solution)/shard_map/ppermute | solution.py:48
  7.4 0.7 %collective-permute-start.3 = (bf16[16,1024]{1,0:T(8,128)(2,1)S(1)}, bf16[16,1024]{1,0:T(8,128)(2,1)S(1)}, u32[]{:S(2)}, u32[]{:S(2)}) collective-permute-start(bf16[16,1024]{1,0:T(8,128)(2,1)S(1)} %get-tuple-element.22), channel_id=1, source_target_pairs={{1,2},{2,1},{5,6},{6,5},{9,10},{10,9},{13,14},{14,13},{17,18},{18,... | collective-permute-start | bytes 98312 | tf_op jit(solution)/shard_map/ppermute | solution.py:64
  8.0 1.8 %collective-permute-done = bf16[8,2,2,512]{3,2,1,0:T(2,128)(2,1)S(1)} collective-permute-done((bf16[8,2,2,512]{3,2,1,0:T(2,128)(2,1)}, bf16[8,2,2,512]{3,2,1,0:T(2,128)(2,1)S(1)}, u32[]{:S(2)}, u32[]{:S(2)}) %collective-permute-start) | collective-permute-done | bytes 32800 | tf_op jit(solution)/shard_map/ppermute | solution.py:48
  9.8 0.2 shard_map.95
  10.0 2.6 %collective-permute-start.4 = (bf16[16,4096]{1,0:T(8,128)(2,1)S(1)}, bf16[16,4096]{1,0:T(8,128)(2,1)S(1)}, u32[]{:S(2)}, u32[]{:S(2)}) collective-permute-start(bf16[16,4096]{1,0:T(8,128)(2,1)S(1)} %pad_maximum_fusion.refs_1_.refs_3_.refs_4_), channel_id=1, source_target_pairs={{0,12},{4,8},{8,4},{12,0},{16,28},{20,24},{24,20},{28,16},{1,13},{... | collective-permute-start | bytes 393224 | tf_op jit(solution)/shard_map/ppermute | solution.py:48
  12.6 0.4 %collective-permute-start.5 = (bf16[16,4096]{1,0:T(8,128)(2,1)S(1)}, bf16[16,4096]{1,0:T(8,128)(2,1)S(1)}, u32[]{:S(2)}, u32[]{:S(2)}) collective-permute-start(bf16[16,4096]{1,0:T(8,128)(2,1)S(1)} %pad_maximum_fusion.refs_1_.refs_3_.refs_4_), channel_id=1, source_target_pairs={{0,8},{4,12},{8,0},{12,4},{16,24},{20,28},{24,16},{28,20},{1,9},{5... | collective-permute-start | bytes 393224 | tf_op jit(solution)/shard_map/ppermute | solution.py:48
  13.1 0.5 %collective-permute-start.6 = (bf16[16,4096]{1,0:T(8,128)(2,1)S(1)}, bf16[16,4096]{1,0:T(8,128)(2,1)S(1)}, u32[]{:S(2)}, u32[]{:S(2)}) collective-permute-start(bf16[16,4096]{1,0:T(8,128)(2,1)S(1)} %pad_maximum_fusion.refs_1_.refs_3_.refs_4_), channel_id=1, source_target_pairs={{0,4},{4,0},{8,12},{12,8},{16,20},{20,16},{24,28},{28,24},{1,5},{5... | collective-permute-start | bytes 393224 | tf_op jit(solution)/shard_map/ppermute | solution.py:48
  13.6 0.3 %fusion.27 = (f32[4,2,512]{2,0,1:T(4,128)S(1)}, f32[4,2,512]{2,0,1:T(4,128)S(1)}) fusion(f32[4]{0:T(128)S(1)} %copy-done.4, f32[7,2,512]{2,1,0:T(2,128)S(1)} %copy-done, s32[4]{0:T(128)S(1)} %copy-done.5), kind=kOutput, calls=%fused_computation.71 | convolution fusion | flops 348188 | bytes 61472 | tf_op jit(solution)/shard_map/wp,prc->wrc/dot_general | solution.py:248
  14.0 0.6 %copy-done.3 = s32[80,2]{0,1:T(2,128)S(1)} copy-done((s32[80,2]{0,1:T(2,128)S(1)}, s32[80,2]{0,1:T(2,128)}, u32[]{:S(2)}) %copy-start.3) | copy-done | bytes 664
  14.7 1.3 %collective-permute-done.4.refs_2_.refs_4_.refs_5_ = bf16[16,4096]{1,0:T(8,128)(2,1)S(1)} collective-permute-done((bf16[16,4096]{1,0:T(8,128)(2,1)S(1)}, bf16[16,4096]{1,0:T(8,128)(2,1)S(1)}, u32[]{:S(2)}, u32[]{:S(2)}) %collective-permute-start.4) | collective-permute-done | bytes 131104 | tf_op jit(solution)/shard_map/ppermute | solution.py:48
  16.0 0.3 %shard_map.97 = (bf16[64,1024]{1,0:T(8,128)(2,1)S(1)}, bf16[64,1024]{1,0:T(8,128)(2,1)S(1)}) custom-call(f32[8,1024]{1,0:T(8,128)S(1)} %tile.9.refs_0_, f32[8,1024]{1,0:T(8,128)S(1)} %tile.21.refs_1_, bf16[2,512,512]{2,1,0:T(8,128)(2,1)S(1)} %copy-done.1, bf16[16,4096]{1,0:T(8,128)(2,1)S(1)} %pad_maximum_fusion.refs_1_.refs_3_.refs_4_, ...), custom_call_target="tpu_custom_call" | custom-call | flops 134217728 | bytes 1638400 | tf_op jit(solution)/shard_map/pallas_call | solution.py:32
  16.3 1.8 %collective-permute-done.5.refs_3_.refs_6_ = bf16[16,4096]{1,0:T(8,128)(2,1)S(1)} collective-permute-done((bf16[16,4096]{1,0:T(8,128)(2,1)S(1)}, bf16[16,4096]{1,0:T(8,128)(2,1)S(1)}, u32[]{:S(2)}, u32[]{:S(2)}) %collective-permute-start.5) | collective-permute-done | bytes 131104 | tf_op jit(solution)/shard_map/ppermute | solution.py:48
  18.1 1.7 %collective-permute-done.6.refs_4_.refs_7_ = bf16[16,4096]{1,0:T(8,128)(2,1)S(1)} collective-permute-done((bf16[16,4096]{1,0:T(8,128)(2,1)S(1)}, bf16[16,4096]{1,0:T(8,128)(2,1)S(1)}, u32[]{:S(2)}, u32[]{:S(2)}) %collective-permute-start.6) | collective-permute-done | bytes 131104 | tf_op jit(solution)/shard_map/ppermute | solution.py:48
  19.8 0.7 %shard_map.98 = (bf16[64,1024]{1,0:T(8,128)(2,1)S(1)}, f32[64,128]{1,0:T(8,128)S(1)}) custom-call(f32[8,1024]{1,0:T(8,128)S(1)} %tile.9.refs_0_, f32[8,1024]{1,0:T(8,128)S(1)} %tile.21.refs_1_, bf16[2,512,512]{2,1,0:T(8,128)(2,1)S(1)} %copy-done.1, bf16[64,1024]{1,0:T(8,128)(2,1)S(1)} %get-tuple-element.17.refs_3_, ...), custom_call_target="tpu_custom_call" | custom-call | flops 167772160 | bytes 1933312 | tf_op jit(solution)/shard_map/pallas_call | solution.py:32
  20.6 2.8 %collective-permute-start.8 = (f32[64,128]{1,0:T(8,128)S(1)}, f32[64,128]{1,0:T(8,128)S(1)}, u32[]{:S(2)}, u32[]{:S(2)}) collective-permute-start(f32[64,128]{1,0:T(8,128)S(1)} %get-tuple-element.19.refs_5_), channel_id=1, source_target_pairs={{0,2},{1,3},{2,0},{3,1},{4,6},{5,7},{6,4},{7,5},{8,10},{9,11},{10,... | collective-permute-start | bytes 98312 | tf_op jit(solution)/shard_map/ppermute | solution.py:48
  23.4 0.3 fusion.refs_0_
  23.7 0.5 %shard_map.96.refs_2_ = bf16[128,1024]{1,0:T(8,128)(2,1)S(1)} custom-call(bf16[2,512,512]{2,1,0:T(8,128)(2,1)S(1)} %copy-done.1, bf16[16,4096]{1,0:T(8,128)(2,1)S(1)} %pad_maximum_fusion.refs_1_.refs_3_.refs_4_, bf16[16,4096]{1,0:T(8,128)(2,1)S(1)} %collective-permute-done.4.refs_2_.refs_4_.refs_5_, ...), custom_call_target="tpu_custom_call" | custom-call | flops 268435456 | bytes 1835008 | tf_op jit(solution)/shard_map/pallas_call | solution.py:32
  24.1 1.4 %collective-permute-done.8.refs_7_ = f32[64,128]{1,0:T(8,128)S(1)} collective-permute-done((f32[64,128]{1,0:T(8,128)S(1)}, f32[64,128]{1,0:T(8,128)S(1)}, u32[]{:S(2)}, u32[]{:S(2)}) %collective-permute-start.8) | collective-permute-done | bytes 32800 | tf_op jit(solution)/shard_map/ppermute | solution.py:48
  25.5 1.0 %shard_map.99 = (f32[2,8,64]{2,1,0:T(8,128)}, f32[4,2,512]{2,1,0:T(2,128)}) custom-call(f32[64,64]{1,0:T(8,128)S(1)} %fusion.refs_0_, f32[64,64]{1,0:T(8,128)S(1)} %fusion.4.refs_1_, bf16[128,1024]{1,0:T(8,128)(2,1)S(1)} %shard_map.96.refs_2_, bf16[64,1024]{1,0:T(8,128)(2,1)S(1)} %get-tuple-element.16.refs_3_, ...), custom_call_target="tpu_custom_call" | custom-call | flops 33554432 | bytes 708608 | tf_op jit(solution)/shard_map/pallas_call | solution.py:32
  (32 shorter events, 0.4 us)
Async XLA Ops:
  0.6 13.0 %copy-start = (f32[7,2,512]{2,1,0:T(2,128)S(1)}, f32[7,2,512]{2,1,0:T(2,128)}, u32[]{:S(2)}) copy-start(f32[7,2,512]{2,1,0:T(2,128)} %param.12) | copy-start | bytes 86020
  0.6 4.3 %copy-start.2 = (bf16[8,2,2,512]{3,2,1,0:T(2,128)(2,1)S(1)}, bf16[8,2,2,512]{3,2,1,0:T(2,128)(2,1)}, u32[]{:S(2)}) copy-start(bf16[8,2,2,512]{3,2,1,0:T(2,128)(2,1)} %param.9) | copy-start | bytes 98308
  0.7 15.3 %copy-start.1 = (bf16[2,512,512]{2,1,0:T(8,128)(2,1)S(1)}, bf16[2,512,512]{2,1,0:T(8,128)(2,1)}, u32[]{:S(2)}) copy-start(bf16[2,512,512]{2,1,0:T(8,128)(2,1)} %refs_2_.3) | copy-start | bytes 3145732
  0.7 6.6 %collective-permute-start.1 = (bf16[8,2,2,512]{3,2,1,0:T(2,128)(2,1)}, bf16[8,2,2,512]{3,2,1,0:T(2,128)(2,1)S(1)}, u32[]{:S(2)}, u32[]{:S(2)}) collective-permute-start(bf16[8,2,2,512]{3,2,1,0:T(2,128)(2,1)} %param.9), channel_id=1, source_target_pairs={{0,16},{4,20},{8,24},{12,28},{16,0},{20,4},{24,8},{28,12},{1,17},{... | collective-permute-start | bytes 98312 | tf_op jit(solution)/shard_map/ppermute | solution.py:48
  4.8 5.0 %collective-permute-start = (bf16[8,2,2,512]{3,2,1,0:T(2,128)(2,1)}, bf16[8,2,2,512]{3,2,1,0:T(2,128)(2,1)S(1)}, u32[]{:S(2)}, u32[]{:S(2)}) collective-permute-start(bf16[8,2,2,512]{3,2,1,0:T(2,128)(2,1)} %param.8), channel_id=1, source_target_pairs={{0,16},{4,20},{8,24},{12,28},{16,0},{20,4},{24,8},{28,12},{1,17},{... | collective-permute-start | bytes 98312 | tf_op jit(solution)/shard_map/ppermute | solution.py:48
  7.3 2.5 %collective-permute-start.2 = (bf16[16,1024]{1,0:T(8,128)(2,1)S(1)}, bf16[16,1024]{1,0:T(8,128)(2,1)S(1)}, u32[]{:S(2)}, u32[]{:S(2)}) collective-permute-start(bf16[16,1024]{1,0:T(8,128)(2,1)S(1)} %get-tuple-element.23), channel_id=1, source_target_pairs={{0,1},{2,3},{1,0},{3,2},{4,5},{6,7},{5,4},{7,6},{8,9},{10,11},{9,8... | collective-permute-start | bytes 98312 | tf_op jit(solution)/shard_map/ppermute | solution.py:65
  7.4 2.5 %collective-permute-start.3 = (bf16[16,1024]{1,0:T(8,128)(2,1)S(1)}, bf16[16,1024]{1,0:T(8,128)(2,1)S(1)}, u32[]{:S(2)}, u32[]{:S(2)}) collective-permute-start(bf16[16,1024]{1,0:T(8,128)(2,1)S(1)} %get-tuple-element.22), channel_id=1, source_target_pairs={{1,2},{2,1},{5,6},{6,5},{9,10},{10,9},{13,14},{14,13},{17,18},{18,... | collective-permute-start | bytes 98312 | tf_op jit(solution)/shard_map/ppermute | solution.py:64
  10.0 3.6 %copy-start.4 = (f32[4]{0:T(128)S(1)}, f32[4]{0:T(128)}, u32[]{:S(2)}) copy-start(f32[4]{0:T(128)} %param.14) | copy-start | bytes 52
  10.0 3.6 %copy-start.5 = (s32[4]{0:T(128)S(1)}, s32[4]{0:T(128)}, u32[]{:S(2)}) copy-start(s32[4]{0:T(128)} %param.13) | copy-start | bytes 52
  10.0 5.9 %collective-permute-start.4 = (bf16[16,4096]{1,0:T(8,128)(2,1)S(1)}, bf16[16,4096]{1,0:T(8,128)(2,1)S(1)}, u32[]{:S(2)}, u32[]{:S(2)}) collective-permute-start(bf16[16,4096]{1,0:T(8,128)(2,1)S(1)} %pad_maximum_fusion.refs_1_.refs_3_.refs_4_), channel_id=1, source_target_pairs={{0,12},{4,8},{8,4},{12,0},{16,28},{20,24},{24,20},{28,16},{1,13},{... | collective-permute-start | bytes 393224 | tf_op jit(solution)/shard_map/ppermute | solution.py:48
  12.6 5.5 %collective-permute-start.5 = (bf16[16,4096]{1,0:T(8,128)(2,1)S(1)}, bf16[16,4096]{1,0:T(8,128)(2,1)S(1)}, u32[]{:S(2)}, u32[]{:S(2)}) collective-permute-start(bf16[16,4096]{1,0:T(8,128)(2,1)S(1)} %pad_maximum_fusion.refs_1_.refs_3_.refs_4_), channel_id=1, source_target_pairs={{0,8},{4,12},{8,0},{12,4},{16,24},{20,28},{24,16},{28,20},{1,9},{5... | collective-permute-start | bytes 393224 | tf_op jit(solution)/shard_map/ppermute | solution.py:48
  13.1 6.8 %collective-permute-start.6 = (bf16[16,4096]{1,0:T(8,128)(2,1)S(1)}, bf16[16,4096]{1,0:T(8,128)(2,1)S(1)}, u32[]{:S(2)}, u32[]{:S(2)}) collective-permute-start(bf16[16,4096]{1,0:T(8,128)(2,1)S(1)} %pad_maximum_fusion.refs_1_.refs_3_.refs_4_), channel_id=1, source_target_pairs={{0,4},{4,0},{8,12},{12,8},{16,20},{20,16},{24,28},{28,24},{1,5},{5... | collective-permute-start | bytes 393224 | tf_op jit(solution)/shard_map/ppermute | solution.py:48
  14.0 0.7 %copy-start.3 = (s32[80,2]{0,1:T(2,128)S(1)}, s32[80,2]{0,1:T(2,128)}, u32[]{:S(2)}) copy-start(s32[80,2]{0,1:T(2,128)} %param.15) | copy-start | bytes 1924
  20.5 3.6 %collective-permute-start.7 = (f32[64,128]{1,0:T(8,128)S(1)}, f32[64,128]{1,0:T(8,128)S(1)}, u32[]{:S(2)}, u32[]{:S(2)}) collective-permute-start(f32[64,128]{1,0:T(8,128)S(1)} %get-tuple-element.19.refs_5_), channel_id=1, source_target_pairs={{0,3},{1,2},{2,1},{3,0},{4,7},{5,6},{6,5},{7,4},{8,11},{9,10},{10,... | collective-permute-start | bytes 98312 | tf_op jit(solution)/shard_map/ppermute | solution.py:48
  20.6 4.9 %collective-permute-start.8 = (f32[64,128]{1,0:T(8,128)S(1)}, f32[64,128]{1,0:T(8,128)S(1)}, u32[]{:S(2)}, u32[]{:S(2)}) collective-permute-start(f32[64,128]{1,0:T(8,128)S(1)} %get-tuple-element.19.refs_5_), channel_id=1, source_target_pairs={{0,2},{1,3},{2,0},{3,1},{4,6},{5,7},{6,4},{7,5},{8,10},{9,11},{10,... | collective-permute-start | bytes 98312 | tf_op jit(solution)/shard_map/ppermute | solution.py:48
  23.4 2.2 %collective-permute-start.9 = (f32[64,128]{1,0:T(8,128)S(1)}, f32[64,128]{1,0:T(8,128)S(1)}, u32[]{:S(2)}, u32[]{:S(2)}) collective-permute-start(f32[64,128]{1,0:T(8,128)S(1)} %get-tuple-element.19.refs_5_), channel_id=1, source_target_pairs={{0,1},{1,0},{2,3},{3,2},{4,5},{5,4},{6,7},{7,6},{8,9},{9,8},{10,11... | collective-permute-start | bytes 98312 | tf_op jit(solution)/shard_map/ppermute | solution.py:48

commit v5 on v4

--- a/solution.py
+++ b/solution.py
@@ -185,7 +185,15 @@
         real = summed[:, :total] * scale_pixels * mask
         imag = summed[:, total:] * scale_pixels * mask
         own = jnp.concatenate([real[:local_modes], imag[:local_modes]], axis=0)
-        own = jnp.dot(own, order, precision=lax.Precision.HIGHEST, preferred_element_type=F32)
+        high = own.astype(BF16)
+        rest = own - high.astype(F32)
+        middle = rest.astype(BF16)
+        low = (rest - middle.astype(F32)).astype(BF16)
+        sorted_parts = jnp.dot(
+            jnp.concatenate([high, middle, low], axis=0), order, preferred_element_type=F32
+        )
+        size = own.shape[0]
+        own = sorted_parts[:size] + sorted_parts[size : 2 * size] + sorted_parts[2 * size :]
         coupling = own.reshape(2, local_modes, total)
         weight_real, weight_imag = real.astype(BF16), imag.astype(BF16)
         weights = jnp.concatenate(
@@ -261,7 +269,7 @@
     mask = lax.dot_general(
         to_forward, to_target, (((0,), (0,)), ((), ())), preferred_element_type=F32
     )
-    order = (numbers[:, None] == places[None, :]).astype(F32)
+    order = (numbers[:, None] == places[None, :]).astype(BF16)
 
     early = (len(pieces) + 1) // 2
     late = len(pieces) - early

time: 27 us -> 26.9 us (level)
  no operation moved by 1% of the time
where the time goes in v5:
time: 26.9 us; the launch traced here: 26.5 us
  starting transfers between devices  11.3 us (42%)
  waiting for transfers between devices  8.77 us (33%)
  Pallas kernels  2.62 us (10%)
  local copies, waits for them, and re-layouts  2.22 us (8%)
  between operations  0.86 us (3%)
  matrix products  0.59 us (2%)
    ppermute x8, starting transfers between devices, swapped(): return lax.ppermute(values, axis, [(i, i ^ distance) for i in range(peers)])  10.6 us
    ppermute x8, waiting for transfers between devices, swapped(): return lax.ppermute(values, axis, [(i, i ^ distance) for i in range(peers)])  8.77 us
    pallas_call x5, Pallas kernels, local_call(): pl.pallas_call(kernel, out_shape=tuple(outs), in_specs=[pl.BlockSpec(memo...  2.62 us
    transpose x4, local copies, waits for them, and re-layouts, body(): fields.transpose(0, 2, 1, 3).reshape(fields.shape[0], 2 * half)  0.8 us
    unnamed x12, local copies, waits for them, and re-layouts  0.68 us
    pad x1, local copies, waits for them, and re-layouts, body(): jnp.pad(row_taps, ((0, 6), (0, 125)))  0.68 us
    ppermute x1, starting transfers between devices, neighbour_rows(): lax.ppermute(jnp.where(odd, last, first), 'row', pairs_of(peers, 1))  0.66 us
  transfers between devices with their start and end apart: 10, of which 6 were waited for; matrix products, arithmetic and copies ran while one was open for 8% of the time, Pallas kernels for 3%

profile of v5, /device:TPU:0, one launch (start us, length us, event | category | flops | bytes accessed | tf_op | source)
XLA Modules:
  0.0 26.5 jit_solution(11553087947267900371)
XLA Ops:
  0.7 4.1 %collective-permute-start.1 = (bf16[8,2,2,512]{3,2,1,0:T(2,128)(2,1)}, bf16[8,2,2,512]{3,2,1,0:T(2,128)(2,1)S(1)}, u32[]{:S(2)}, u32[]{:S(2)}) collective-permute-start(bf16[8,2,2,512]{3,2,1,0:T(2,128)(2,1)} %param.9), channel_id=1, source_target_pairs={{0,16},{4,20},{8,24},{12,28},{16,0},{20,4},{24,8},{28,12},{1,17},{... | collective-permute-start | bytes 98312 | tf_op jit(solution)/shard_map/ppermute | solution.py:48
  4.8 0.1 collective-permute-start
  4.9 0.1 fusion.4.refs_1_
  5.0 0.8 %copy.10 = bf16[8,2,2,512]{3,0,2,1:T(8,128)(2,1)S(1)} copy(bf16[8,2,2,512]{3,1,2,0:T(2,128)(2,1)} %bitcast.26) | data formatting | bytes 65536 | tf_op jit(solution)/shard_map/transpose | solution.py:228
  5.7 0.7 %pad.4.refs_0_ = f32[8,128]{1,0:T(8,128)S(1)} pad(f32[2,3]{1,0:T(2,128)} %param.11, f32[]{:T(128)} %constant.109.clone.1), padding=0_6x0_125 | pad | bytes 4124 | tf_op jit(solution)/shard_map/jit(_pad)/pad | solution.py:245
  6.4 0.8 %collective-permute-done.1 = bf16[8,2,2,512]{3,2,1,0:T(2,128)(2,1)S(1)} collective-permute-done((bf16[8,2,2,512]{3,2,1,0:T(2,128)(2,1)}, bf16[8,2,2,512]{3,2,1,0:T(2,128)(2,1)S(1)}, u32[]{:S(2)}, u32[]{:S(2)}) %collective-permute-start.1) | collective-permute-done | bytes 32800 | tf_op jit(solution)/shard_map/ppermute | solution.py:48
  7.4 0.7 %collective-permute-start.3 = (bf16[16,1024]{1,0:T(8,128)(2,1)S(1)}, bf16[16,1024]{1,0:T(8,128)(2,1)S(1)}, u32[]{:S(2)}, u32[]{:S(2)}) collective-permute-start(bf16[16,1024]{1,0:T(8,128)(2,1)S(1)} %get-tuple-element.22), channel_id=1, source_target_pairs={{1,2},{2,1},{5,6},{6,5},{9,10},{10,9},{13,14},{14,13},{17,18},{18,... | collective-permute-start | bytes 98312 | tf_op jit(solution)/shard_map/ppermute | solution.py:64
  8.0 1.8 %collective-permute-done = bf16[8,2,2,512]{3,2,1,0:T(2,128)(2,1)S(1)} collective-permute-done((bf16[8,2,2,512]{3,2,1,0:T(2,128)(2,1)}, bf16[8,2,2,512]{3,2,1,0:T(2,128)(2,1)S(1)}, u32[]{:S(2)}, u32[]{:S(2)}) %collective-permute-start) | collective-permute-done | bytes 32800 | tf_op jit(solution)/shard_map/ppermute | solution.py:48
  9.8 0.2 shard_map.95
  10.0 2.6 %collective-permute-start.4 = (bf16[16,4096]{1,0:T(8,128)(2,1)S(1)}, bf16[16,4096]{1,0:T(8,128)(2,1)S(1)}, u32[]{:S(2)}, u32[]{:S(2)}) collective-permute-start(bf16[16,4096]{1,0:T(8,128)(2,1)S(1)} %pad_maximum_fusion.refs_1_.refs_3_.refs_4_), channel_id=1, source_target_pairs={{0,12},{4,8},{8,4},{12,0},{16,28},{20,24},{24,20},{28,16},{1,13},{... | collective-permute-start | bytes 393224 | tf_op jit(solution)/shard_map/ppermute | solution.py:48
  12.6 0.4 %collective-permute-start.5 = (bf16[16,4096]{1,0:T(8,128)(2,1)S(1)}, bf16[16,4096]{1,0:T(8,128)(2,1)S(1)}, u32[]{:S(2)}, u32[]{:S(2)}) collective-permute-start(bf16[16,4096]{1,0:T(8,128)(2,1)S(1)} %pad_maximum_fusion.refs_1_.refs_3_.refs_4_), channel_id=1, source_target_pairs={{0,8},{4,12},{8,0},{12,4},{16,24},{20,28},{24,16},{28,20},{1,9},{5... | collective-permute-start | bytes 393224 | tf_op jit(solution)/shard_map/ppermute | solution.py:48
  13.1 0.5 %collective-permute-start.6 = (bf16[16,4096]{1,0:T(8,128)(2,1)S(1)}, bf16[16,4096]{1,0:T(8,128)(2,1)S(1)}, u32[]{:S(2)}, u32[]{:S(2)}) collective-permute-start(bf16[16,4096]{1,0:T(8,128)(2,1)S(1)} %pad_maximum_fusion.refs_1_.refs_3_.refs_4_), channel_id=1, source_target_pairs={{0,4},{4,0},{8,12},{12,8},{16,20},{20,16},{24,28},{28,24},{1,5},{5... | collective-permute-start | bytes 393224 | tf_op jit(solution)/shard_map/ppermute | solution.py:48
  13.6 0.3 %fusion.27 = (f32[4,2,512]{2,0,1:T(4,128)S(1)}, f32[4,2,512]{2,0,1:T(4,128)S(1)}) fusion(f32[4]{0:T(128)S(1)} %copy-done.4, f32[7,2,512]{2,1,0:T(2,128)S(1)} %copy-done, s32[4]{0:T(128)S(1)} %copy-done.5), kind=kOutput, calls=%fused_computation.71 | convolution fusion | flops 348188 | bytes 61472 | tf_op jit(solution)/shard_map/wp,prc->wrc/dot_general | solution.py:256
  14.0 0.6 %copy-done.3 = s32[80,2]{0,1:T(2,128)S(1)} copy-done((s32[80,2]{0,1:T(2,128)S(1)}, s32[80,2]{0,1:T(2,128)}, u32[]{:S(2)}) %copy-start.3) | copy-done | bytes 664
  14.7 1.3 %collective-permute-done.4.refs_2_.refs_4_.refs_5_ = bf16[16,4096]{1,0:T(8,128)(2,1)S(1)} collective-permute-done((bf16[16,4096]{1,0:T(8,128)(2,1)S(1)}, bf16[16,4096]{1,0:T(8,128)(2,1)S(1)}, u32[]{:S(2)}, u32[]{:S(2)}) %collective-permute-start.4) | collective-permute-done | bytes 131104 | tf_op jit(solution)/shard_map/ppermute | solution.py:48
  16.0 0.3 %shard_map.97 = (bf16[64,1024]{1,0:T(8,128)(2,1)S(1)}, bf16[64,1024]{1,0:T(8,128)(2,1)S(1)}) custom-call(f32[8,1024]{1,0:T(8,128)S(1)} %tile.9.refs_0_, f32[8,1024]{1,0:T(8,128)S(1)} %tile.21.refs_1_, bf16[2,512,512]{2,1,0:T(8,128)(2,1)S(1)} %copy-done.1, bf16[16,4096]{1,0:T(8,128)(2,1)S(1)} %pad_maximum_fusion.refs_1_.refs_3_.refs_4_, ...), custom_call_target="tpu_custom_call" | custom-call | flops 134217728 | bytes 1638400 | tf_op jit(solution)/shard_map/pallas_call | solution.py:32
  16.3 1.8 %collective-permute-done.5.refs_3_.refs_6_ = bf16[16,4096]{1,0:T(8,128)(2,1)S(1)} collective-permute-done((bf16[16,4096]{1,0:T(8,128)(2,1)S(1)}, bf16[16,4096]{1,0:T(8,128)(2,1)S(1)}, u32[]{:S(2)}, u32[]{:S(2)}) %collective-permute-start.5) | collective-permute-done | bytes 131104 | tf_op jit(solution)/shard_map/ppermute | solution.py:48
  18.1 1.7 %collective-permute-done.6.refs_4_.refs_7_ = bf16[16,4096]{1,0:T(8,128)(2,1)S(1)} collective-permute-done((bf16[16,4096]{1,0:T(8,128)(2,1)S(1)}, bf16[16,4096]{1,0:T(8,128)(2,1)S(1)}, u32[]{:S(2)}, u32[]{:S(2)}) %collective-permute-start.6) | collective-permute-done | bytes 131104 | tf_op jit(solution)/shard_map/ppermute | solution.py:48
  19.8 0.7 %shard_map.98 = (bf16[64,1024]{1,0:T(8,128)(2,1)S(1)}, f32[64,128]{1,0:T(8,128)S(1)}) custom-call(f32[8,1024]{1,0:T(8,128)S(1)} %tile.9.refs_0_, f32[8,1024]{1,0:T(8,128)S(1)} %tile.21.refs_1_, bf16[2,512,512]{2,1,0:T(8,128)(2,1)S(1)} %copy-done.1, bf16[64,1024]{1,0:T(8,128)(2,1)S(1)} %get-tuple-element.17.refs_3_, ...), custom_call_target="tpu_custom_call" | custom-call | flops 167772160 | bytes 1933312 | tf_op jit(solution)/shard_map/pallas_call | solution.py:32
  20.6 2.8 %collective-permute-start.8 = (f32[64,128]{1,0:T(8,128)S(1)}, f32[64,128]{1,0:T(8,128)S(1)}, u32[]{:S(2)}, u32[]{:S(2)}) collective-permute-start(f32[64,128]{1,0:T(8,128)S(1)} %get-tuple-element.19.refs_5_), channel_id=1, source_target_pairs={{0,2},{1,3},{2,0},{3,1},{4,6},{5,7},{6,4},{7,5},{8,10},{9,11},{10,... | collective-permute-start | bytes 98312 | tf_op jit(solution)/shard_map/ppermute | solution.py:48
  23.4 0.3 fusion.refs_0_
  23.7 0.5 %shard_map.96.refs_2_ = bf16[128,1024]{1,0:T(8,128)(2,1)S(1)} custom-call(bf16[2,512,512]{2,1,0:T(8,128)(2,1)S(1)} %copy-done.1, bf16[16,4096]{1,0:T(8,128)(2,1)S(1)} %pad_maximum_fusion.refs_1_.refs_3_.refs_4_, bf16[16,4096]{1,0:T(8,128)(2,1)S(1)} %collective-permute-done.4.refs_2_.refs_4_.refs_5_, ...), custom_call_target="tpu_custom_call" | custom-call | flops 268435456 | bytes 1835008 | tf_op jit(solution)/shard_map/pallas_call | solution.py:32
  24.1 1.4 %collective-permute-done.8.refs_7_ = f32[64,128]{1,0:T(8,128)S(1)} collective-permute-done((f32[64,128]{1,0:T(8,128)S(1)}, f32[64,128]{1,0:T(8,128)S(1)}, u32[]{:S(2)}, u32[]{:S(2)}) %collective-permute-start.8) | collective-permute-done | bytes 32800 | tf_op jit(solution)/shard_map/ppermute | solution.py:48
  25.5 1.0 %shard_map.99 = (f32[2,8,64]{2,1,0:T(8,128)}, f32[4,2,512]{2,1,0:T(2,128)}) custom-call(f32[64,64]{1,0:T(8,128)S(1)} %fusion.refs_0_, bf16[64,64]{1,0:T(8,128)(2,1)S(1)} %fusion.4.refs_1_, bf16[128,1024]{1,0:T(8,128)(2,1)S(1)} %shard_map.96.refs_2_, bf16[64,1024]{1,0:T(8,128)(2,1)S(1)} %get-tuple-element.16.refs_3_, ...), custom_call_target="tpu_custom_call" | custom-call | flops 33554432 | bytes 700416 | tf_op jit(solution)/shard_map/pallas_call | solution.py:32
  (32 shorter events, 0.4 us)
Async XLA Ops:
  0.6 13.0 %copy-start = (f32[7,2,512]{2,1,0:T(2,128)S(1)}, f32[7,2,512]{2,1,0:T(2,128)}, u32[]{:S(2)}) copy-start(f32[7,2,512]{2,1,0:T(2,128)} %param.12) | copy-start | bytes 86020
  0.6 4.3 %copy-start.2 = (bf16[8,2,2,512]{3,2,1,0:T(2,128)(2,1)S(1)}, bf16[8,2,2,512]{3,2,1,0:T(2,128)(2,1)}, u32[]{:S(2)}) copy-start(bf16[8,2,2,512]{3,2,1,0:T(2,128)(2,1)} %param.9) | copy-start | bytes 98308
  0.7 15.3 %copy-start.1 = (bf16[2,512,512]{2,1,0:T(8,128)(2,1)S(1)}, bf16[2,512,512]{2,1,0:T(8,128)(2,1)}, u32[]{:S(2)}) copy-start(bf16[2,512,512]{2,1,0:T(8,128)(2,1)} %refs_2_.3) | copy-start | bytes 3145732
  0.7 6.6 %collective-permute-start.1 = (bf16[8,2,2,512]{3,2,1,0:T(2,128)(2,1)}, bf16[8,2,2,512]{3,2,1,0:T(2,128)(2,1)S(1)}, u32[]{:S(2)}, u32[]{:S(2)}) collective-permute-start(bf16[8,2,2,512]{3,2,1,0:T(2,128)(2,1)} %param.9), channel_id=1, source_target_pairs={{0,16},{4,20},{8,24},{12,28},{16,0},{20,4},{24,8},{28,12},{1,17},{... | collective-permute-start | bytes 98312 | tf_op jit(solution)/shard_map/ppermute | solution.py:48
  4.8 5.0 %collective-permute-start = (bf16[8,2,2,512]{3,2,1,0:T(2,128)(2,1)}, bf16[8,2,2,512]{3,2,1,0:T(2,128)(2,1)S(1)}, u32[]{:S(2)}, u32[]{:S(2)}) collective-permute-start(bf16[8,2,2,512]{3,2,1,0:T(2,128)(2,1)} %param.8), channel_id=1, source_target_pairs={{0,16},{4,20},{8,24},{12,28},{16,0},{20,4},{24,8},{28,12},{1,17},{... | collective-permute-start | bytes 98312 | tf_op jit(solution)/shard_map/ppermute | solution.py:48
  7.3 2.5 %collective-permute-start.2 = (bf16[16,1024]{1,0:T(8,128)(2,1)S(1)}, bf16[16,1024]{1,0:T(8,128)(2,1)S(1)}, u32[]{:S(2)}, u32[]{:S(2)}) collective-permute-start(bf16[16,1024]{1,0:T(8,128)(2,1)S(1)} %get-tuple-element.23), channel_id=1, source_target_pairs={{0,1},{2,3},{1,0},{3,2},{4,5},{6,7},{5,4},{7,6},{8,9},{10,11},{9,8... | collective-permute-start | bytes 98312 | tf_op jit(solution)/shard_map/ppermute | solution.py:65
  7.4 2.5 %collective-permute-start.3 = (bf16[16,1024]{1,0:T(8,128)(2,1)S(1)}, bf16[16,1024]{1,0:T(8,128)(2,1)S(1)}, u32[]{:S(2)}, u32[]{:S(2)}) collective-permute-start(bf16[16,1024]{1,0:T(8,128)(2,1)S(1)} %get-tuple-element.22), channel_id=1, source_target_pairs={{1,2},{2,1},{5,6},{6,5},{9,10},{10,9},{13,14},{14,13},{17,18},{18,... | collective-permute-start | bytes 98312 | tf_op jit(solution)/shard_map/ppermute | solution.py:64
  10.0 3.6 %copy-start.4 = (f32[4]{0:T(128)S(1)}, f32[4]{0:T(128)}, u32[]{:S(2)}) copy-start(f32[4]{0:T(128)} %param.14) | copy-start | bytes 52
  10.0 3.6 %copy-start.5 = (s32[4]{0:T(128)S(1)}, s32[4]{0:T(128)}, u32[]{:S(2)}) copy-start(s32[4]{0:T(128)} %param.13) | copy-start | bytes 52
  10.0 5.9 %collective-permute-start.4 = (bf16[16,4096]{1,0:T(8,128)(2,1)S(1)}, bf16[16,4096]{1,0:T(8,128)(2,1)S(1)}, u32[]{:S(2)}, u32[]{:S(2)}) collective-permute-start(bf16[16,4096]{1,0:T(8,128)(2,1)S(1)} %pad_maximum_fusion.refs_1_.refs_3_.refs_4_), channel_id=1, source_target_pairs={{0,12},{4,8},{8,4},{12,0},{16,28},{20,24},{24,20},{28,16},{1,13},{... | collective-permute-start | bytes 393224 | tf_op jit(solution)/shard_map/ppermute | solution.py:48
  12.6 5.5 %collective-permute-start.5 = (bf16[16,4096]{1,0:T(8,128)(2,1)S(1)}, bf16[16,4096]{1,0:T(8,128)(2,1)S(1)}, u32[]{:S(2)}, u32[]{:S(2)}) collective-permute-start(bf16[16,4096]{1,0:T(8,128)(2,1)S(1)} %pad_maximum_fusion.refs_1_.refs_3_.refs_4_), channel_id=1, source_target_pairs={{0,8},{4,12},{8,0},{12,4},{16,24},{20,28},{24,16},{28,20},{1,9},{5... | collective-permute-start | bytes 393224 | tf_op jit(solution)/shard_map/ppermute | solution.py:48
  13.1 6.8 %collective-permute-start.6 = (bf16[16,4096]{1,0:T(8,128)(2,1)S(1)}, bf16[16,4096]{1,0:T(8,128)(2,1)S(1)}, u32[]{:S(2)}, u32[]{:S(2)}) collective-permute-start(bf16[16,4096]{1,0:T(8,128)(2,1)S(1)} %pad_maximum_fusion.refs_1_.refs_3_.refs_4_), channel_id=1, source_target_pairs={{0,4},{4,0},{8,12},{12,8},{16,20},{20,16},{24,28},{28,24},{1,5},{5... | collective-permute-start | bytes 393224 | tf_op jit(solution)/shard_map/ppermute | solution.py:48
  14.0 0.7 %copy-start.3 = (s32[80,2]{0,1:T(2,128)S(1)}, s32[80,2]{0,1:T(2,128)}, u32[]{:S(2)}) copy-start(s32[80,2]{0,1:T(2,128)} %param.15) | copy-start | bytes 1924
  20.5 3.6 %collective-permute-start.7 = (f32[64,128]{1,0:T(8,128)S(1)}, f32[64,128]{1,0:T(8,128)S(1)}, u32[]{:S(2)}, u32[]{:S(2)}) collective-permute-start(f32[64,128]{1,0:T(8,128)S(1)} %get-tuple-element.19.refs_5_), channel_id=1, source_target_pairs={{0,3},{1,2},{2,1},{3,0},{4,7},{5,6},{6,5},{7,4},{8,11},{9,10},{10,... | collective-permute-start | bytes 98312 | tf_op jit(solution)/shard_map/ppermute | solution.py:48
  20.6 4.9 %collective-permute-start.8 = (f32[64,128]{1,0:T(8,128)S(1)}, f32[64,128]{1,0:T(8,128)S(1)}, u32[]{:S(2)}, u32[]{:S(2)}) collective-permute-start(f32[64,128]{1,0:T(8,128)S(1)} %get-tuple-element.19.refs_5_), channel_id=1, source_target_pairs={{0,2},{1,3},{2,0},{3,1},{4,6},{5,7},{6,4},{7,5},{8,10},{9,11},{10,... | collective-permute-start | bytes 98312 | tf_op jit(solution)/shard_map/ppermute | solution.py:48
  23.4 2.2 %collective-permute-start.9 = (f32[64,128]{1,0:T(8,128)S(1)}, f32[64,128]{1,0:T(8,128)S(1)}, u32[]{:S(2)}, u32[]{:S(2)}) collective-permute-start(f32[64,128]{1,0:T(8,128)S(1)} %get-tuple-element.19.refs_5_), channel_id=1, source_target_pairs={{0,1},{1,0},{2,3},{3,2},{4,5},{5,4},{6,7},{7,6},{8,9},{9,8},{10,11... | collective-permute-start | bytes 98312 | tf_op jit(solution)/shard_map/ppermute | solution.py:48

commit v6 on v5

--- a/solution.py
+++ b/solution.py
@@ -63,7 +63,7 @@
     first, last = row_at(0), row_at(half - width)
     over_odd = lax.ppermute(jnp.where(odd, last, first), "row", pairs_of(peers, 1))
     over_even = lax.ppermute(jnp.where(odd, first, last), "row", pairs_of(peers, 0))
-    return jnp.where(odd, over_even, over_odd), jnp.where(odd, over_odd, over_even)
+    return over_even, over_odd
 
 
 def rounds_of(peers):
@@ -78,8 +78,11 @@
 
 
 def pulled_rows(rows, width):
-    def fn(taps, own, before, after):
+    def fn(taps, fields, own, over_even, over_odd):
         half = rows * width
+        odd = jnp.broadcast_to(taps[2:3, 0:1], over_even.shape) > 0.5
+        before = jnp.where(odd, over_even.astype(F32), over_odd.astype(F32))
+        after = jnp.where(odd, over_odd.astype(F32), over_even.astype(F32))
         real = [before[:, :width]] + [own[:, j * width : (j + 1) * width] for j in range(rows)]
         imag = [before[:, width:]] + [
             own[:, half + j * width : half + (j + 1) * width] for j in range(rows)
@@ -96,7 +99,8 @@
                 total_imag = total_imag + a * imag[sources[k]] - b * real[sources[k]]
             out_real.append(total_real)
             out_imag.append(total_imag)
-        return (jnp.concatenate(out_real + out_imag, axis=1).astype(BF16),)
+        pulled = jnp.concatenate(out_real + out_imag, axis=1).astype(BF16)
+        return (jnp.concatenate([fields, pulled], axis=1),)
 
     return fn
 
@@ -238,14 +242,15 @@
         targets, fields = [jnp.concatenate(both, axis=0) for both in zip(near, far)]
     if targets.ndim > 2:
         targets, fields = flat(targets), flat(fields)
-    before, after = neighbour_rows(targets, width)
-    (pulled,) = local_call(
+    over_even, over_odd = neighbour_rows(targets, width)
+    odd = (lax.axis_index("row") % 2).astype(F32)
+    taps = jnp.concatenate([row_taps, jnp.full((1, row_taps.shape[1]), odd)], axis=0)
+    (both,) = local_call(
         pulled_rows(rows, width),
-        [array(targets.shape, BF16)],
-        [jnp.pad(row_taps, ((0, 6), (0, 125))), targets, before, after],
+        [array((targets.shape[0], 4 * half), BF16)],
+        [jnp.pad(taps, ((0, 5), (0, 125))), fields, targets, over_even, over_odd],
         flops=24 * targets.shape[0] * half,
     )
-    both = jnp.concatenate([fields, pulled], axis=1)
     both, pair_list, plane_index, wave_ratio, phase_masks = lax.optimization_barrier(
         (both, pair_list, plane_index, wave_ratio, phase_masks)
     )
@@ -271,7 +276,7 @@
     )
     order = (numbers[:, None] == places[None, :]).astype(BF16)
 
-    early = (len(pieces) + 1) // 2
+    early = len(pieces) - 1
     late = len(pieces) - early
     early_total, late_total = early * both.shape[0], late * both.shape[0]
     early_masked, early_spread = local_call(

time: 26.9 us -> 26.9 us (level)
  local copies, waits for them, and re-layouts: 2.22 us -> 0.89 us
  other arithmetic: 0.14 us -> 0.82 us
  waiting for transfers between devices: 8.77 us -> 9.37 us
    pad x0 -> x1, other arithmetic: none -> 0.69 us  [body(): jnp.pad(taps, ((0, 5), (0, 125)))]
    pad x1 -> x0, local copies, waits for them, and re-layouts: 0.68 us -> none  [body(): jnp.pad(row_taps, ((0, 6), (0, 125)))]
    unnamed x12, local copies, waits for them, and re-layouts: 0.68 us -> 0.04 us
    ppermute x8, waiting for transfers between devices: 8.77 us -> 9.36 us  [swapped(): return lax.ppermute(values, axis, [(i, i ^ distance) for i in range(peers)])]
  transfers between devices with their start and end apart: 10 -> 10, of which waited for: 6 -> 6; matrix products, arithmetic and copies ran while one was open for 8% -> 9% of each run, Pallas kernels for 3% -> 3%
where the time goes in v6:
time: 26.9 us; the launch traced here: 26.5 us
  starting transfers between devices  11.3 us (42%)
  waiting for transfers between devices  9.37 us (35%)
  Pallas kernels  2.7 us (10%)
  local copies, waits for them, and re-layouts  0.89 us (3%)
  between operations  0.85 us (3%)
  other arithmetic  0.82 us (3%)
  matrix products  0.59 us (2%)
    ppermute x8, starting transfers between devices, swapped(): return lax.ppermute(values, axis, [(i, i ^ distance) for i in range(peers)])  10.6 us
    ppermute x8, waiting for transfers between devices, swapped(): return lax.ppermute(values, axis, [(i, i ^ distance) for i in range(peers)])  9.36 us
    pallas_call x5, Pallas kernels, local_call(): pl.pallas_call(kernel, out_shape=tuple(outs), in_specs=[pl.BlockSpec(memo...  2.7 us
    transpose x4, local copies, waits for them, and re-layouts, body(): fields.transpose(0, 2, 1, 3).reshape(fields.shape[0], 2 * half)  0.8 us
    pad x1, other arithmetic, body(): jnp.pad(taps, ((0, 5), (0, 125)))  0.69 us
    ppermute x1, starting transfers between devices, neighbour_rows(): lax.ppermute(jnp.where(odd, last, first), 'row', pairs_of(peers, 1))  0.66 us
  transfers between devices with their start and end apart: 10, of which 6 were waited for; matrix products, arithmetic and copies ran while one was open for 9% of the time, Pallas kernels for 3%

profile of v6, /device:TPU:0, one launch (start us, length us, event | category | flops | bytes accessed | tf_op | source)
XLA Modules:
  0.0 26.5 jit_solution(611969957571705860)
XLA Ops:
  0.7 4.1 %collective-permute-start.1 = (bf16[8,2,2,512]{3,2,1,0:T(2,128)(2,1)}, bf16[8,2,2,512]{3,2,1,0:T(2,128)(2,1)S(1)}, u32[]{:S(2)}, u32[]{:S(2)}) collective-permute-start(bf16[8,2,2,512]{3,2,1,0:T(2,128)(2,1)} %param.9), channel_id=1, source_target_pairs={{0,16},{4,20},{8,24},{12,28},{16,0},{20,4},{24,8},{28,12},{1,17},{... | collective-permute-start | bytes 98312 | tf_op jit(solution)/shard_map/ppermute | solution.py:48
  4.8 0.1 collective-permute-start
  4.9 0.1 fusion.8.refs_1_
  4.9 0.7 %select_select_fusion.refs_0_ = f32[8,128]{1,0:T(8,128)S(1)} fusion(f32[2,3]{1,0:T(2,128)} %param.11, f32[]{:T(128)S(6)} %convert_element_type.6), kind=kLoop, calls=%fused_computation.30 | loop fusion | flops 5120 | bytes 4124 | tf_op jit(solution)/shard_map/jit(_pad)/pad | solution.py:251
  5.6 0.8 %copy.10 = bf16[8,2,2,512]{3,0,2,1:T(8,128)(2,1)S(1)} copy(bf16[8,2,2,512]{3,1,2,0:T(2,128)(2,1)} %bitcast.26) | data formatting | bytes 65536 | tf_op jit(solution)/shard_map/transpose | solution.py:232
  6.4 0.8 %collective-permute-done.1 = bf16[8,2,2,512]{3,2,1,0:T(2,128)(2,1)S(1)} collective-permute-done((bf16[8,2,2,512]{3,2,1,0:T(2,128)(2,1)}, bf16[8,2,2,512]{3,2,1,0:T(2,128)(2,1)S(1)}, u32[]{:S(2)}, u32[]{:S(2)}) %collective-permute-start.1) | collective-permute-done | bytes 32800 | tf_op jit(solution)/shard_map/ppermute | solution.py:48
  7.3 0.1 collective-permute-start.2
  7.4 0.7 %collective-permute-start.3 = (bf16[16,1024]{1,0:T(8,128)(2,1)S(1)}, bf16[16,1024]{1,0:T(8,128)(2,1)S(1)}, u32[]{:S(2)}, u32[]{:S(2)}) collective-permute-start(bf16[16,1024]{1,0:T(8,128)(2,1)S(1)} %get-tuple-element.20), channel_id=1, source_target_pairs={{1,2},{2,1},{5,6},{6,5},{9,10},{10,9},{13,14},{14,13},{17,18},{18,... | collective-permute-start | bytes 98312 | tf_op jit(solution)/shard_map/ppermute | solution.py:64
  8.0 1.8 %collective-permute-done = bf16[8,2,2,512]{3,2,1,0:T(2,128)(2,1)S(1)} collective-permute-done((bf16[8,2,2,512]{3,2,1,0:T(2,128)(2,1)}, bf16[8,2,2,512]{3,2,1,0:T(2,128)(2,1)S(1)}, u32[]{:S(2)}, u32[]{:S(2)}) %collective-permute-start) | collective-permute-done | bytes 32800 | tf_op jit(solution)/shard_map/ppermute | solution.py:48
  9.9 0.1 shard_map.95.refs_1_.refs_3_.refs_4_
  10.0 2.6 %collective-permute-start.4 = (bf16[16,4096]{1,0:T(8,128)(2,1)S(1)}, bf16[16,4096]{1,0:T(8,128)(2,1)S(1)}, u32[]{:S(2)}, u32[]{:S(2)}) collective-permute-start(bf16[16,4096]{1,0:T(8,128)(2,1)S(1)} %shard_map.95.refs_1_.refs_3_.refs_4_), channel_id=1, source_target_pairs={{0,12},{4,8},{8,4},{12,0},{16,28},{20,24},{24,20},{28,16},{1,13},{... | collective-permute-start | bytes 393224 | tf_op jit(solution)/shard_map/ppermute | solution.py:48
  12.6 0.4 %collective-permute-start.5 = (bf16[16,4096]{1,0:T(8,128)(2,1)S(1)}, bf16[16,4096]{1,0:T(8,128)(2,1)S(1)}, u32[]{:S(2)}, u32[]{:S(2)}) collective-permute-start(bf16[16,4096]{1,0:T(8,128)(2,1)S(1)} %shard_map.95.refs_1_.refs_3_.refs_4_), channel_id=1, source_target_pairs={{0,8},{4,12},{8,0},{12,4},{16,24},{20,28},{24,16},{28,20},{1,9},{5... | collective-permute-start | bytes 393224 | tf_op jit(solution)/shard_map/ppermute | solution.py:48
  13.1 0.5 %collective-permute-start.6 = (bf16[16,4096]{1,0:T(8,128)(2,1)S(1)}, bf16[16,4096]{1,0:T(8,128)(2,1)S(1)}, u32[]{:S(2)}, u32[]{:S(2)}) collective-permute-start(bf16[16,4096]{1,0:T(8,128)(2,1)S(1)} %shard_map.95.refs_1_.refs_3_.refs_4_), channel_id=1, source_target_pairs={{0,4},{4,0},{8,12},{12,8},{16,20},{20,16},{24,28},{28,24},{1,5},{5... | collective-permute-start | bytes 393224 | tf_op jit(solution)/shard_map/ppermute | solution.py:48
  13.6 0.3 %fusion.32 = (f32[4,2,512]{2,0,1:T(4,128)S(1)}, f32[4,2,512]{2,0,1:T(4,128)S(1)}) fusion(f32[4]{0:T(128)S(1)} %copy-done.4, f32[7,2,512]{2,1,0:T(2,128)S(1)} %copy-done, s32[4]{0:T(128)S(1)} %copy-done.5), kind=kOutput, calls=%fused_computation.74 | convolution fusion | flops 348188 | bytes 61472 | tf_op jit(solution)/shard_map/wp,prc->wrc/dot_general | solution.py:261
  14.0 1.9 %collective-permute-done.4.refs_2_.refs_4_.refs_5_ = bf16[16,4096]{1,0:T(8,128)(2,1)S(1)} collective-permute-done((bf16[16,4096]{1,0:T(8,128)(2,1)S(1)}, bf16[16,4096]{1,0:T(8,128)(2,1)S(1)}, u32[]{:S(2)}, u32[]{:S(2)}) %collective-permute-start.4) | collective-permute-done | bytes 131104 | tf_op jit(solution)/shard_map/ppermute | solution.py:48
  16.0 2.2 %collective-permute-done.5.refs_3_.refs_5_.refs_6_ = bf16[16,4096]{1,0:T(8,128)(2,1)S(1)} collective-permute-done((bf16[16,4096]{1,0:T(8,128)(2,1)S(1)}, bf16[16,4096]{1,0:T(8,128)(2,1)S(1)}, u32[]{:S(2)}, u32[]{:S(2)}) %collective-permute-start.5) | collective-permute-done | bytes 131104 | tf_op jit(solution)/shard_map/ppermute | solution.py:48
  18.1 0.4 %shard_map.97 = (bf16[96,1024]{1,0:T(8,128)(2,1)S(1)}, bf16[96,1024]{1,0:T(8,128)(2,1)S(1)}) custom-call(f32[8,1024]{1,0:T(8,128)S(1)} %tile.9.refs_0_, f32[8,1024]{1,0:T(8,128)S(1)} %tile.21.refs_1_, bf16[2,512,512]{2,1,0:T(8,128)(2,1)S(1)} %copy-done.1, bf16[16,4096]{1,0:T(8,128)(2,1)S(1)} %shard_map.95.refs_1_.refs_3_.refs_4_, ...), custom_call_target="tpu_custom_call" | custom-call | flops 201326592 | bytes 1900544 | tf_op jit(solution)/shard_map/pallas_call | solution.py:32
  18.5 1.3 %collective-permute-done.6.refs_4_.refs_7_ = bf16[16,4096]{1,0:T(8,128)(2,1)S(1)} collective-permute-done((bf16[16,4096]{1,0:T(8,128)(2,1)S(1)}, bf16[16,4096]{1,0:T(8,128)(2,1)S(1)}, u32[]{:S(2)}, u32[]{:S(2)}) %collective-permute-start.6) | collective-permute-done | bytes 131104 | tf_op jit(solution)/shard_map/ppermute | solution.py:48
  19.8 0.7 %shard_map.98 = (bf16[32,1024]{1,0:T(8,128)(2,1)S(1)}, f32[64,128]{1,0:T(8,128)S(1)}) custom-call(f32[8,1024]{1,0:T(8,128)S(1)} %tile.9.refs_0_, f32[8,1024]{1,0:T(8,128)S(1)} %tile.21.refs_1_, bf16[2,512,512]{2,1,0:T(8,128)(2,1)S(1)} %copy-done.1, bf16[96,1024]{1,0:T(8,128)(2,1)S(1)} %get-tuple-element.17.refs_3_, ...), custom_call_target="tpu_custom_call" | custom-call | flops 100663296 | bytes 1933312 | tf_op jit(solution)/shard_map/pallas_call | solution.py:32
  20.6 2.7 %collective-permute-start.8 = (f32[64,128]{1,0:T(8,128)S(1)}, f32[64,128]{1,0:T(8,128)S(1)}, u32[]{:S(2)}, u32[]{:S(2)}) collective-permute-start(f32[64,128]{1,0:T(8,128)S(1)} %get-tuple-element.19.refs_5_), channel_id=1, source_target_pairs={{0,2},{1,3},{2,0},{3,1},{4,6},{5,7},{6,4},{7,5},{8,10},{9,11},{10,... | collective-permute-start | bytes 98312 | tf_op jit(solution)/shard_map/ppermute | solution.py:48
  23.3 0.3 fusion.refs_0_
  23.6 0.5 %shard_map.96.refs_2_ = bf16[128,1024]{1,0:T(8,128)(2,1)S(1)} custom-call(bf16[2,512,512]{2,1,0:T(8,128)(2,1)S(1)} %copy-done.1, bf16[16,4096]{1,0:T(8,128)(2,1)S(1)} %shard_map.95.refs_1_.refs_3_.refs_4_, bf16[16,4096]{1,0:T(8,128)(2,1)S(1)} %collective-permute-done.4.refs_2_.refs_4_.refs_5_, ...), custom_call_target="tpu_custom_call" | custom-call | flops 268435456 | bytes 1835008 | tf_op jit(solution)/shard_map/pallas_call | solution.py:32
  24.1 1.4 %collective-permute-done.8.refs_7_ = f32[64,128]{1,0:T(8,128)S(1)} collective-permute-done((f32[64,128]{1,0:T(8,128)S(1)}, f32[64,128]{1,0:T(8,128)S(1)}, u32[]{:S(2)}, u32[]{:S(2)}) %collective-permute-start.8) | collective-permute-done | bytes 32800 | tf_op jit(solution)/shard_map/ppermute | solution.py:48
  25.5 1.0 %shard_map.99 = (f32[2,8,64]{2,1,0:T(8,128)}, f32[4,2,512]{2,1,0:T(2,128)}) custom-call(f32[64,64]{1,0:T(8,128)S(1)} %fusion.refs_0_, bf16[64,64]{1,0:T(8,128)(2,1)S(1)} %fusion.8.refs_1_, bf16[128,1024]{1,0:T(8,128)(2,1)S(1)} %shard_map.96.refs_2_, bf16[96,1024]{1,0:T(8,128)(2,1)S(1)} %get-tuple-element.16.refs_3_, ...), custom_call_target="tpu_custom_call" | custom-call | flops 33554432 | bytes 700416 | tf_op jit(solution)/shard_map/pallas_call | solution.py:32
  (30 shorter events, 0.3 us)
Async XLA Ops:
  0.6 13.0 %copy-start = (f32[7,2,512]{2,1,0:T(2,128)S(1)}, f32[7,2,512]{2,1,0:T(2,128)}, u32[]{:S(2)}) copy-start(f32[7,2,512]{2,1,0:T(2,128)} %param.12) | copy-start | bytes 86020
  0.6 5.0 %copy-start.2 = (bf16[8,2,2,512]{3,2,1,0:T(2,128)(2,1)S(1)}, bf16[8,2,2,512]{3,2,1,0:T(2,128)(2,1)}, u32[]{:S(2)}) copy-start(bf16[8,2,2,512]{3,2,1,0:T(2,128)(2,1)} %param.9) | copy-start | bytes 98308
  0.7 17.5 %copy-start.1 = (bf16[2,512,512]{2,1,0:T(8,128)(2,1)S(1)}, bf16[2,512,512]{2,1,0:T(8,128)(2,1)}, u32[]{:S(2)}) copy-start(bf16[2,512,512]{2,1,0:T(8,128)(2,1)} %refs_2_.3) | copy-start | bytes 3145732
  0.7 6.6 %collective-permute-start.1 = (bf16[8,2,2,512]{3,2,1,0:T(2,128)(2,1)}, bf16[8,2,2,512]{3,2,1,0:T(2,128)(2,1)S(1)}, u32[]{:S(2)}, u32[]{:S(2)}) collective-permute-start(bf16[8,2,2,512]{3,2,1,0:T(2,128)(2,1)} %param.9), channel_id=1, source_target_pairs={{0,16},{4,20},{8,24},{12,28},{16,0},{20,4},{24,8},{28,12},{1,17},{... | collective-permute-start | bytes 98312 | tf_op jit(solution)/shard_map/ppermute | solution.py:48
  4.8 5.0 %collective-permute-start = (bf16[8,2,2,512]{3,2,1,0:T(2,128)(2,1)}, bf16[8,2,2,512]{3,2,1,0:T(2,128)(2,1)S(1)}, u32[]{:S(2)}, u32[]{:S(2)}) collective-permute-start(bf16[8,2,2,512]{3,2,1,0:T(2,128)(2,1)} %param.8), channel_id=1, source_target_pairs={{0,16},{4,20},{8,24},{12,28},{16,0},{20,4},{24,8},{28,12},{1,17},{... | collective-permute-start | bytes 98312 | tf_op jit(solution)/shard_map/ppermute | solution.py:48
  7.3 2.6 %collective-permute-start.2 = (bf16[16,1024]{1,0:T(8,128)(2,1)S(1)}, bf16[16,1024]{1,0:T(8,128)(2,1)S(1)}, u32[]{:S(2)}, u32[]{:S(2)}) collective-permute-start(bf16[16,1024]{1,0:T(8,128)(2,1)S(1)} %get-tuple-element.21), channel_id=1, source_target_pairs={{0,1},{2,3},{1,0},{3,2},{4,5},{6,7},{5,4},{7,6},{8,9},{10,11},{9,8... | collective-permute-start | bytes 98312 | tf_op jit(solution)/shard_map/ppermute | solution.py:65
  7.4 2.5 %collective-permute-start.3 = (bf16[16,1024]{1,0:T(8,128)(2,1)S(1)}, bf16[16,1024]{1,0:T(8,128)(2,1)S(1)}, u32[]{:S(2)}, u32[]{:S(2)}) collective-permute-start(bf16[16,1024]{1,0:T(8,128)(2,1)S(1)} %get-tuple-element.20), channel_id=1, source_target_pairs={{1,2},{2,1},{5,6},{6,5},{9,10},{10,9},{13,14},{14,13},{17,18},{18,... | collective-permute-start | bytes 98312 | tf_op jit(solution)/shard_map/ppermute | solution.py:64
  9.8 3.8 %copy-start.4 = (f32[4]{0:T(128)S(1)}, f32[4]{0:T(128)}, u32[]{:S(2)}) copy-start(f32[4]{0:T(128)} %param.14) | copy-start | bytes 52
  9.9 3.7 %copy-start.5 = (s32[4]{0:T(128)S(1)}, s32[4]{0:T(128)}, u32[]{:S(2)}) copy-start(s32[4]{0:T(128)} %param.13) | copy-start | bytes 52
  10.0 3.9 %copy-start.3 = (s32[80,2]{0,1:T(2,128)S(1)}, s32[80,2]{0,1:T(2,128)}, u32[]{:S(2)}) copy-start(s32[80,2]{0,1:T(2,128)} %param.15) | copy-start | bytes 1924
  10.0 5.9 %collective-permute-start.4 = (bf16[16,4096]{1,0:T(8,128)(2,1)S(1)}, bf16[16,4096]{1,0:T(8,128)(2,1)S(1)}, u32[]{:S(2)}, u32[]{:S(2)}) collective-permute-start(bf16[16,4096]{1,0:T(8,128)(2,1)S(1)} %shard_map.95.refs_1_.refs_3_.refs_4_), channel_id=1, source_target_pairs={{0,12},{4,8},{8,4},{12,0},{16,28},{20,24},{24,20},{28,16},{1,13},{... | collective-permute-start | bytes 393224 | tf_op jit(solution)/shard_map/ppermute | solution.py:48
  12.6 5.5 %collective-permute-start.5 = (bf16[16,4096]{1,0:T(8,128)(2,1)S(1)}, bf16[16,4096]{1,0:T(8,128)(2,1)S(1)}, u32[]{:S(2)}, u32[]{:S(2)}) collective-permute-start(bf16[16,4096]{1,0:T(8,128)(2,1)S(1)} %shard_map.95.refs_1_.refs_3_.refs_4_), channel_id=1, source_target_pairs={{0,8},{4,12},{8,0},{12,4},{16,24},{20,28},{24,16},{28,20},{1,9},{5... | collective-permute-start | bytes 393224 | tf_op jit(solution)/shard_map/ppermute | solution.py:48
  13.1 6.8 %collective-permute-start.6 = (bf16[16,4096]{1,0:T(8,128)(2,1)S(1)}, bf16[16,4096]{1,0:T(8,128)(2,1)S(1)}, u32[]{:S(2)}, u32[]{:S(2)}) collective-permute-start(bf16[16,4096]{1,0:T(8,128)(2,1)S(1)} %shard_map.95.refs_1_.refs_3_.refs_4_), channel_id=1, source_target_pairs={{0,4},{4,0},{8,12},{12,8},{16,20},{20,16},{24,28},{28,24},{1,5},{5... | collective-permute-start | bytes 393224 | tf_op jit(solution)/shard_map/ppermute | solution.py:48
  20.5 3.6 %collective-permute-start.7 = (f32[64,128]{1,0:T(8,128)S(1)}, f32[64,128]{1,0:T(8,128)S(1)}, u32[]{:S(2)}, u32[]{:S(2)}) collective-permute-start(f32[64,128]{1,0:T(8,128)S(1)} %get-tuple-element.19.refs_5_), channel_id=1, source_target_pairs={{0,3},{1,2},{2,1},{3,0},{4,7},{5,6},{6,5},{7,4},{8,11},{9,10},{10,... | collective-permute-start | bytes 98312 | tf_op jit(solution)/shard_map/ppermute | solution.py:48
  20.6 4.9 %collective-permute-start.8 = (f32[64,128]{1,0:T(8,128)S(1)}, f32[64,128]{1,0:T(8,128)S(1)}, u32[]{:S(2)}, u32[]{:S(2)}) collective-permute-start(f32[64,128]{1,0:T(8,128)S(1)} %get-tuple-element.19.refs_5_), channel_id=1, source_target_pairs={{0,2},{1,3},{2,0},{3,1},{4,6},{5,7},{6,4},{7,5},{8,10},{9,11},{10,... | collective-permute-start | bytes 98312 | tf_op jit(solution)/shard_map/ppermute | solution.py:48
  23.3 2.2 %collective-permute-start.9 = (f32[64,128]{1,0:T(8,128)S(1)}, f32[64,128]{1,0:T(8,128)S(1)}, u32[]{:S(2)}, u32[]{:S(2)}) collective-permute-start(f32[64,128]{1,0:T(8,128)S(1)} %get-tuple-element.19.refs_5_), channel_id=1, source_target_pairs={{0,1},{1,0},{2,3},{3,2},{4,5},{5,4},{6,7},{7,6},{8,9},{9,8},{10,11... | collective-permute-start | bytes 98312 | tf_op jit(solution)/shard_map/ppermute | solution.py:48

commit v7 on v6

--- a/solution.py
+++ b/solution.py
@@ -180,8 +180,8 @@
     return fn
 
 
-def finish(local_modes, waves, rows, width, scale_pixels, scale_grad):
-    def fn(mask, order, back, early, late, *partials):
+def couple(local_modes, scale_pixels, exact_parts):
+    def fn(mask, order, *partials):
         total = mask.shape[0]
         summed = partials[0]
         for part in partials[1:]:
@@ -189,16 +189,17 @@
         real = summed[:, :total] * scale_pixels * mask
         imag = summed[:, total:] * scale_pixels * mask
         own = jnp.concatenate([real[:local_modes], imag[:local_modes]], axis=0)
-        high = own.astype(BF16)
-        rest = own - high.astype(F32)
-        middle = rest.astype(BF16)
-        low = (rest - middle.astype(F32)).astype(BF16)
-        sorted_parts = jnp.dot(
-            jnp.concatenate([high, middle, low], axis=0), order, preferred_element_type=F32
-        )
-        size = own.shape[0]
-        own = sorted_parts[:size] + sorted_parts[size : 2 * size] + sorted_parts[2 * size :]
-        coupling = own.reshape(2, local_modes, total)
+        if exact_parts:
+            high = own.astype(BF16)
+            rest = own - high.astype(F32)
+            middle = rest.astype(BF16)
+            low = (rest - middle.astype(F32)).astype(BF16)
+            parts = jnp.concatenate([high, middle, low], axis=0)
+            parts = jnp.dot(parts, order, preferred_element_type=F32)
+            size = own.shape[0]
+            own = parts[:size] + parts[size : 2 * size] + parts[2 * size :]
+        else:
+            own = jnp.dot(own, order.astype(F32), precision=lax.Precision.HIGHEST)
         weight_real, weight_imag = real.astype(BF16), imag.astype(BF16)
         weights = jnp.concatenate(
             [
@@ -207,14 +208,21 @@
             ],
             axis=0,
         )
+        return own.reshape(2, local_modes, total), weights
+
+    return fn
+
+
+def gradient(waves, rows, width, scale_grad):
+    def fn(weights, back, early, late):
+        total = weights.shape[0] // 2
         adjoint = jnp.dot(weights, back, preferred_element_type=F32)
         fields = both_parts([early, late]).astype(F32)
         term = fields[total:] * adjoint[:total] - fields[:total] * adjoint[total:]
         group = 2 * waves
         folded = jnp.sum(term.reshape(total // group, group, rows * width), axis=0)
         folded = (folded[:waves] + folded[waves:]) * scale_grad
-        grad = jnp.stack(by_rows(folded, width), axis=1)
-        return coupling, grad
+        return jnp.stack(by_rows(folded, width), axis=1)
 
     return fn
 
@@ -298,19 +306,17 @@
         [propagator, *pieces],
         flops=8 * total * half * width,
     )
-    coupling, mask_grad = local_call(
-        finish(
-            local_modes,
-            waves,
-            rows,
-            width,
-            1.0 / math.sqrt(row_total * width),
-            -2.0 / total,
-        ),
-        [array((2, local_modes, total), F32), array((waves, rows, width), F32)],
-        [mask, order, back, early_masked, late_masked, *partials],
-        flops=8 * total * total * half,
-    )
+    arrays = [mask, order, back, early_masked, late_masked, *partials]
+    outs = [array((2, local_modes, total), F32), array((waves, rows, width), F32)]
+    large = sum(size_of(item) for item in (*arrays, *outs)) > VMEM_BYTES
+    first = couple(local_modes, 1.0 / math.sqrt(row_total * width), not large)
+    second = gradient(waves, rows, width, -2.0 / total)
+
+    def finish(mask, order, back, early, late, *partials):
+        coupling, weights = first(mask, order, *partials)
+        return coupling, second(weights, back, early, late)
+
+    coupling, mask_grad = local_call(finish, outs, arrays, flops=8 * total * total * half)
     return coupling, mask_grad
 
 

time: 26.9 us -> 26.9 us (level)
  no operation moved by 1% of the time
where the time goes in v7:
time: 26.9 us; the launch traced here: 26.5 us
  starting transfers between devices  11.3 us (42%)
  waiting for transfers between devices  9.37 us (35%)
  Pallas kernels  2.7 us (10%)
  local copies, waits for them, and re-layouts  0.89 us (3%)
  between operations  0.85 us (3%)
  other arithmetic  0.82 us (3%)
  matrix products  0.59 us (2%)
    ppermute x8, starting transfers between devices, swapped(): return lax.ppermute(values, axis, [(i, i ^ distance) for i in range(peers)])  10.6 us
    ppermute x8, waiting for transfers between devices, swapped(): return lax.ppermute(values, axis, [(i, i ^ distance) for i in range(peers)])  9.36 us
    pallas_call x5, Pallas kernels, local_call(): pl.pallas_call(kernel, out_shape=tuple(outs), in_specs=[pl.BlockSpec(memo...  2.7 us
    transpose x4, local copies, waits for them, and re-layouts, body(): fields.transpose(0, 2, 1, 3).reshape(fields.shape[0], 2 * half)  0.8 us
    pad x1, other arithmetic, body(): jnp.pad(taps, ((0, 5), (0, 125)))  0.69 us
    ppermute x1, starting transfers between devices, neighbour_rows(): lax.ppermute(jnp.where(odd, last, first), 'row', pairs_of(peers, 1))  0.66 us
  transfers between devices with their start and end apart: 10, of which 6 were waited for; matrix products, arithmetic and copies ran while one was open for 9% of the time, Pallas kernels for 3%

profile of v7, /device:TPU:0, one launch (start us, length us, event | category | flops | bytes accessed | tf_op | source)
XLA Modules:
  0.0 26.5 jit_solution(611969957571705860)
XLA Ops:
  0.7 4.1 %collective-permute-start.1 = (bf16[8,2,2,512]{3,2,1,0:T(2,128)(2,1)}, bf16[8,2,2,512]{3,2,1,0:T(2,128)(2,1)S(1)}, u32[]{:S(2)}, u32[]{:S(2)}) collective-permute-start(bf16[8,2,2,512]{3,2,1,0:T(2,128)(2,1)} %param.9), channel_id=1, source_target_pairs={{0,16},{4,20},{8,24},{12,28},{16,0},{20,4},{24,8},{28,12},{1,17},{... | collective-permute-start | bytes 98312 | tf_op jit(solution)/shard_map/ppermute | solution.py:48
  4.8 0.1 collective-permute-start
  4.9 0.1 fusion.8.refs_1_
  4.9 0.7 %select_select_fusion.refs_0_ = f32[8,128]{1,0:T(8,128)S(1)} fusion(f32[2,3]{1,0:T(2,128)} %param.11, f32[]{:T(128)S(6)} %convert_element_type.6), kind=kLoop, calls=%fused_computation.30 | loop fusion | flops 5120 | bytes 4124 | tf_op jit(solution)/shard_map/jit(_pad)/pad | solution.py:259
  5.6 0.8 %copy.10 = bf16[8,2,2,512]{3,0,2,1:T(8,128)(2,1)S(1)} copy(bf16[8,2,2,512]{3,1,2,0:T(2,128)(2,1)} %bitcast.26) | data formatting | bytes 65536 | tf_op jit(solution)/shard_map/transpose | solution.py:240
  6.4 0.8 %collective-permute-done.1 = bf16[8,2,2,512]{3,2,1,0:T(2,128)(2,1)S(1)} collective-permute-done((bf16[8,2,2,512]{3,2,1,0:T(2,128)(2,1)}, bf16[8,2,2,512]{3,2,1,0:T(2,128)(2,1)S(1)}, u32[]{:S(2)}, u32[]{:S(2)}) %collective-permute-start.1) | collective-permute-done | bytes 32800 | tf_op jit(solution)/shard_map/ppermute | solution.py:48
  7.3 0.1 collective-permute-start.2
  7.4 0.7 %collective-permute-start.3 = (bf16[16,1024]{1,0:T(8,128)(2,1)S(1)}, bf16[16,1024]{1,0:T(8,128)(2,1)S(1)}, u32[]{:S(2)}, u32[]{:S(2)}) collective-permute-start(bf16[16,1024]{1,0:T(8,128)(2,1)S(1)} %get-tuple-element.20), channel_id=1, source_target_pairs={{1,2},{2,1},{5,6},{6,5},{9,10},{10,9},{13,14},{14,13},{17,18},{18,... | collective-permute-start | bytes 98312 | tf_op jit(solution)/shard_map/ppermute | solution.py:64
  8.0 1.8 %collective-permute-done = bf16[8,2,2,512]{3,2,1,0:T(2,128)(2,1)S(1)} collective-permute-done((bf16[8,2,2,512]{3,2,1,0:T(2,128)(2,1)}, bf16[8,2,2,512]{3,2,1,0:T(2,128)(2,1)S(1)}, u32[]{:S(2)}, u32[]{:S(2)}) %collective-permute-start) | collective-permute-done | bytes 32800 | tf_op jit(solution)/shard_map/ppermute | solution.py:48
  9.9 0.1 shard_map.95.refs_1_.refs_3_.refs_4_
  10.0 2.6 %collective-permute-start.4 = (bf16[16,4096]{1,0:T(8,128)(2,1)S(1)}, bf16[16,4096]{1,0:T(8,128)(2,1)S(1)}, u32[]{:S(2)}, u32[]{:S(2)}) collective-permute-start(bf16[16,4096]{1,0:T(8,128)(2,1)S(1)} %shard_map.95.refs_1_.refs_3_.refs_4_), channel_id=1, source_target_pairs={{0,12},{4,8},{8,4},{12,0},{16,28},{20,24},{24,20},{28,16},{1,13},{... | collective-permute-start | bytes 393224 | tf_op jit(solution)/shard_map/ppermute | solution.py:48
  12.6 0.4 %collective-permute-start.5 = (bf16[16,4096]{1,0:T(8,128)(2,1)S(1)}, bf16[16,4096]{1,0:T(8,128)(2,1)S(1)}, u32[]{:S(2)}, u32[]{:S(2)}) collective-permute-start(bf16[16,4096]{1,0:T(8,128)(2,1)S(1)} %shard_map.95.refs_1_.refs_3_.refs_4_), channel_id=1, source_target_pairs={{0,8},{4,12},{8,0},{12,4},{16,24},{20,28},{24,16},{28,20},{1,9},{5... | collective-permute-start | bytes 393224 | tf_op jit(solution)/shard_map/ppermute | solution.py:48
  13.1 0.5 %collective-permute-start.6 = (bf16[16,4096]{1,0:T(8,128)(2,1)S(1)}, bf16[16,4096]{1,0:T(8,128)(2,1)S(1)}, u32[]{:S(2)}, u32[]{:S(2)}) collective-permute-start(bf16[16,4096]{1,0:T(8,128)(2,1)S(1)} %shard_map.95.refs_1_.refs_3_.refs_4_), channel_id=1, source_target_pairs={{0,4},{4,0},{8,12},{12,8},{16,20},{20,16},{24,28},{28,24},{1,5},{5... | collective-permute-start | bytes 393224 | tf_op jit(solution)/shard_map/ppermute | solution.py:48
  13.6 0.3 %fusion.32 = (f32[4,2,512]{2,0,1:T(4,128)S(1)}, f32[4,2,512]{2,0,1:T(4,128)S(1)}) fusion(f32[4]{0:T(128)S(1)} %copy-done.4, f32[7,2,512]{2,1,0:T(2,128)S(1)} %copy-done, s32[4]{0:T(128)S(1)} %copy-done.5), kind=kOutput, calls=%fused_computation.74 | convolution fusion | flops 348188 | bytes 61472 | tf_op jit(solution)/shard_map/wp,prc->wrc/dot_general | solution.py:269
  14.0 1.9 %collective-permute-done.4.refs_2_.refs_4_.refs_5_ = bf16[16,4096]{1,0:T(8,128)(2,1)S(1)} collective-permute-done((bf16[16,4096]{1,0:T(8,128)(2,1)S(1)}, bf16[16,4096]{1,0:T(8,128)(2,1)S(1)}, u32[]{:S(2)}, u32[]{:S(2)}) %collective-permute-start.4) | collective-permute-done | bytes 131104 | tf_op jit(solution)/shard_map/ppermute | solution.py:48
  16.0 2.2 %collective-permute-done.5.refs_3_.refs_5_.refs_6_ = bf16[16,4096]{1,0:T(8,128)(2,1)S(1)} collective-permute-done((bf16[16,4096]{1,0:T(8,128)(2,1)S(1)}, bf16[16,4096]{1,0:T(8,128)(2,1)S(1)}, u32[]{:S(2)}, u32[]{:S(2)}) %collective-permute-start.5) | collective-permute-done | bytes 131104 | tf_op jit(solution)/shard_map/ppermute | solution.py:48
  18.1 0.4 %shard_map.97 = (bf16[96,1024]{1,0:T(8,128)(2,1)S(1)}, bf16[96,1024]{1,0:T(8,128)(2,1)S(1)}) custom-call(f32[8,1024]{1,0:T(8,128)S(1)} %tile.9.refs_0_, f32[8,1024]{1,0:T(8,128)S(1)} %tile.21.refs_1_, bf16[2,512,512]{2,1,0:T(8,128)(2,1)S(1)} %copy-done.1, bf16[16,4096]{1,0:T(8,128)(2,1)S(1)} %shard_map.95.refs_1_.refs_3_.refs_4_, ...), custom_call_target="tpu_custom_call" | custom-call | flops 201326592 | bytes 1900544 | tf_op jit(solution)/shard_map/pallas_call | solution.py:32
  18.5 1.3 %collective-permute-done.6.refs_4_.refs_7_ = bf16[16,4096]{1,0:T(8,128)(2,1)S(1)} collective-permute-done((bf16[16,4096]{1,0:T(8,128)(2,1)S(1)}, bf16[16,4096]{1,0:T(8,128)(2,1)S(1)}, u32[]{:S(2)}, u32[]{:S(2)}) %collective-permute-start.6) | collective-permute-done | bytes 131104 | tf_op jit(solution)/shard_map/ppermute | solution.py:48
  19.8 0.7 %shard_map.98 = (bf16[32,1024]{1,0:T(8,128)(2,1)S(1)}, f32[64,128]{1,0:T(8,128)S(1)}) custom-call(f32[8,1024]{1,0:T(8,128)S(1)} %tile.9.refs_0_, f32[8,1024]{1,0:T(8,128)S(1)} %tile.21.refs_1_, bf16[2,512,512]{2,1,0:T(8,128)(2,1)S(1)} %copy-done.1, bf16[96,1024]{1,0:T(8,128)(2,1)S(1)} %get-tuple-element.17.refs_3_, ...), custom_call_target="tpu_custom_call" | custom-call | flops 100663296 | bytes 1933312 | tf_op jit(solution)/shard_map/pallas_call | solution.py:32
  20.6 2.7 %collective-permute-start.8 = (f32[64,128]{1,0:T(8,128)S(1)}, f32[64,128]{1,0:T(8,128)S(1)}, u32[]{:S(2)}, u32[]{:S(2)}) collective-permute-start(f32[64,128]{1,0:T(8,128)S(1)} %get-tuple-element.19.refs_5_), channel_id=1, source_target_pairs={{0,2},{1,3},{2,0},{3,1},{4,6},{5,7},{6,4},{7,5},{8,10},{9,11},{10,... | collective-permute-start | bytes 98312 | tf_op jit(solution)/shard_map/ppermute | solution.py:48
  23.3 0.3 fusion.refs_0_
  23.6 0.5 %shard_map.96.refs_2_ = bf16[128,1024]{1,0:T(8,128)(2,1)S(1)} custom-call(bf16[2,512,512]{2,1,0:T(8,128)(2,1)S(1)} %copy-done.1, bf16[16,4096]{1,0:T(8,128)(2,1)S(1)} %shard_map.95.refs_1_.refs_3_.refs_4_, bf16[16,4096]{1,0:T(8,128)(2,1)S(1)} %collective-permute-done.4.refs_2_.refs_4_.refs_5_, ...), custom_call_target="tpu_custom_call" | custom-call | flops 268435456 | bytes 1835008 | tf_op jit(solution)/shard_map/pallas_call | solution.py:32
  24.1 1.4 %collective-permute-done.8.refs_7_ = f32[64,128]{1,0:T(8,128)S(1)} collective-permute-done((f32[64,128]{1,0:T(8,128)S(1)}, f32[64,128]{1,0:T(8,128)S(1)}, u32[]{:S(2)}, u32[]{:S(2)}) %collective-permute-start.8) | collective-permute-done | bytes 32800 | tf_op jit(solution)/shard_map/ppermute | solution.py:48
  25.5 1.0 %shard_map.99 = (f32[2,8,64]{2,1,0:T(8,128)}, f32[4,2,512]{2,1,0:T(2,128)}) custom-call(f32[64,64]{1,0:T(8,128)S(1)} %fusion.refs_0_, bf16[64,64]{1,0:T(8,128)(2,1)S(1)} %fusion.8.refs_1_, bf16[128,1024]{1,0:T(8,128)(2,1)S(1)} %shard_map.96.refs_2_, bf16[96,1024]{1,0:T(8,128)(2,1)S(1)} %get-tuple-element.16.refs_3_, ...), custom_call_target="tpu_custom_call" | custom-call | flops 33554432 | bytes 700416 | tf_op jit(solution)/shard_map/pallas_call | solution.py:32
  (30 shorter events, 0.3 us)
Async XLA Ops:
  0.6 13.0 %copy-start = (f32[7,2,512]{2,1,0:T(2,128)S(1)}, f32[7,2,512]{2,1,0:T(2,128)}, u32[]{:S(2)}) copy-start(f32[7,2,512]{2,1,0:T(2,128)} %param.12) | copy-start | bytes 86020
  0.6 5.0 %copy-start.2 = (bf16[8,2,2,512]{3,2,1,0:T(2,128)(2,1)S(1)}, bf16[8,2,2,512]{3,2,1,0:T(2,128)(2,1)}, u32[]{:S(2)}) copy-start(bf16[8,2,2,512]{3,2,1,0:T(2,128)(2,1)} %param.9) | copy-start | bytes 98308
  0.7 17.5 %copy-start.1 = (bf16[2,512,512]{2,1,0:T(8,128)(2,1)S(1)}, bf16[2,512,512]{2,1,0:T(8,128)(2,1)}, u32[]{:S(2)}) copy-start(bf16[2,512,512]{2,1,0:T(8,128)(2,1)} %refs_2_.3) | copy-start | bytes 3145732
  0.7 6.6 %collective-permute-start.1 = (bf16[8,2,2,512]{3,2,1,0:T(2,128)(2,1)}, bf16[8,2,2,512]{3,2,1,0:T(2,128)(2,1)S(1)}, u32[]{:S(2)}, u32[]{:S(2)}) collective-permute-start(bf16[8,2,2,512]{3,2,1,0:T(2,128)(2,1)} %param.9), channel_id=1, source_target_pairs={{0,16},{4,20},{8,24},{12,28},{16,0},{20,4},{24,8},{28,12},{1,17},{... | collective-permute-start | bytes 98312 | tf_op jit(solution)/shard_map/ppermute | solution.py:48
  4.8 5.0 %collective-permute-start = (bf16[8,2,2,512]{3,2,1,0:T(2,128)(2,1)}, bf16[8,2,2,512]{3,2,1,0:T(2,128)(2,1)S(1)}, u32[]{:S(2)}, u32[]{:S(2)}) collective-permute-start(bf16[8,2,2,512]{3,2,1,0:T(2,128)(2,1)} %param.8), channel_id=1, source_target_pairs={{0,16},{4,20},{8,24},{12,28},{16,0},{20,4},{24,8},{28,12},{1,17},{... | collective-permute-start | bytes 98312 | tf_op jit(solution)/shard_map/ppermute | solution.py:48
  7.3 2.6 %collective-permute-start.2 = (bf16[16,1024]{1,0:T(8,128)(2,1)S(1)}, bf16[16,1024]{1,0:T(8,128)(2,1)S(1)}, u32[]{:S(2)}, u32[]{:S(2)}) collective-permute-start(bf16[16,1024]{1,0:T(8,128)(2,1)S(1)} %get-tuple-element.21), channel_id=1, source_target_pairs={{0,1},{2,3},{1,0},{3,2},{4,5},{6,7},{5,4},{7,6},{8,9},{10,11},{9,8... | collective-permute-start | bytes 98312 | tf_op jit(solution)/shard_map/ppermute | solution.py:65
  7.4 2.5 %collective-permute-start.3 = (bf16[16,1024]{1,0:T(8,128)(2,1)S(1)}, bf16[16,1024]{1,0:T(8,128)(2,1)S(1)}, u32[]{:S(2)}, u32[]{:S(2)}) collective-permute-start(bf16[16,1024]{1,0:T(8,128)(2,1)S(1)} %get-tuple-element.20), channel_id=1, source_target_pairs={{1,2},{2,1},{5,6},{6,5},{9,10},{10,9},{13,14},{14,13},{17,18},{18,... | collective-permute-start | bytes 98312 | tf_op jit(solution)/shard_map/ppermute | solution.py:64
  9.8 3.8 %copy-start.4 = (f32[4]{0:T(128)S(1)}, f32[4]{0:T(128)}, u32[]{:S(2)}) copy-start(f32[4]{0:T(128)} %param.14) | copy-start | bytes 52
  9.9 3.7 %copy-start.5 = (s32[4]{0:T(128)S(1)}, s32[4]{0:T(128)}, u32[]{:S(2)}) copy-start(s32[4]{0:T(128)} %param.13) | copy-start | bytes 52
  10.0 3.9 %copy-start.3 = (s32[80,2]{0,1:T(2,128)S(1)}, s32[80,2]{0,1:T(2,128)}, u32[]{:S(2)}) copy-start(s32[80,2]{0,1:T(2,128)} %param.15) | copy-start | bytes 1924
  10.0 5.9 %collective-permute-start.4 = (bf16[16,4096]{1,0:T(8,128)(2,1)S(1)}, bf16[16,4096]{1,0:T(8,128)(2,1)S(1)}, u32[]{:S(2)}, u32[]{:S(2)}) collective-permute-start(bf16[16,4096]{1,0:T(8,128)(2,1)S(1)} %shard_map.95.refs_1_.refs_3_.refs_4_), channel_id=1, source_target_pairs={{0,12},{4,8},{8,4},{12,0},{16,28},{20,24},{24,20},{28,16},{1,13},{... | collective-permute-start | bytes 393224 | tf_op jit(solution)/shard_map/ppermute | solution.py:48
  12.6 5.5 %collective-permute-start.5 = (bf16[16,4096]{1,0:T(8,128)(2,1)S(1)}, bf16[16,4096]{1,0:T(8,128)(2,1)S(1)}, u32[]{:S(2)}, u32[]{:S(2)}) collective-permute-start(bf16[16,4096]{1,0:T(8,128)(2,1)S(1)} %shard_map.95.refs_1_.refs_3_.refs_4_), channel_id=1, source_target_pairs={{0,8},{4,12},{8,0},{12,4},{16,24},{20,28},{24,16},{28,20},{1,9},{5... | collective-permute-start | bytes 393224 | tf_op jit(solution)/shard_map/ppermute | solution.py:48
  13.1 6.8 %collective-permute-start.6 = (bf16[16,4096]{1,0:T(8,128)(2,1)S(1)}, bf16[16,4096]{1,0:T(8,128)(2,1)S(1)}, u32[]{:S(2)}, u32[]{:S(2)}) collective-permute-start(bf16[16,4096]{1,0:T(8,128)(2,1)S(1)} %shard_map.95.refs_1_.refs_3_.refs_4_), channel_id=1, source_target_pairs={{0,4},{4,0},{8,12},{12,8},{16,20},{20,16},{24,28},{28,24},{1,5},{5... | collective-permute-start | bytes 393224 | tf_op jit(solution)/shard_map/ppermute | solution.py:48
  20.5 3.6 %collective-permute-start.7 = (f32[64,128]{1,0:T(8,128)S(1)}, f32[64,128]{1,0:T(8,128)S(1)}, u32[]{:S(2)}, u32[]{:S(2)}) collective-permute-start(f32[64,128]{1,0:T(8,128)S(1)} %get-tuple-element.19.refs_5_), channel_id=1, source_target_pairs={{0,3},{1,2},{2,1},{3,0},{4,7},{5,6},{6,5},{7,4},{8,11},{9,10},{10,... | collective-permute-start | bytes 98312 | tf_op jit(solution)/shard_map/ppermute | solution.py:48
  20.6 4.9 %collective-permute-start.8 = (f32[64,128]{1,0:T(8,128)S(1)}, f32[64,128]{1,0:T(8,128)S(1)}, u32[]{:S(2)}, u32[]{:S(2)}) collective-permute-start(f32[64,128]{1,0:T(8,128)S(1)} %get-tuple-element.19.refs_5_), channel_id=1, source_target_pairs={{0,2},{1,3},{2,0},{3,1},{4,6},{5,7},{6,4},{7,5},{8,10},{9,11},{10,... | collective-permute-start | bytes 98312 | tf_op jit(solution)/shard_map/ppermute | solution.py:48
  23.3 2.2 %collective-permute-start.9 = (f32[64,128]{1,0:T(8,128)S(1)}, f32[64,128]{1,0:T(8,128)S(1)}, u32[]{:S(2)}, u32[]{:S(2)}) collective-permute-start(f32[64,128]{1,0:T(8,128)S(1)} %get-tuple-element.19.refs_5_), channel_id=1, source_target_pairs={{0,1},{1,0},{2,3},{3,2},{4,5},{5,4},{6,7},{7,6},{8,9},{9,8},{10,11... | collective-permute-start | bytes 98312 | tf_op jit(solution)/shard_map/ppermute | solution.py:48

commit v8 on v7

--- a/solution.py
+++ b/solution.py
@@ -242,12 +242,15 @@
     distances = head + last[:2]
     targets, fields = backward, forward
     for distance in head:
-        near, far = (targets, fields), [
-            swapped(values, "mode", distance) for values in (targets, fields)
-        ]
+        far = [swapped(values, "mode", distance) for values in (targets, fields)]
         if targets.ndim > 2:
-            near, far = [flat(values) for values in near], [flat(values) for values in far]
-        targets, fields = [jnp.concatenate(both, axis=0) for both in zip(near, far)]
+            targets, far = flat(targets), [flat(values) for values in far]
+            targets = jnp.concatenate([targets, far[0]], axis=0)
+            targets, fields = lax.optimization_barrier((targets, fields))
+            fields = jnp.concatenate([flat(fields), far[1]], axis=0)
+        else:
+            targets = jnp.concatenate([targets, far[0]], axis=0)
+            fields = jnp.concatenate([fields, far[1]], axis=0)
     if targets.ndim > 2:
         targets, fields = flat(targets), flat(fields)
     over_even, over_odd = neighbour_rows(targets, width)

time: 26.9 us -> 26.9 us (level)
  no operation moved by 1% of the time
where the time goes in v8:
time: 26.9 us; the launch traced here: 26.5 us
  starting transfers between devices  11.3 us (42%)
  waiting for transfers between devices  9.35 us (35%)
  Pallas kernels  2.7 us (10%)
  local copies, waits for them, and re-layouts  0.89 us (3%)
  between operations  0.85 us (3%)
  other arithmetic  0.81 us (3%)
  matrix products  0.59 us (2%)
    ppermute x8, starting transfers between devices, swapped(): return lax.ppermute(values, axis, [(i, i ^ distance) for i in range(peers)])  10.6 us
    ppermute x8, waiting for transfers between devices, swapped(): return lax.ppermute(values, axis, [(i, i ^ distance) for i in range(peers)])  9.34 us
    pallas_call x5, Pallas kernels, local_call(): pl.pallas_call(kernel, out_shape=tuple(outs), in_specs=[pl.BlockSpec(memo...  2.7 us
    transpose x4, local copies, waits for them, and re-layouts, body(): fields.transpose(0, 2, 1, 3).reshape(fields.shape[0], 2 * half)  0.8 us
    pad x1, other arithmetic, body(): jnp.pad(taps, ((0, 5), (0, 125)))  0.69 us
    ppermute x1, starting transfers between devices, neighbour_rows(): lax.ppermute(jnp.where(odd, last, first), 'row', pairs_of(peers, 1))  0.66 us
  transfers between devices with their start and end apart: 10, of which 6 were waited for; matrix products, arithmetic and copies ran while one was open for 9% of the time, Pallas kernels for 3%

profile of v8, /device:TPU:0, one launch (start us, length us, event | category | flops | bytes accessed | tf_op | source)
XLA Modules:
  0.0 26.5 jit_solution(5830485054779819621)
XLA Ops:
  0.7 4.1 %collective-permute-start = (bf16[8,2,2,512]{3,2,1,0:T(2,128)(2,1)}, bf16[8,2,2,512]{3,2,1,0:T(2,128)(2,1)S(1)}, u32[]{:S(2)}, u32[]{:S(2)}) collective-permute-start(bf16[8,2,2,512]{3,2,1,0:T(2,128)(2,1)} %param.9), channel_id=1, source_target_pairs={{0,16},{4,20},{8,24},{12,28},{16,0},{20,4},{24,8},{28,12},{1,17},{... | collective-permute-start | bytes 98312 | tf_op jit(solution)/shard_map/ppermute | solution.py:48
  4.8 0.1 collective-permute-start.1
  4.9 0.1 fusion.8.refs_1_
  4.9 0.7 %select_select_fusion.refs_0_ = f32[8,128]{1,0:T(8,128)S(1)} fusion(f32[2,3]{1,0:T(2,128)} %param.11, f32[]{:T(128)S(6)} %convert_element_type.6), kind=kLoop, calls=%fused_computation.18 | loop fusion | flops 5120 | bytes 4124 | tf_op jit(solution)/shard_map/jit(_pad)/pad | solution.py:262
  5.6 1.6 %collective-permute-done = bf16[8,2,2,512]{3,2,1,0:T(2,128)(2,1)S(1)} collective-permute-done((bf16[8,2,2,512]{3,2,1,0:T(2,128)(2,1)}, bf16[8,2,2,512]{3,2,1,0:T(2,128)(2,1)S(1)}, u32[]{:S(2)}, u32[]{:S(2)}) %collective-permute-start) | collective-permute-done | bytes 32800 | tf_op jit(solution)/shard_map/ppermute | solution.py:48
  7.3 0.1 collective-permute-start.2
  7.4 0.7 %collective-permute-start.3 = (bf16[16,1024]{1,0:T(8,128)(2,1)S(1)}, bf16[16,1024]{1,0:T(8,128)(2,1)S(1)}, u32[]{:S(2)}, u32[]{:S(2)}) collective-permute-start(bf16[16,1024]{1,0:T(8,128)(2,1)S(1)} %get-tuple-element.24), channel_id=1, source_target_pairs={{1,2},{2,1},{5,6},{6,5},{9,10},{10,9},{13,14},{14,13},{17,18},{18,... | collective-permute-start | bytes 98312 | tf_op jit(solution)/shard_map/ppermute | solution.py:64
  8.0 0.8 %copy.12 = bf16[8,2,2,512]{3,0,2,1:T(8,128)(2,1)S(1)} copy(bf16[8,2,2,512]{3,1,2,0:T(2,128)(2,1)} %bitcast.24) | data formatting | bytes 65536 | tf_op jit(solution)/shard_map/transpose | solution.py:240
  8.8 1.0 %collective-permute-done.1 = bf16[8,2,2,512]{3,2,1,0:T(2,128)(2,1)S(1)} collective-permute-done((bf16[8,2,2,512]{3,2,1,0:T(2,128)(2,1)}, bf16[8,2,2,512]{3,2,1,0:T(2,128)(2,1)S(1)}, u32[]{:S(2)}, u32[]{:S(2)}) %collective-permute-start.1) | collective-permute-done | bytes 32800 | tf_op jit(solution)/shard_map/ppermute | solution.py:48
  9.9 0.1 shard_map.95.refs_1_.refs_3_.refs_4_
  10.0 2.6 %collective-permute-start.4 = (bf16[16,4096]{1,0:T(8,128)(2,1)S(1)}, bf16[16,4096]{1,0:T(8,128)(2,1)S(1)}, u32[]{:S(2)}, u32[]{:S(2)}) collective-permute-start(bf16[16,4096]{1,0:T(8,128)(2,1)S(1)} %shard_map.95.refs_1_.refs_3_.refs_4_), channel_id=1, source_target_pairs={{0,12},{4,8},{8,4},{12,0},{16,28},{20,24},{24,20},{28,16},{1,13},{... | collective-permute-start | bytes 393224 | tf_op jit(solution)/shard_map/ppermute | solution.py:48
  12.6 0.4 %collective-permute-start.5 = (bf16[16,4096]{1,0:T(8,128)(2,1)S(1)}, bf16[16,4096]{1,0:T(8,128)(2,1)S(1)}, u32[]{:S(2)}, u32[]{:S(2)}) collective-permute-start(bf16[16,4096]{1,0:T(8,128)(2,1)S(1)} %shard_map.95.refs_1_.refs_3_.refs_4_), channel_id=1, source_target_pairs={{0,8},{4,12},{8,0},{12,4},{16,24},{20,28},{24,16},{28,20},{1,9},{5... | collective-permute-start | bytes 393224 | tf_op jit(solution)/shard_map/ppermute | solution.py:48
  13.1 0.5 %collective-permute-start.6 = (bf16[16,4096]{1,0:T(8,128)(2,1)S(1)}, bf16[16,4096]{1,0:T(8,128)(2,1)S(1)}, u32[]{:S(2)}, u32[]{:S(2)}) collective-permute-start(bf16[16,4096]{1,0:T(8,128)(2,1)S(1)} %shard_map.95.refs_1_.refs_3_.refs_4_), channel_id=1, source_target_pairs={{0,4},{4,0},{8,12},{12,8},{16,20},{20,16},{24,28},{28,24},{1,5},{5... | collective-permute-start | bytes 393224 | tf_op jit(solution)/shard_map/ppermute | solution.py:48
  13.6 0.3 %fusion.29 = (f32[4,2,512]{2,0,1:T(4,128)S(1)}, f32[4,2,512]{2,0,1:T(4,128)S(1)}) fusion(f32[4]{0:T(128)S(1)} %copy-done.4, f32[7,2,512]{2,1,0:T(2,128)S(1)} %copy-done, s32[4]{0:T(128)S(1)} %copy-done.5), kind=kOutput, calls=%fused_computation.63 | convolution fusion | flops 348188 | bytes 61472 | tf_op jit(solution)/shard_map/wp,prc->wrc/dot_general | solution.py:272
  14.0 1.9 %collective-permute-done.4.refs_2_.refs_4_.refs_5_ = bf16[16,4096]{1,0:T(8,128)(2,1)S(1)} collective-permute-done((bf16[16,4096]{1,0:T(8,128)(2,1)S(1)}, bf16[16,4096]{1,0:T(8,128)(2,1)S(1)}, u32[]{:S(2)}, u32[]{:S(2)}) %collective-permute-start.4) | collective-permute-done | bytes 131104 | tf_op jit(solution)/shard_map/ppermute | solution.py:48
  16.0 2.1 %collective-permute-done.5.refs_3_.refs_5_.refs_6_ = bf16[16,4096]{1,0:T(8,128)(2,1)S(1)} collective-permute-done((bf16[16,4096]{1,0:T(8,128)(2,1)S(1)}, bf16[16,4096]{1,0:T(8,128)(2,1)S(1)}, u32[]{:S(2)}, u32[]{:S(2)}) %collective-permute-start.5) | collective-permute-done | bytes 131104 | tf_op jit(solution)/shard_map/ppermute | solution.py:48
  18.1 0.4 %shard_map.97 = (bf16[96,1024]{1,0:T(8,128)(2,1)S(1)}, bf16[96,1024]{1,0:T(8,128)(2,1)S(1)}) custom-call(f32[8,1024]{1,0:T(8,128)S(1)} %tile.9.refs_0_, f32[8,1024]{1,0:T(8,128)S(1)} %tile.21.refs_1_, bf16[2,512,512]{2,1,0:T(8,128)(2,1)S(1)} %copy-done.1, bf16[16,4096]{1,0:T(8,128)(2,1)S(1)} %shard_map.95.refs_1_.refs_3_.refs_4_, ...), custom_call_target="tpu_custom_call" | custom-call | flops 201326592 | bytes 1900544 | tf_op jit(solution)/shard_map/pallas_call | solution.py:32
  18.5 1.3 %collective-permute-done.6.refs_4_.refs_7_ = bf16[16,4096]{1,0:T(8,128)(2,1)S(1)} collective-permute-done((bf16[16,4096]{1,0:T(8,128)(2,1)S(1)}, bf16[16,4096]{1,0:T(8,128)(2,1)S(1)}, u32[]{:S(2)}, u32[]{:S(2)}) %collective-permute-start.6) | collective-permute-done | bytes 131104 | tf_op jit(solution)/shard_map/ppermute | solution.py:48
  19.8 0.7 %shard_map.98 = (bf16[32,1024]{1,0:T(8,128)(2,1)S(1)}, f32[64,128]{1,0:T(8,128)S(1)}) custom-call(f32[8,1024]{1,0:T(8,128)S(1)} %tile.9.refs_0_, f32[8,1024]{1,0:T(8,128)S(1)} %tile.21.refs_1_, bf16[2,512,512]{2,1,0:T(8,128)(2,1)S(1)} %copy-done.1, bf16[96,1024]{1,0:T(8,128)(2,1)S(1)} %get-tuple-element.21.refs_3_, ...), custom_call_target="tpu_custom_call" | custom-call | flops 100663296 | bytes 1933312 | tf_op jit(solution)/shard_map/pallas_call | solution.py:32
  20.6 2.7 %collective-permute-start.8 = (f32[64,128]{1,0:T(8,128)S(1)}, f32[64,128]{1,0:T(8,128)S(1)}, u32[]{:S(2)}, u32[]{:S(2)}) collective-permute-start(f32[64,128]{1,0:T(8,128)S(1)} %get-tuple-element.23.refs_5_), channel_id=1, source_target_pairs={{0,2},{1,3},{2,0},{3,1},{4,6},{5,7},{6,4},{7,5},{8,10},{9,11},{10,... | collective-permute-start | bytes 98312 | tf_op jit(solution)/shard_map/ppermute | solution.py:48
  23.4 0.3 fusion.refs_0_
  23.6 0.5 %shard_map.96.refs_2_ = bf16[128,1024]{1,0:T(8,128)(2,1)S(1)} custom-call(bf16[2,512,512]{2,1,0:T(8,128)(2,1)S(1)} %copy-done.1, bf16[16,4096]{1,0:T(8,128)(2,1)S(1)} %shard_map.95.refs_1_.refs_3_.refs_4_, bf16[16,4096]{1,0:T(8,128)(2,1)S(1)} %collective-permute-done.4.refs_2_.refs_4_.refs_5_, ...), custom_call_target="tpu_custom_call" | custom-call | flops 268435456 | bytes 1835008 | tf_op jit(solution)/shard_map/pallas_call | solution.py:32
  24.1 1.4 %collective-permute-done.8.refs_7_ = f32[64,128]{1,0:T(8,128)S(1)} collective-permute-done((f32[64,128]{1,0:T(8,128)S(1)}, f32[64,128]{1,0:T(8,128)S(1)}, u32[]{:S(2)}, u32[]{:S(2)}) %collective-permute-start.8) | collective-permute-done | bytes 32800 | tf_op jit(solution)/shard_map/ppermute | solution.py:48
  25.5 1.0 %shard_map.99 = (f32[2,8,64]{2,1,0:T(8,128)}, f32[4,2,512]{2,1,0:T(2,128)}) custom-call(f32[64,64]{1,0:T(8,128)S(1)} %fusion.refs_0_, bf16[64,64]{1,0:T(8,128)(2,1)S(1)} %fusion.8.refs_1_, bf16[128,1024]{1,0:T(8,128)(2,1)S(1)} %shard_map.96.refs_2_, bf16[96,1024]{1,0:T(8,128)(2,1)S(1)} %get-tuple-element.20.refs_3_, ...), custom_call_target="tpu_custom_call" | custom-call | flops 33554432 | bytes 700416 | tf_op jit(solution)/shard_map/pallas_call | solution.py:32
  (31 shorter events, 0.3 us)
Async XLA Ops:
  0.6 13.0 %copy-start = (f32[7,2,512]{2,1,0:T(2,128)S(1)}, f32[7,2,512]{2,1,0:T(2,128)}, u32[]{:S(2)}) copy-start(f32[7,2,512]{2,1,0:T(2,128)} %param.12) | copy-start | bytes 86020
  0.6 5.0 %copy-start.2 = (bf16[8,2,2,512]{3,2,1,0:T(2,128)(2,1)S(1)}, bf16[8,2,2,512]{3,2,1,0:T(2,128)(2,1)}, u32[]{:S(2)}) copy-start(bf16[8,2,2,512]{3,2,1,0:T(2,128)(2,1)} %param.9) | copy-start | bytes 98308
  0.7 17.5 %copy-start.1 = (bf16[2,512,512]{2,1,0:T(8,128)(2,1)S(1)}, bf16[2,512,512]{2,1,0:T(8,128)(2,1)}, u32[]{:S(2)}) copy-start(bf16[2,512,512]{2,1,0:T(8,128)(2,1)} %refs_2_.3) | copy-start | bytes 3145732
  0.7 6.6 %collective-permute-start = (bf16[8,2,2,512]{3,2,1,0:T(2,128)(2,1)}, bf16[8,2,2,512]{3,2,1,0:T(2,128)(2,1)S(1)}, u32[]{:S(2)}, u32[]{:S(2)}) collective-permute-start(bf16[8,2,2,512]{3,2,1,0:T(2,128)(2,1)} %param.9), channel_id=1, source_target_pairs={{0,16},{4,20},{8,24},{12,28},{16,0},{20,4},{24,8},{28,12},{1,17},{... | collective-permute-start | bytes 98312 | tf_op jit(solution)/shard_map/ppermute | solution.py:48
  4.8 5.0 %collective-permute-start.1 = (bf16[8,2,2,512]{3,2,1,0:T(2,128)(2,1)}, bf16[8,2,2,512]{3,2,1,0:T(2,128)(2,1)S(1)}, u32[]{:S(2)}, u32[]{:S(2)}) collective-permute-start(bf16[8,2,2,512]{3,2,1,0:T(2,128)(2,1)} %param.8), channel_id=1, source_target_pairs={{0,16},{4,20},{8,24},{12,28},{16,0},{20,4},{24,8},{28,12},{1,17},{... | collective-permute-start | bytes 98312 | tf_op jit(solution)/shard_map/ppermute | solution.py:48
  7.3 2.6 %collective-permute-start.2 = (bf16[16,1024]{1,0:T(8,128)(2,1)S(1)}, bf16[16,1024]{1,0:T(8,128)(2,1)S(1)}, u32[]{:S(2)}, u32[]{:S(2)}) collective-permute-start(bf16[16,1024]{1,0:T(8,128)(2,1)S(1)} %get-tuple-element.25), channel_id=1, source_target_pairs={{0,1},{2,3},{1,0},{3,2},{4,5},{6,7},{5,4},{7,6},{8,9},{10,11},{9,8... | collective-permute-start | bytes 98312 | tf_op jit(solution)/shard_map/ppermute | solution.py:65
  7.4 2.5 %collective-permute-start.3 = (bf16[16,1024]{1,0:T(8,128)(2,1)S(1)}, bf16[16,1024]{1,0:T(8,128)(2,1)S(1)}, u32[]{:S(2)}, u32[]{:S(2)}) collective-permute-start(bf16[16,1024]{1,0:T(8,128)(2,1)S(1)} %get-tuple-element.24), channel_id=1, source_target_pairs={{1,2},{2,1},{5,6},{6,5},{9,10},{10,9},{13,14},{14,13},{17,18},{18,... | collective-permute-start | bytes 98312 | tf_op jit(solution)/shard_map/ppermute | solution.py:64
  9.8 3.8 %copy-start.4 = (f32[4]{0:T(128)S(1)}, f32[4]{0:T(128)}, u32[]{:S(2)}) copy-start(f32[4]{0:T(128)} %param.14) | copy-start | bytes 52
  9.8 3.8 %copy-start.5 = (s32[4]{0:T(128)S(1)}, s32[4]{0:T(128)}, u32[]{:S(2)}) copy-start(s32[4]{0:T(128)} %param.13) | copy-start | bytes 52
  10.0 3.9 %copy-start.3 = (s32[80,2]{0,1:T(2,128)S(1)}, s32[80,2]{0,1:T(2,128)}, u32[]{:S(2)}) copy-start(s32[80,2]{0,1:T(2,128)} %param.15) | copy-start | bytes 1924
  10.0 5.9 %collective-permute-start.4 = (bf16[16,4096]{1,0:T(8,128)(2,1)S(1)}, bf16[16,4096]{1,0:T(8,128)(2,1)S(1)}, u32[]{:S(2)}, u32[]{:S(2)}) collective-permute-start(bf16[16,4096]{1,0:T(8,128)(2,1)S(1)} %shard_map.95.refs_1_.refs_3_.refs_4_), channel_id=1, source_target_pairs={{0,12},{4,8},{8,4},{12,0},{16,28},{20,24},{24,20},{28,16},{1,13},{... | collective-permute-start | bytes 393224 | tf_op jit(solution)/shard_map/ppermute | solution.py:48
  12.6 5.5 %collective-permute-start.5 = (bf16[16,4096]{1,0:T(8,128)(2,1)S(1)}, bf16[16,4096]{1,0:T(8,128)(2,1)S(1)}, u32[]{:S(2)}, u32[]{:S(2)}) collective-permute-start(bf16[16,4096]{1,0:T(8,128)(2,1)S(1)} %shard_map.95.refs_1_.refs_3_.refs_4_), channel_id=1, source_target_pairs={{0,8},{4,12},{8,0},{12,4},{16,24},{20,28},{24,16},{28,20},{1,9},{5... | collective-permute-start | bytes 393224 | tf_op jit(solution)/shard_map/ppermute | solution.py:48
  13.1 6.8 %collective-permute-start.6 = (bf16[16,4096]{1,0:T(8,128)(2,1)S(1)}, bf16[16,4096]{1,0:T(8,128)(2,1)S(1)}, u32[]{:S(2)}, u32[]{:S(2)}) collective-permute-start(bf16[16,4096]{1,0:T(8,128)(2,1)S(1)} %shard_map.95.refs_1_.refs_3_.refs_4_), channel_id=1, source_target_pairs={{0,4},{4,0},{8,12},{12,8},{16,20},{20,16},{24,28},{28,24},{1,5},{5... | collective-permute-start | bytes 393224 | tf_op jit(solution)/shard_map/ppermute | solution.py:48
  20.5 3.6 %collective-permute-start.7 = (f32[64,128]{1,0:T(8,128)S(1)}, f32[64,128]{1,0:T(8,128)S(1)}, u32[]{:S(2)}, u32[]{:S(2)}) collective-permute-start(f32[64,128]{1,0:T(8,128)S(1)} %get-tuple-element.23.refs_5_), channel_id=1, source_target_pairs={{0,3},{1,2},{2,1},{3,0},{4,7},{5,6},{6,5},{7,4},{8,11},{9,10},{10,... | collective-permute-start | bytes 98312 | tf_op jit(solution)/shard_map/ppermute | solution.py:48
  20.6 4.9 %collective-permute-start.8 = (f32[64,128]{1,0:T(8,128)S(1)}, f32[64,128]{1,0:T(8,128)S(1)}, u32[]{:S(2)}, u32[]{:S(2)}) collective-permute-start(f32[64,128]{1,0:T(8,128)S(1)} %get-tuple-element.23.refs_5_), channel_id=1, source_target_pairs={{0,2},{1,3},{2,0},{3,1},{4,6},{5,7},{6,4},{7,5},{8,10},{9,11},{10,... | collective-permute-start | bytes 98312 | tf_op jit(solution)/shard_map/ppermute | solution.py:48
  23.3 2.2 %collective-permute-start.9 = (f32[64,128]{1,0:T(8,128)S(1)}, f32[64,128]{1,0:T(8,128)S(1)}, u32[]{:S(2)}, u32[]{:S(2)}) collective-permute-start(f32[64,128]{1,0:T(8,128)S(1)} %get-tuple-element.23.refs_5_), channel_id=1, source_target_pairs={{0,1},{1,0},{2,3},{3,2},{4,5},{5,4},{6,7},{7,6},{8,9},{9,8},{10,11... | collective-permute-start | bytes 98312 | tf_op jit(solution)/shard_map/ppermute | solution.py:48

commit v9 on v7

--- a/solution.py
+++ b/solution.py
@@ -69,7 +69,7 @@
 def rounds_of(peers):
     bits = [1 << k for k in reversed(range(peers.bit_length() - 1))]
     head, tail = bits[:-2], bits[-2:]
-    last = [tail[0] ^ tail[1], tail[0], tail[1]] if len(tail) == 2 else tail
+    last = [tail[1], tail[0] ^ tail[1], tail[0]] if len(tail) == 2 else tail
     return head, last
 
 
@@ -284,7 +284,7 @@
     )
     order = (numbers[:, None] == places[None, :]).astype(BF16)
 
-    early = len(pieces) - 1
+    early = (len(pieces) + 1) // 2
     late = len(pieces) - early
     early_total, late_total = early * both.shape[0], late * both.shape[0]
     early_masked, early_spread = local_call(

time: 26.9 us -> 26.9 us (level)
  waiting for transfers between devices: 9.37 us -> 8.16 us
  starting transfers between devices: 11.3 us -> 12 us
  local copies, waits for them, and re-layouts: 0.89 us -> 1.53 us
    ppermute x8, waiting for transfers between devices: 9.36 us -> 8.15 us  [swapped(): return lax.ppermute(values, axis, [(i, i ^ distance) for i in range(peers)])]
    ppermute x8, starting transfers between devices: 10.6 us -> 11.2 us  [swapped(): return lax.ppermute(values, axis, [(i, i ^ distance) for i in range(peers)])]
    unnamed x12, local copies, waits for them, and re-layouts: 0.04 us -> 0.68 us
  transfers between devices with their start and end apart: 10 -> 10, of which waited for: 6 -> 6; matrix products, arithmetic and copies ran while one was open for 9% -> 8% of each run, Pallas kernels for 3% -> 3%
where the time goes in v9:
time: 26.9 us; the launch traced here: 26.5 us
  starting transfers between devices  12 us (45%)
  waiting for transfers between devices  8.16 us (30%)
  Pallas kernels  2.62 us (10%)
  local copies, waits for them, and re-layouts  1.53 us (6%)
  between operations  0.83 us (3%)
  other arithmetic  0.82 us (3%)
  matrix products  0.59 us (2%)
    ppermute x8, starting transfers between devices, swapped(): return lax.ppermute(values, axis, [(i, i ^ distance) for i in range(peers)])  11.2 us
    ppermute x8, waiting for transfers between devices, swapped(): return lax.ppermute(values, axis, [(i, i ^ distance) for i in range(peers)])  8.15 us
    pallas_call x5, Pallas kernels, local_call(): pl.pallas_call(kernel, out_shape=tuple(outs), in_specs=[pl.BlockSpec(memo...  2.62 us
    transpose x4, local copies, waits for them, and re-layouts, body(): fields.transpose(0, 2, 1, 3).reshape(fields.shape[0], 2 * half)  0.8 us
    pad x1, other arithmetic, body(): jnp.pad(taps, ((0, 5), (0, 125)))  0.69 us
    unnamed x12, local copies, waits for them, and re-layouts  0.68 us
    ppermute x1, starting transfers between devices, neighbour_rows(): lax.ppermute(jnp.where(odd, last, first), 'row', pairs_of(peers, 1))  0.66 us
  transfers between devices with their start and end apart: 10, of which 6 were waited for; matrix products, arithmetic and copies ran while one was open for 8% of the time, Pallas kernels for 3%

profile of v9, /device:TPU:0, one launch (start us, length us, event | category | flops | bytes accessed | tf_op | source)
XLA Modules:
  0.0 26.5 jit_solution(9623813196033147600)
XLA Ops:
  0.7 4.1 %collective-permute-start.1 = (bf16[8,2,2,512]{3,2,1,0:T(2,128)(2,1)}, bf16[8,2,2,512]{3,2,1,0:T(2,128)(2,1)S(1)}, u32[]{:S(2)}, u32[]{:S(2)}) collective-permute-start(bf16[8,2,2,512]{3,2,1,0:T(2,128)(2,1)} %param.9), channel_id=1, source_target_pairs={{0,16},{4,20},{8,24},{12,28},{16,0},{20,4},{24,8},{28,12},{1,17},{... | collective-permute-start | bytes 98312 | tf_op jit(solution)/shard_map/ppermute | solution.py:48
  4.8 0.1 collective-permute-start
  4.9 0.1 fusion.8.refs_1_
  4.9 0.7 %select_select_fusion.refs_0_ = f32[8,128]{1,0:T(8,128)S(1)} fusion(f32[2,3]{1,0:T(2,128)} %param.11, f32[]{:T(128)S(6)} %convert_element_type.6), kind=kLoop, calls=%fused_computation.30 | loop fusion | flops 5120 | bytes 4124 | tf_op jit(solution)/shard_map/jit(_pad)/pad | solution.py:259
  5.6 0.8 %copy.10 = bf16[8,2,2,512]{3,0,2,1:T(8,128)(2,1)S(1)} copy(bf16[8,2,2,512]{3,1,2,0:T(2,128)(2,1)} %bitcast.26) | data formatting | bytes 65536 | tf_op jit(solution)/shard_map/transpose | solution.py:240
  6.4 0.8 %collective-permute-done.1 = bf16[8,2,2,512]{3,2,1,0:T(2,128)(2,1)S(1)} collective-permute-done((bf16[8,2,2,512]{3,2,1,0:T(2,128)(2,1)}, bf16[8,2,2,512]{3,2,1,0:T(2,128)(2,1)S(1)}, u32[]{:S(2)}, u32[]{:S(2)}) %collective-permute-start.1) | collective-permute-done | bytes 32800 | tf_op jit(solution)/shard_map/ppermute | solution.py:48
  7.4 0.7 %collective-permute-start.3 = (bf16[16,1024]{1,0:T(8,128)(2,1)S(1)}, bf16[16,1024]{1,0:T(8,128)(2,1)S(1)}, u32[]{:S(2)}, u32[]{:S(2)}) collective-permute-start(bf16[16,1024]{1,0:T(8,128)(2,1)S(1)} %get-tuple-element.20), channel_id=1, source_target_pairs={{1,2},{2,1},{5,6},{6,5},{9,10},{10,9},{13,14},{14,13},{17,18},{18,... | collective-permute-start | bytes 98312 | tf_op jit(solution)/shard_map/ppermute | solution.py:64
  8.0 1.8 %collective-permute-done = bf16[8,2,2,512]{3,2,1,0:T(2,128)(2,1)S(1)} collective-permute-done((bf16[8,2,2,512]{3,2,1,0:T(2,128)(2,1)}, bf16[8,2,2,512]{3,2,1,0:T(2,128)(2,1)S(1)}, u32[]{:S(2)}, u32[]{:S(2)}) %collective-permute-start) | collective-permute-done | bytes 32800 | tf_op jit(solution)/shard_map/ppermute | solution.py:48
  9.9 0.1 shard_map.95.refs_1_.refs_3_.refs_4_
  10.0 1.6 %collective-permute-start.4 = (bf16[16,4096]{1,0:T(8,128)(2,1)S(1)}, bf16[16,4096]{1,0:T(8,128)(2,1)S(1)}, u32[]{:S(2)}, u32[]{:S(2)}) collective-permute-start(bf16[16,4096]{1,0:T(8,128)(2,1)S(1)} %shard_map.95.refs_1_.refs_3_.refs_4_), channel_id=1, source_target_pairs={{0,4},{4,0},{8,12},{12,8},{16,20},{20,16},{24,28},{28,24},{1,5},{5... | collective-permute-start | bytes 393224 | tf_op jit(solution)/shard_map/ppermute | solution.py:48
  11.6 1.5 %collective-permute-start.5 = (bf16[16,4096]{1,0:T(8,128)(2,1)S(1)}, bf16[16,4096]{1,0:T(8,128)(2,1)S(1)}, u32[]{:S(2)}, u32[]{:S(2)}) collective-permute-start(bf16[16,4096]{1,0:T(8,128)(2,1)S(1)} %shard_map.95.refs_1_.refs_3_.refs_4_), channel_id=1, source_target_pairs={{0,12},{4,8},{8,4},{12,0},{16,28},{20,24},{24,20},{28,16},{1,13},{... | collective-permute-start | bytes 393224 | tf_op jit(solution)/shard_map/ppermute | solution.py:48
  13.1 0.4 %collective-permute-start.6 = (bf16[16,4096]{1,0:T(8,128)(2,1)S(1)}, bf16[16,4096]{1,0:T(8,128)(2,1)S(1)}, u32[]{:S(2)}, u32[]{:S(2)}) collective-permute-start(bf16[16,4096]{1,0:T(8,128)(2,1)S(1)} %shard_map.95.refs_1_.refs_3_.refs_4_), channel_id=1, source_target_pairs={{0,8},{4,12},{8,0},{12,4},{16,24},{20,28},{24,16},{28,20},{1,9},{5... | collective-permute-start | bytes 393224 | tf_op jit(solution)/shard_map/ppermute | solution.py:48
  13.6 0.3 %fusion.31 = (f32[4,2,512]{2,0,1:T(4,128)S(1)}, f32[4,2,512]{2,0,1:T(4,128)S(1)}) fusion(f32[4]{0:T(128)S(1)} %copy-done.4, f32[7,2,512]{2,1,0:T(2,128)S(1)} %copy-done, s32[4]{0:T(128)S(1)} %copy-done.5), kind=kOutput, calls=%fused_computation.73 | convolution fusion | flops 348188 | bytes 61472 | tf_op jit(solution)/shard_map/wp,prc->wrc/dot_general | solution.py:269
  14.0 0.6 %copy-done.3 = s32[80,2]{0,1:T(2,128)S(1)} copy-done((s32[80,2]{0,1:T(2,128)S(1)}, s32[80,2]{0,1:T(2,128)}, u32[]{:S(2)}) %copy-start.3) | copy-done | bytes 664
  14.7 0.4 %collective-permute-done.4.refs_2_.refs_4_.refs_5_ = bf16[16,4096]{1,0:T(8,128)(2,1)S(1)} collective-permute-done((bf16[16,4096]{1,0:T(8,128)(2,1)S(1)}, bf16[16,4096]{1,0:T(8,128)(2,1)S(1)}, u32[]{:S(2)}, u32[]{:S(2)}) %collective-permute-start.4) | collective-permute-done | bytes 131104 | tf_op jit(solution)/shard_map/ppermute | solution.py:48
  15.1 0.3 %shard_map.97 = (bf16[64,1024]{1,0:T(8,128)(2,1)S(1)}, bf16[64,1024]{1,0:T(8,128)(2,1)S(1)}) custom-call(f32[8,1024]{1,0:T(8,128)S(1)} %tile.9.refs_0_, f32[8,1024]{1,0:T(8,128)S(1)} %tile.21.refs_1_, bf16[2,512,512]{2,1,0:T(8,128)(2,1)S(1)} %copy-done.1, bf16[16,4096]{1,0:T(8,128)(2,1)S(1)} %shard_map.95.refs_1_.refs_3_.refs_4_, ...), custom_call_target="tpu_custom_call" | custom-call | flops 134217728 | bytes 1638400 | tf_op jit(solution)/shard_map/pallas_call | solution.py:32
  15.4 2.2 %collective-permute-done.5.refs_3_.refs_6_ = bf16[16,4096]{1,0:T(8,128)(2,1)S(1)} collective-permute-done((bf16[16,4096]{1,0:T(8,128)(2,1)S(1)}, bf16[16,4096]{1,0:T(8,128)(2,1)S(1)}, u32[]{:S(2)}, u32[]{:S(2)}) %collective-permute-start.5) | collective-permute-done | bytes 131104 | tf_op jit(solution)/shard_map/ppermute | solution.py:48
  17.6 1.6 %collective-permute-done.6.refs_4_.refs_7_ = bf16[16,4096]{1,0:T(8,128)(2,1)S(1)} collective-permute-done((bf16[16,4096]{1,0:T(8,128)(2,1)S(1)}, bf16[16,4096]{1,0:T(8,128)(2,1)S(1)}, u32[]{:S(2)}, u32[]{:S(2)}) %collective-permute-start.6) | collective-permute-done | bytes 131104 | tf_op jit(solution)/shard_map/ppermute | solution.py:48
  19.2 0.7 %shard_map.98 = (bf16[64,1024]{1,0:T(8,128)(2,1)S(1)}, f32[64,128]{1,0:T(8,128)S(1)}) custom-call(f32[8,1024]{1,0:T(8,128)S(1)} %tile.9.refs_0_, f32[8,1024]{1,0:T(8,128)S(1)} %tile.21.refs_1_, bf16[2,512,512]{2,1,0:T(8,128)(2,1)S(1)} %copy-done.1, bf16[64,1024]{1,0:T(8,128)(2,1)S(1)} %get-tuple-element.17.refs_3_, ...), custom_call_target="tpu_custom_call" | custom-call | flops 167772160 | bytes 1933312 | tf_op jit(solution)/shard_map/pallas_call | solution.py:32
  19.9 3.4 %collective-permute-start.8 = (f32[64,128]{1,0:T(8,128)S(1)}, f32[64,128]{1,0:T(8,128)S(1)}, u32[]{:S(2)}, u32[]{:S(2)}) collective-permute-start(f32[64,128]{1,0:T(8,128)S(1)} %get-tuple-element.19.refs_5_), channel_id=1, source_target_pairs={{0,2},{1,3},{2,0},{3,1},{4,6},{5,7},{6,4},{7,5},{8,10},{9,11},{10,... | collective-permute-start | bytes 98312 | tf_op jit(solution)/shard_map/ppermute | solution.py:48
  23.4 0.3 fusion.refs_0_
  23.6 0.5 %shard_map.96.refs_2_ = bf16[128,1024]{1,0:T(8,128)(2,1)S(1)} custom-call(bf16[2,512,512]{2,1,0:T(8,128)(2,1)S(1)} %copy-done.1, bf16[16,4096]{1,0:T(8,128)(2,1)S(1)} %shard_map.95.refs_1_.refs_3_.refs_4_, bf16[16,4096]{1,0:T(8,128)(2,1)S(1)} %collective-permute-done.4.refs_2_.refs_4_.refs_5_, bf16[16,4096]{1,0:T(8,128)(2,1)S(1)} %collective-permute-done.5.refs_3_.refs_6_, ...), custom_call_target="tpu_custom_call" | custom-call | flops 268435456 | bytes 1835008 | tf_op jit(solution)/shard_map/pallas_call | solution.py:32
  24.1 1.4 %collective-permute-done.8.refs_7_ = f32[64,128]{1,0:T(8,128)S(1)} collective-permute-done((f32[64,128]{1,0:T(8,128)S(1)}, f32[64,128]{1,0:T(8,128)S(1)}, u32[]{:S(2)}, u32[]{:S(2)}) %collective-permute-start.8) | collective-permute-done | bytes 32800 | tf_op jit(solution)/shard_map/ppermute | solution.py:48
  25.5 1.0 %shard_map.99 = (f32[2,8,64]{2,1,0:T(8,128)}, f32[4,2,512]{2,1,0:T(2,128)}) custom-call(f32[64,64]{1,0:T(8,128)S(1)} %fusion.refs_0_, bf16[64,64]{1,0:T(8,128)(2,1)S(1)} %fusion.8.refs_1_, bf16[128,1024]{1,0:T(8,128)(2,1)S(1)} %shard_map.96.refs_2_, bf16[64,1024]{1,0:T(8,128)(2,1)S(1)} %get-tuple-element.16.refs_3_, ...), custom_call_target="tpu_custom_call" | custom-call | flops 33554432 | bytes 700416 | tf_op jit(solution)/shard_map/pallas_call | solution.py:32
  (30 shorter events, 0.4 us)
Async XLA Ops:
  0.6 13.0 %copy-start = (f32[7,2,512]{2,1,0:T(2,128)S(1)}, f32[7,2,512]{2,1,0:T(2,128)}, u32[]{:S(2)}) copy-start(f32[7,2,512]{2,1,0:T(2,128)} %param.12) | copy-start | bytes 86020
  0.6 5.0 %copy-start.2 = (bf16[8,2,2,512]{3,2,1,0:T(2,128)(2,1)S(1)}, bf16[8,2,2,512]{3,2,1,0:T(2,128)(2,1)}, u32[]{:S(2)}) copy-start(bf16[8,2,2,512]{3,2,1,0:T(2,128)(2,1)} %param.9) | copy-start | bytes 98308
  0.7 14.4 %copy-start.1 = (bf16[2,512,512]{2,1,0:T(8,128)(2,1)S(1)}, bf16[2,512,512]{2,1,0:T(8,128)(2,1)}, u32[]{:S(2)}) copy-start(bf16[2,512,512]{2,1,0:T(8,128)(2,1)} %refs_2_.3) | copy-start | bytes 3145732
  0.7 6.6 %collective-permute-start.1 = (bf16[8,2,2,512]{3,2,1,0:T(2,128)(2,1)}, bf16[8,2,2,512]{3,2,1,0:T(2,128)(2,1)S(1)}, u32[]{:S(2)}, u32[]{:S(2)}) collective-permute-start(bf16[8,2,2,512]{3,2,1,0:T(2,128)(2,1)} %param.9), channel_id=1, source_target_pairs={{0,16},{4,20},{8,24},{12,28},{16,0},{20,4},{24,8},{28,12},{1,17},{... | collective-permute-start | bytes 98312 | tf_op jit(solution)/shard_map/ppermute | solution.py:48
  4.8 5.0 %collective-permute-start = (bf16[8,2,2,512]{3,2,1,0:T(2,128)(2,1)}, bf16[8,2,2,512]{3,2,1,0:T(2,128)(2,1)S(1)}, u32[]{:S(2)}, u32[]{:S(2)}) collective-permute-start(bf16[8,2,2,512]{3,2,1,0:T(2,128)(2,1)} %param.8), channel_id=1, source_target_pairs={{0,16},{4,20},{8,24},{12,28},{16,0},{20,4},{24,8},{28,12},{1,17},{... | collective-permute-start | bytes 98312 | tf_op jit(solution)/shard_map/ppermute | solution.py:48
  7.3 2.6 %collective-permute-start.2 = (bf16[16,1024]{1,0:T(8,128)(2,1)S(1)}, bf16[16,1024]{1,0:T(8,128)(2,1)S(1)}, u32[]{:S(2)}, u32[]{:S(2)}) collective-permute-start(bf16[16,1024]{1,0:T(8,128)(2,1)S(1)} %get-tuple-element.21), channel_id=1, source_target_pairs={{0,1},{2,3},{1,0},{3,2},{4,5},{6,7},{5,4},{7,6},{8,9},{10,11},{9,8... | collective-permute-start | bytes 98312 | tf_op jit(solution)/shard_map/ppermute | solution.py:65
  7.4 2.5 %collective-permute-start.3 = (bf16[16,1024]{1,0:T(8,128)(2,1)S(1)}, bf16[16,1024]{1,0:T(8,128)(2,1)S(1)}, u32[]{:S(2)}, u32[]{:S(2)}) collective-permute-start(bf16[16,1024]{1,0:T(8,128)(2,1)S(1)} %get-tuple-element.20), channel_id=1, source_target_pairs={{1,2},{2,1},{5,6},{6,5},{9,10},{10,9},{13,14},{14,13},{17,18},{18,... | collective-permute-start | bytes 98312 | tf_op jit(solution)/shard_map/ppermute | solution.py:64
  9.8 3.7 %copy-start.4 = (f32[4]{0:T(128)S(1)}, f32[4]{0:T(128)}, u32[]{:S(2)}) copy-start(f32[4]{0:T(128)} %param.14) | copy-start | bytes 52
  9.9 3.7 %copy-start.5 = (s32[4]{0:T(128)S(1)}, s32[4]{0:T(128)}, u32[]{:S(2)}) copy-start(s32[4]{0:T(128)} %param.13) | copy-start | bytes 52
  10.0 5.0 %collective-permute-start.4 = (bf16[16,4096]{1,0:T(8,128)(2,1)S(1)}, bf16[16,4096]{1,0:T(8,128)(2,1)S(1)}, u32[]{:S(2)}, u32[]{:S(2)}) collective-permute-start(bf16[16,4096]{1,0:T(8,128)(2,1)S(1)} %shard_map.95.refs_1_.refs_3_.refs_4_), channel_id=1, source_target_pairs={{0,4},{4,0},{8,12},{12,8},{16,20},{20,16},{24,28},{28,24},{1,5},{5... | collective-permute-start | bytes 393224 | tf_op jit(solution)/shard_map/ppermute | solution.py:48
  11.6 6.0 %collective-permute-start.5 = (bf16[16,4096]{1,0:T(8,128)(2,1)S(1)}, bf16[16,4096]{1,0:T(8,128)(2,1)S(1)}, u32[]{:S(2)}, u32[]{:S(2)}) collective-permute-start(bf16[16,4096]{1,0:T(8,128)(2,1)S(1)} %shard_map.95.refs_1_.refs_3_.refs_4_), channel_id=1, source_target_pairs={{0,12},{4,8},{8,4},{12,0},{16,28},{20,24},{24,20},{28,16},{1,13},{... | collective-permute-start | bytes 393224 | tf_op jit(solution)/shard_map/ppermute | solution.py:48
  13.1 6.0 %collective-permute-start.6 = (bf16[16,4096]{1,0:T(8,128)(2,1)S(1)}, bf16[16,4096]{1,0:T(8,128)(2,1)S(1)}, u32[]{:S(2)}, u32[]{:S(2)}) collective-permute-start(bf16[16,4096]{1,0:T(8,128)(2,1)S(1)} %shard_map.95.refs_1_.refs_3_.refs_4_), channel_id=1, source_target_pairs={{0,8},{4,12},{8,0},{12,4},{16,24},{20,28},{24,16},{28,20},{1,9},{5... | collective-permute-start | bytes 393224 | tf_op jit(solution)/shard_map/ppermute | solution.py:48
  14.0 0.7 %copy-start.3 = (s32[80,2]{0,1:T(2,128)S(1)}, s32[80,2]{0,1:T(2,128)}, u32[]{:S(2)}) copy-start(s32[80,2]{0,1:T(2,128)} %param.15) | copy-start | bytes 1924
  19.9 4.2 %collective-permute-start.7 = (f32[64,128]{1,0:T(8,128)S(1)}, f32[64,128]{1,0:T(8,128)S(1)}, u32[]{:S(2)}, u32[]{:S(2)}) collective-permute-start(f32[64,128]{1,0:T(8,128)S(1)} %get-tuple-element.19.refs_5_), channel_id=1, source_target_pairs={{0,3},{1,2},{2,1},{3,0},{4,7},{5,6},{6,5},{7,4},{8,11},{9,10},{10,... | collective-permute-start | bytes 98312 | tf_op jit(solution)/shard_map/ppermute | solution.py:48
  19.9 5.5 %collective-permute-start.8 = (f32[64,128]{1,0:T(8,128)S(1)}, f32[64,128]{1,0:T(8,128)S(1)}, u32[]{:S(2)}, u32[]{:S(2)}) collective-permute-start(f32[64,128]{1,0:T(8,128)S(1)} %get-tuple-element.19.refs_5_), channel_id=1, source_target_pairs={{0,2},{1,3},{2,0},{3,1},{4,6},{5,7},{6,4},{7,5},{8,10},{9,11},{10,... | collective-permute-start | bytes 98312 | tf_op jit(solution)/shard_map/ppermute | solution.py:48
  23.3 2.2 %collective-permute-start.9 = (f32[64,128]{1,0:T(8,128)S(1)}, f32[64,128]{1,0:T(8,128)S(1)}, u32[]{:S(2)}, u32[]{:S(2)}) collective-permute-start(f32[64,128]{1,0:T(8,128)S(1)} %get-tuple-element.19.refs_5_), channel_id=1, source_target_pairs={{0,1},{1,0},{2,3},{3,2},{4,5},{5,4},{6,7},{7,6},{8,9},{9,8},{10,11... | collective-permute-start | bytes 98312 | tf_op jit(solution)/shard_map/ppermute | solution.py:48

commit v10 on v7

--- a/solution.py
+++ b/solution.py
@@ -69,7 +69,7 @@
 def rounds_of(peers):
     bits = [1 << k for k in reversed(range(peers.bit_length() - 1))]
     head, tail = bits[:-2], bits[-2:]
-    last = [tail[0] ^ tail[1], tail[0], tail[1]] if len(tail) == 2 else tail
+    last = [tail[0] ^ tail[1], tail[1], tail[0]] if len(tail) == 2 else tail
     return head, last
 
 

time: 26.9 us -> 26.9 us (level)
  transfers between devices with their start and end apart: 10 -> 10, of which waited for: 6 -> 5; matrix products, arithmetic and copies ran while one was open for 9% -> 9% of each run, Pallas kernels for 3% -> 3%
where the time goes in v10:
time: 26.9 us; the launch traced here: 26.5 us
  starting transfers between devices  11.4 us (42%)
  waiting for transfers between devices  9.27 us (34%)
  Pallas kernels  2.7 us (10%)
  local copies, waits for them, and re-layouts  0.89 us (3%)
  between operations  0.85 us (3%)
  other arithmetic  0.82 us (3%)
  matrix products  0.59 us (2%)
    ppermute x8, starting transfers between devices, swapped(): return lax.ppermute(values, axis, [(i, i ^ distance) for i in range(peers)])  10.7 us
    ppermute x8, waiting for transfers between devices, swapped(): return lax.ppermute(values, axis, [(i, i ^ distance) for i in range(peers)])  9.27 us
    pallas_call x5, Pallas kernels, local_call(): pl.pallas_call(kernel, out_shape=tuple(outs), in_specs=[pl.BlockSpec(memo...  2.7 us
    transpose x4, local copies, waits for them, and re-layouts, body(): fields.transpose(0, 2, 1, 3).reshape(fields.shape[0], 2 * half)  0.8 us
    pad x1, other arithmetic, body(): jnp.pad(taps, ((0, 5), (0, 125)))  0.69 us
    ppermute x1, starting transfers between devices, neighbour_rows(): lax.ppermute(jnp.where(odd, last, first), 'row', pairs_of(peers, 1))  0.66 us
  transfers between devices with their start and end apart: 10, of which 5 were waited for; matrix products, arithmetic and copies ran while one was open for 9% of the time, Pallas kernels for 3%

profile of v10, /device:TPU:0, one launch (start us, length us, event | category | flops | bytes accessed | tf_op | source)
XLA Modules:
  0.0 26.5 jit_solution(11995326084068537348)
XLA Ops:
  0.7 4.1 %collective-permute-start.1 = (bf16[8,2,2,512]{3,2,1,0:T(2,128)(2,1)}, bf16[8,2,2,512]{3,2,1,0:T(2,128)(2,1)S(1)}, u32[]{:S(2)}, u32[]{:S(2)}) collective-permute-start(bf16[8,2,2,512]{3,2,1,0:T(2,128)(2,1)} %param.9), channel_id=1, source_target_pairs={{0,16},{4,20},{8,24},{12,28},{16,0},{20,4},{24,8},{28,12},{1,17},{... | collective-permute-start | bytes 98312 | tf_op jit(solution)/shard_map/ppermute | solution.py:48
  4.8 0.1 collective-permute-start
  4.9 0.1 fusion.8.refs_1_
  4.9 0.7 %select_select_fusion.refs_0_ = f32[8,128]{1,0:T(8,128)S(1)} fusion(f32[2,3]{1,0:T(2,128)} %param.11, f32[]{:T(128)S(6)} %convert_element_type.6), kind=kLoop, calls=%fused_computation.30 | loop fusion | flops 5120 | bytes 4124 | tf_op jit(solution)/shard_map/jit(_pad)/pad | solution.py:259
  5.6 0.8 %copy.10 = bf16[8,2,2,512]{3,0,2,1:T(8,128)(2,1)S(1)} copy(bf16[8,2,2,512]{3,1,2,0:T(2,128)(2,1)} %bitcast.26) | data formatting | bytes 65536 | tf_op jit(solution)/shard_map/transpose | solution.py:240
  6.4 0.8 %collective-permute-done.1 = bf16[8,2,2,512]{3,2,1,0:T(2,128)(2,1)S(1)} collective-permute-done((bf16[8,2,2,512]{3,2,1,0:T(2,128)(2,1)}, bf16[8,2,2,512]{3,2,1,0:T(2,128)(2,1)S(1)}, u32[]{:S(2)}, u32[]{:S(2)}) %collective-permute-start.1) | collective-permute-done | bytes 32800 | tf_op jit(solution)/shard_map/ppermute | solution.py:48
  7.3 0.1 collective-permute-start.2
  7.4 0.7 %collective-permute-start.3 = (bf16[16,1024]{1,0:T(8,128)(2,1)S(1)}, bf16[16,1024]{1,0:T(8,128)(2,1)S(1)}, u32[]{:S(2)}, u32[]{:S(2)}) collective-permute-start(bf16[16,1024]{1,0:T(8,128)(2,1)S(1)} %get-tuple-element.20), channel_id=1, source_target_pairs={{1,2},{2,1},{5,6},{6,5},{9,10},{10,9},{13,14},{14,13},{17,18},{18,... | collective-permute-start | bytes 98312 | tf_op jit(solution)/shard_map/ppermute | solution.py:64
  8.0 1.8 %collective-permute-done = bf16[8,2,2,512]{3,2,1,0:T(2,128)(2,1)S(1)} collective-permute-done((bf16[8,2,2,512]{3,2,1,0:T(2,128)(2,1)}, bf16[8,2,2,512]{3,2,1,0:T(2,128)(2,1)S(1)}, u32[]{:S(2)}, u32[]{:S(2)}) %collective-permute-start) | collective-permute-done | bytes 32800 | tf_op jit(solution)/shard_map/ppermute | solution.py:48
  9.9 0.1 shard_map.95.refs_1_.refs_3_.refs_4_
  10.0 2.6 %collective-permute-start.4 = (bf16[16,4096]{1,0:T(8,128)(2,1)S(1)}, bf16[16,4096]{1,0:T(8,128)(2,1)S(1)}, u32[]{:S(2)}, u32[]{:S(2)}) collective-permute-start(bf16[16,4096]{1,0:T(8,128)(2,1)S(1)} %shard_map.95.refs_1_.refs_3_.refs_4_), channel_id=1, source_target_pairs={{0,12},{4,8},{8,4},{12,0},{16,28},{20,24},{24,20},{28,16},{1,13},{... | collective-permute-start | bytes 393224 | tf_op jit(solution)/shard_map/ppermute | solution.py:48
  12.6 0.5 %collective-permute-start.5 = (bf16[16,4096]{1,0:T(8,128)(2,1)S(1)}, bf16[16,4096]{1,0:T(8,128)(2,1)S(1)}, u32[]{:S(2)}, u32[]{:S(2)}) collective-permute-start(bf16[16,4096]{1,0:T(8,128)(2,1)S(1)} %shard_map.95.refs_1_.refs_3_.refs_4_), channel_id=1, source_target_pairs={{0,4},{4,0},{8,12},{12,8},{16,20},{20,16},{24,28},{28,24},{1,5},{5... | collective-permute-start | bytes 393224 | tf_op jit(solution)/shard_map/ppermute | solution.py:48
  13.1 0.4 %collective-permute-start.6 = (bf16[16,4096]{1,0:T(8,128)(2,1)S(1)}, bf16[16,4096]{1,0:T(8,128)(2,1)S(1)}, u32[]{:S(2)}, u32[]{:S(2)}) collective-permute-start(bf16[16,4096]{1,0:T(8,128)(2,1)S(1)} %shard_map.95.refs_1_.refs_3_.refs_4_), channel_id=1, source_target_pairs={{0,8},{4,12},{8,0},{12,4},{16,24},{20,28},{24,16},{28,20},{1,9},{5... | collective-permute-start | bytes 393224 | tf_op jit(solution)/shard_map/ppermute | solution.py:48
  13.6 0.3 %fusion.31 = (f32[4,2,512]{2,0,1:T(4,128)S(1)}, f32[4,2,512]{2,0,1:T(4,128)S(1)}) fusion(f32[4]{0:T(128)S(1)} %copy-done.4, f32[7,2,512]{2,1,0:T(2,128)S(1)} %copy-done, s32[4]{0:T(128)S(1)} %copy-done.5), kind=kOutput, calls=%fused_computation.73 | convolution fusion | flops 348188 | bytes 61472 | tf_op jit(solution)/shard_map/wp,prc->wrc/dot_general | solution.py:269
  14.0 1.9 %collective-permute-done.4.refs_2_.refs_4_.refs_5_ = bf16[16,4096]{1,0:T(8,128)(2,1)S(1)} collective-permute-done((bf16[16,4096]{1,0:T(8,128)(2,1)S(1)}, bf16[16,4096]{1,0:T(8,128)(2,1)S(1)}, u32[]{:S(2)}, u32[]{:S(2)}) %collective-permute-start.4) | collective-permute-done | bytes 131104 | tf_op jit(solution)/shard_map/ppermute | solution.py:48
  16.0 3.4 %collective-permute-done.5.refs_3_.refs_5_.refs_6_ = bf16[16,4096]{1,0:T(8,128)(2,1)S(1)} collective-permute-done((bf16[16,4096]{1,0:T(8,128)(2,1)S(1)}, bf16[16,4096]{1,0:T(8,128)(2,1)S(1)}, u32[]{:S(2)}, u32[]{:S(2)}) %collective-permute-start.5) | collective-permute-done | bytes 131104 | tf_op jit(solution)/shard_map/ppermute | solution.py:48
  19.3 0.4 %shard_map.97 = (bf16[96,1024]{1,0:T(8,128)(2,1)S(1)}, bf16[96,1024]{1,0:T(8,128)(2,1)S(1)}) custom-call(f32[8,1024]{1,0:T(8,128)S(1)} %tile.9.refs_0_, f32[8,1024]{1,0:T(8,128)S(1)} %tile.21.refs_1_, bf16[2,512,512]{2,1,0:T(8,128)(2,1)S(1)} %copy-done.1, bf16[16,4096]{1,0:T(8,128)(2,1)S(1)} %shard_map.95.refs_1_.refs_3_.refs_4_, ...), custom_call_target="tpu_custom_call" | custom-call | flops 201326592 | bytes 1900544 | tf_op jit(solution)/shard_map/pallas_call | solution.py:32
  19.7 0.7 %shard_map.98 = (bf16[32,1024]{1,0:T(8,128)(2,1)S(1)}, f32[64,128]{1,0:T(8,128)S(1)}) custom-call(f32[8,1024]{1,0:T(8,128)S(1)} %tile.9.refs_0_, f32[8,1024]{1,0:T(8,128)S(1)} %tile.21.refs_1_, bf16[2,512,512]{2,1,0:T(8,128)(2,1)S(1)} %copy-done.1, bf16[96,1024]{1,0:T(8,128)(2,1)S(1)} %get-tuple-element.17.refs_3_, ...), custom_call_target="tpu_custom_call" | custom-call | flops 100663296 | bytes 1933312 | tf_op jit(solution)/shard_map/pallas_call | solution.py:32
  20.4 0.1 collective-permute-start.7
  20.5 2.8 %collective-permute-start.8 = (f32[64,128]{1,0:T(8,128)S(1)}, f32[64,128]{1,0:T(8,128)S(1)}, u32[]{:S(2)}, u32[]{:S(2)}) collective-permute-start(f32[64,128]{1,0:T(8,128)S(1)} %get-tuple-element.19.refs_5_), channel_id=1, source_target_pairs={{0,2},{1,3},{2,0},{3,1},{4,6},{5,7},{6,4},{7,5},{8,10},{9,11},{10,... | collective-permute-start | bytes 98312 | tf_op jit(solution)/shard_map/ppermute | solution.py:48
  23.4 0.3 fusion.refs_0_
  23.6 0.5 %shard_map.96.refs_2_ = bf16[128,1024]{1,0:T(8,128)(2,1)S(1)} custom-call(bf16[2,512,512]{2,1,0:T(8,128)(2,1)S(1)} %copy-done.1, bf16[16,4096]{1,0:T(8,128)(2,1)S(1)} %shard_map.95.refs_1_.refs_3_.refs_4_, bf16[16,4096]{1,0:T(8,128)(2,1)S(1)} %collective-permute-done.4.refs_2_.refs_4_.refs_5_, ...), custom_call_target="tpu_custom_call" | custom-call | flops 268435456 | bytes 1835008 | tf_op jit(solution)/shard_map/pallas_call | solution.py:32
  24.1 1.4 %collective-permute-done.8.refs_7_ = f32[64,128]{1,0:T(8,128)S(1)} collective-permute-done((f32[64,128]{1,0:T(8,128)S(1)}, f32[64,128]{1,0:T(8,128)S(1)}, u32[]{:S(2)}, u32[]{:S(2)}) %collective-permute-start.8) | collective-permute-done | bytes 32800 | tf_op jit(solution)/shard_map/ppermute | solution.py:48
  25.5 1.0 %shard_map.99 = (f32[2,8,64]{2,1,0:T(8,128)}, f32[4,2,512]{2,1,0:T(2,128)}) custom-call(f32[64,64]{1,0:T(8,128)S(1)} %fusion.refs_0_, bf16[64,64]{1,0:T(8,128)(2,1)S(1)} %fusion.8.refs_1_, bf16[128,1024]{1,0:T(8,128)(2,1)S(1)} %shard_map.96.refs_2_, bf16[96,1024]{1,0:T(8,128)(2,1)S(1)} %get-tuple-element.16.refs_3_, ...), custom_call_target="tpu_custom_call" | custom-call | flops 33554432 | bytes 700416 | tf_op jit(solution)/shard_map/pallas_call | solution.py:32
  (30 shorter events, 0.2 us)
Async XLA Ops:
  0.6 13.0 %copy-start = (f32[7,2,512]{2,1,0:T(2,128)S(1)}, f32[7,2,512]{2,1,0:T(2,128)}, u32[]{:S(2)}) copy-start(f32[7,2,512]{2,1,0:T(2,128)} %param.12) | copy-start | bytes 86020
  0.6 5.0 %copy-start.2 = (bf16[8,2,2,512]{3,2,1,0:T(2,128)(2,1)S(1)}, bf16[8,2,2,512]{3,2,1,0:T(2,128)(2,1)}, u32[]{:S(2)}) copy-start(bf16[8,2,2,512]{3,2,1,0:T(2,128)(2,1)} %param.9) | copy-start | bytes 98308
  0.7 18.7 %copy-start.1 = (bf16[2,512,512]{2,1,0:T(8,128)(2,1)S(1)}, bf16[2,512,512]{2,1,0:T(8,128)(2,1)}, u32[]{:S(2)}) copy-start(bf16[2,512,512]{2,1,0:T(8,128)(2,1)} %refs_2_.3) | copy-start | bytes 3145732
  0.7 6.6 %collective-permute-start.1 = (bf16[8,2,2,512]{3,2,1,0:T(2,128)(2,1)}, bf16[8,2,2,512]{3,2,1,0:T(2,128)(2,1)S(1)}, u32[]{:S(2)}, u32[]{:S(2)}) collective-permute-start(bf16[8,2,2,512]{3,2,1,0:T(2,128)(2,1)} %param.9), channel_id=1, source_target_pairs={{0,16},{4,20},{8,24},{12,28},{16,0},{20,4},{24,8},{28,12},{1,17},{... | collective-permute-start | bytes 98312 | tf_op jit(solution)/shard_map/ppermute | solution.py:48
  4.8 5.0 %collective-permute-start = (bf16[8,2,2,512]{3,2,1,0:T(2,128)(2,1)}, bf16[8,2,2,512]{3,2,1,0:T(2,128)(2,1)S(1)}, u32[]{:S(2)}, u32[]{:S(2)}) collective-permute-start(bf16[8,2,2,512]{3,2,1,0:T(2,128)(2,1)} %param.8), channel_id=1, source_target_pairs={{0,16},{4,20},{8,24},{12,28},{16,0},{20,4},{24,8},{28,12},{1,17},{... | collective-permute-start | bytes 98312 | tf_op jit(solution)/shard_map/ppermute | solution.py:48
  7.3 2.6 %collective-permute-start.2 = (bf16[16,1024]{1,0:T(8,128)(2,1)S(1)}, bf16[16,1024]{1,0:T(8,128)(2,1)S(1)}, u32[]{:S(2)}, u32[]{:S(2)}) collective-permute-start(bf16[16,1024]{1,0:T(8,128)(2,1)S(1)} %get-tuple-element.21), channel_id=1, source_target_pairs={{0,1},{2,3},{1,0},{3,2},{4,5},{6,7},{5,4},{7,6},{8,9},{10,11},{9,8... | collective-permute-start | bytes 98312 | tf_op jit(solution)/shard_map/ppermute | solution.py:65
  7.4 2.5 %collective-permute-start.3 = (bf16[16,1024]{1,0:T(8,128)(2,1)S(1)}, bf16[16,1024]{1,0:T(8,128)(2,1)S(1)}, u32[]{:S(2)}, u32[]{:S(2)}) collective-permute-start(bf16[16,1024]{1,0:T(8,128)(2,1)S(1)} %get-tuple-element.20), channel_id=1, source_target_pairs={{1,2},{2,1},{5,6},{6,5},{9,10},{10,9},{13,14},{14,13},{17,18},{18,... | collective-permute-start | bytes 98312 | tf_op jit(solution)/shard_map/ppermute | solution.py:64
  9.8 3.8 %copy-start.4 = (f32[4]{0:T(128)S(1)}, f32[4]{0:T(128)}, u32[]{:S(2)}) copy-start(f32[4]{0:T(128)} %param.14) | copy-start | bytes 52
  9.9 3.7 %copy-start.5 = (s32[4]{0:T(128)S(1)}, s32[4]{0:T(128)}, u32[]{:S(2)}) copy-start(s32[4]{0:T(128)} %param.13) | copy-start | bytes 52
  10.0 3.9 %copy-start.3 = (s32[80,2]{0,1:T(2,128)S(1)}, s32[80,2]{0,1:T(2,128)}, u32[]{:S(2)}) copy-start(s32[80,2]{0,1:T(2,128)} %param.15) | copy-start | bytes 1924
  10.0 5.9 %collective-permute-start.4 = (bf16[16,4096]{1,0:T(8,128)(2,1)S(1)}, bf16[16,4096]{1,0:T(8,128)(2,1)S(1)}, u32[]{:S(2)}, u32[]{:S(2)}) collective-permute-start(bf16[16,4096]{1,0:T(8,128)(2,1)S(1)} %shard_map.95.refs_1_.refs_3_.refs_4_), channel_id=1, source_target_pairs={{0,12},{4,8},{8,4},{12,0},{16,28},{20,24},{24,20},{28,16},{1,13},{... | collective-permute-start | bytes 393224 | tf_op jit(solution)/shard_map/ppermute | solution.py:48
  12.6 6.7 %collective-permute-start.5 = (bf16[16,4096]{1,0:T(8,128)(2,1)S(1)}, bf16[16,4096]{1,0:T(8,128)(2,1)S(1)}, u32[]{:S(2)}, u32[]{:S(2)}) collective-permute-start(bf16[16,4096]{1,0:T(8,128)(2,1)S(1)} %shard_map.95.refs_1_.refs_3_.refs_4_), channel_id=1, source_target_pairs={{0,4},{4,0},{8,12},{12,8},{16,20},{20,16},{24,28},{28,24},{1,5},{5... | collective-permute-start | bytes 393224 | tf_op jit(solution)/shard_map/ppermute | solution.py:48
  13.1 6.6 %collective-permute-start.6 = (bf16[16,4096]{1,0:T(8,128)(2,1)S(1)}, bf16[16,4096]{1,0:T(8,128)(2,1)S(1)}, u32[]{:S(2)}, u32[]{:S(2)}) collective-permute-start(bf16[16,4096]{1,0:T(8,128)(2,1)S(1)} %shard_map.95.refs_1_.refs_3_.refs_4_), channel_id=1, source_target_pairs={{0,8},{4,12},{8,0},{12,4},{16,24},{20,28},{24,16},{28,20},{1,9},{5... | collective-permute-start | bytes 393224 | tf_op jit(solution)/shard_map/ppermute | solution.py:48
  20.4 3.7 %collective-permute-start.7 = (f32[64,128]{1,0:T(8,128)S(1)}, f32[64,128]{1,0:T(8,128)S(1)}, u32[]{:S(2)}, u32[]{:S(2)}) collective-permute-start(f32[64,128]{1,0:T(8,128)S(1)} %get-tuple-element.19.refs_5_), channel_id=1, source_target_pairs={{0,3},{1,2},{2,1},{3,0},{4,7},{5,6},{6,5},{7,4},{8,11},{9,10},{10,... | collective-permute-start | bytes 98312 | tf_op jit(solution)/shard_map/ppermute | solution.py:48
  20.5 5.0 %collective-permute-start.8 = (f32[64,128]{1,0:T(8,128)S(1)}, f32[64,128]{1,0:T(8,128)S(1)}, u32[]{:S(2)}, u32[]{:S(2)}) collective-permute-start(f32[64,128]{1,0:T(8,128)S(1)} %get-tuple-element.19.refs_5_), channel_id=1, source_target_pairs={{0,2},{1,3},{2,0},{3,1},{4,6},{5,7},{6,4},{7,5},{8,10},{9,11},{10,... | collective-permute-start | bytes 98312 | tf_op jit(solution)/shard_map/ppermute | solution.py:48
  23.3 2.2 %collective-permute-start.9 = (f32[64,128]{1,0:T(8,128)S(1)}, f32[64,128]{1,0:T(8,128)S(1)}, u32[]{:S(2)}, u32[]{:S(2)}) collective-permute-start(f32[64,128]{1,0:T(8,128)S(1)} %get-tuple-element.19.refs_5_), channel_id=1, source_target_pairs={{0,1},{1,0},{2,3},{3,2},{4,5},{5,4},{6,7},{7,6},{8,9},{9,8},{10,11... | collective-permute-start | bytes 98312 | tf_op jit(solution)/shard_map/ppermute | solution.py:48
